TPU v7x, 512 devices: a whole 4x8x8 slice. The times are simulated.
512 devices in a mesh: rhs: 64 (over x, z, core), row: 8 (over y).
Axes of the slice: x: 4, y: 8, z: 8, core: 2. Of those that a mesh axis runs over, the one named last changes fastest.
Arguments:
- rhs_block: float32 [4096, 16384], P('row', 'rhs'), may hold values from -6 to 6
- below: float32 [64, 4096, 512], P('rhs', 'row'), may hold values from -0.25 to 0.25
- inverse: float32 [64, 512, 512], P('rhs', 'row'), may hold values from -0.25 to 0.25
- owner_map: int32 [64], replicated, may hold values from 0 to 63, each once
- row_perm: int32 [4096], P('row'), may hold values from 0 to 4095, as said below
Outputs:
- solved_front: float32 [4096, 16384], P('row', 'rhs')
Inputs may be any that keep to these rules, and one draw needn't show every extreme that they name: `owner_map`: entries 0 to 2 name the slots of the panels; all entries are distinct. `row_perm`: A permutation of the 4096 rows that maps each aligned block of 512 rows onto itself.
All inputs are finite; a program needn't handle non-finite values.
Results may differ from a plain program's by a relative error of at most 0.00013.
Values sent between devices are 32-bit elements; how exact they have to be, the bound alone decides.
No kernel may reach another device: no remote copies, remote signals or barrier semaphores. Data moves between devices by JAX's collectives and lax.ppermute only.
A program may use at most 64 MiB of HBM per device.

v0:
```python
import jax
import jax.numpy as jnp
from jax import lax
from jax.sharding import PartitionSpec as P

PANELS = 3


def broadcast(block, axis, owner):
    block = jnp.where(lax.axis_index(axis) == owner, block, jnp.zeros_like(block))
    return lax.psum(block, axis)


def sent_to_all(x, axis):
    count = lax.axis_size(axis)
    return lax.all_to_all(jnp.broadcast_to(x[None], (count, *x.shape)), axis, 0, 0, tiled=True)


def joined_along(tiles, dim):
    tiles = jnp.moveaxis(tiles, 0, dim)
    dims = tiles.shape
    return tiles.reshape(*dims[:dim], dims[dim] * dims[dim + 1], *dims[dim + 2 :])


def collect(x, axis, dim):
    tiles = sent_to_all(x, axis)
    return joined_along(tiles, dim)


def per_device(rhs_block, below, inverse, owner_map, row_perm):
    rows_dev = rhs_block.shape[0]
    slab_rows = inverse.shape[1]
    position = lax.axis_index("row")
    working = jnp.take(rhs_block, row_perm - position * rows_dev, axis=0)
    for panel_index in range(PANELS):
        after_rows = (panel_index + 1) * slab_rows
        lower_rows = broadcast(below[0][after_rows:], "rhs", owner_map[panel_index])
        inverse_rows = broadcast(inverse[0], "rhs", owner_map[panel_index])
        first_row = panel_index * slab_rows
        last_row = first_row + slab_rows
        pivot_slab = collect(working[first_row:last_row], "row", 0)
        trailing = lower_rows
        own_rows = jnp.dot(
            inverse_rows,
            pivot_slab,
            precision=lax.Precision.HIGHEST,
            preferred_element_type=jnp.float32,
        )

        def accumulate(total, piece, start, trailing=trailing):
            return jnp.dot(
                trailing, piece, precision=lax.Precision.HIGHEST, preferred_element_type=jnp.float32
            )

        empty = jnp.zeros((trailing.shape[0], working.shape[1]), jnp.float32)
        update = accumulate(empty, collect(own_rows, "row", 0), jnp.int32(0))
        working = working.at[first_row:last_row].set(own_rows)
        working = working.at[last_row:].add(-update)
    return working


def solution(mesh):
    return jax.shard_map(
        per_device,
        mesh=mesh,
        in_specs=(P("row", "rhs"), P("rhs", "row", None), P("rhs", "row", None), P(), P("row")),
        out_specs=P("row", "rhs"),
        check_vma=False,
    )
```

profile of v0, /device:TPU:65, one launch (start us, length us, event | category | flops | bytes accessed | tf_op | source)
XLA Modules:
  0.0 344.8 jit_solution(5734071325942240349)
XLA Ops:
  6.5 1.5 fusion.4
  9.9 2.2 select_bitcast_fusion
  12.1 1.0 select_bitcast_fusion.1
  13.1 0.9 select_bitcast_fusion.2
  14.0 0.8 select_bitcast_fusion.3
  14.8 0.7 copy-done.9
  15.5 1.6 gather_fusion
  17.3 22.7 %all_to_all.30 = f32[8,64,256]{2,1,0:T(8,128)S(1)} all-to-all(f32[8,64,256]{2,1,0:T(8,128)S(1)} %broadcast_in_dim.60), channel_id=1, replica_groups=mesh['rhs'=64,'row'=8] {'row'}, dimensions={0} | all-to-all | bytes 1048576 | tf_op jit(solution)/shard_map/all_to_all | solution.py:16
  40.0 182.1 %all-reduce.3.cloned.1.call-done = (f32[64,512]{1,0:T(8,128)}, f32[448,512]{1,0:T(8,128)}, f32[64,512]{1,0:T(8,128)}, f32[384,512]{1,0:T(8,128)}, f32[64,512]{1,0:T(8,128)}, /*index=5*/f32[320,512]{1,0:T(8,128)}) async-done(((f32[64,512]{1,0:T(8,128)}, f32[448,512]{1,0:T(8,128)}, f32[64,512]{1,0:T(8,128)}, f32[384,512]{1,0:T(8,128)}, f32[64,512]{1,0:T(8,128)}, /*index=5*/f32[320,512]{1,0:T(8,128)}), ...) | async-done | bytes 2752528 | tf_op jit(solution)/shard_map/psum | solution.py:11
  222.1 1.3 constant_dynamic-update-slice_fusion.4
  223.4 24.4 %all_to_all.31 = f32[8,64,256]{2,1,0:T(8,128)S(1)} all-to-all(f32[8,64,256]{2,1,0:T(8,128)S(1)} %broadcast_in_dim.62), channel_id=1, replica_groups=mesh['rhs'=64,'row'=8] {'row'}, dimensions={0} | all-to-all | bytes 1048576 | tf_op jit(solution)/shard_map/all_to_all | solution.py:16
  247.8 0.9 fusion
  248.7 0.8 broadcast_in_dim.63
  249.6 3.5 %all-to-all-start.2 = ((f32[8,64,256]{2,1,0:T(8,128)}), f32[8,64,256]{2,1,0:T(8,128)S(1)}, u32[]{:S(2)}, u32[]{:S(2)}) async-start(f32[8,64,256]{2,1,0:T(8,128)} %broadcast_in_dim.63), calls=%async_computation.2 | async-start | bytes 1048576 | tf_op jit(solution)/shard_map/all_to_all | solution.py:16
  253.1 17.8 %all-to-all-done.2 = f32[8,64,256]{2,1,0:T(8,128)S(1)} async-done(((f32[8,64,256]{2,1,0:T(8,128)}), f32[8,64,256]{2,1,0:T(8,128)S(1)}, u32[]{:S(2)}, u32[]{:S(2)}) %all-to-all-start.2) | async-done | bytes 524320 | tf_op jit(solution)/shard_map/all_to_all | solution.py:16
  271.0 0.4 constant_dynamic-update-slice_fusion.2
  271.4 20.4 %all_to_all.32 = f32[8,64,256]{2,1,0:T(8,128)S(1)} all-to-all(f32[8,64,256]{2,1,0:T(8,128)S(1)} %broadcast_in_dim.65), channel_id=1, replica_groups=mesh['rhs'=64,'row'=8] {'row'}, dimensions={0} | all-to-all | bytes 1048576 | tf_op jit(solution)/shard_map/all_to_all | solution.py:16
  291.8 0.8 fusion.1
  292.6 0.8 broadcast_in_dim.66
  293.4 3.5 %all-to-all-start.4 = ((f32[8,64,256]{2,1,0:T(8,128)}), f32[8,64,256]{2,1,0:T(8,128)S(1)}, u32[]{:S(2)}, u32[]{:S(2)}) async-start(f32[8,64,256]{2,1,0:T(8,128)} %broadcast_in_dim.66), calls=%async_computation.4 | async-start | bytes 1048576 | tf_op jit(solution)/shard_map/all_to_all | solution.py:16
  297.0 17.8 %all-to-all-done.4 = f32[8,64,256]{2,1,0:T(8,128)S(1)} async-done(((f32[8,64,256]{2,1,0:T(8,128)}), f32[8,64,256]{2,1,0:T(8,128)S(1)}, u32[]{:S(2)}, u32[]{:S(2)}) %all-to-all-start.4) | async-done | bytes 524320 | tf_op jit(solution)/shard_map/all_to_all | solution.py:16
  314.8 0.4 constant_dynamic-update-slice_fusion
  315.2 20.4 %all_to_all.33 = f32[8,64,256]{2,1,0:T(8,128)S(1)} all-to-all(f32[8,64,256]{2,1,0:T(8,128)S(1)} %broadcast_in_dim.68), channel_id=1, replica_groups=mesh['rhs'=64,'row'=8] {'row'}, dimensions={0} | all-to-all | bytes 1048576 | tf_op jit(solution)/shard_map/all_to_all | solution.py:16
  335.6 2.4 fusion.3
  (33 shorter events, 0.4 us)
Async XLA Ops:
  6.5 9.0 %copy-start = (f32[512,256]{1,0:T(8,128)S(1)}, f32[512,256]{1,0:T(8,128)}, u32[]{:S(2)}) copy-start(f32[512,256]{1,0:T(8,128)} %param.17) | copy-start | bytes 1572868
  6.5 5.6 %copy-start.2 = (f32[1,512,512]{2,1,0:T(8,128)S(1)}, f32[1,512,512]{2,1,0:T(8,128)}, u32[]{:S(2)}) copy-start(f32[1,512,512]{2,1,0:T(8,128)} %param.18) | copy-start | bytes 3145732
  6.5 215.6 %all-reduce.3.cloned.1.call-start = ((), (), s32[]{:S(2)}) async-start(), calls=%async_computation.6 | async-start | bytes 5505024 | tf_op jit(solution)/shard_map/psum | solution.py:11
  13.1 0.9 copy-start.6
  14.8 0.7 copy-start.9
  223.4 24.5 %copy-start.3 = (f32[448,512]{1,0:T(8,128)S(1)}, f32[448,512]{1,0:T(8,128)}, u32[]{:S(2)}) copy-start(f32[448,512]{1,0:T(8,128)} %get-tuple-element.78) | copy-start | bytes 2752516
  249.6 21.4 %all-to-all-start.2 = ((f32[8,64,256]{2,1,0:T(8,128)}), f32[8,64,256]{2,1,0:T(8,128)S(1)}, u32[]{:S(2)}, u32[]{:S(2)}) async-start(f32[8,64,256]{2,1,0:T(8,128)} %broadcast_in_dim.63), calls=%async_computation.2 | async-start | bytes 1048576 | tf_op jit(solution)/shard_map/all_to_all | solution.py:16
  253.1 17.9 %copy-start.8 = (f32[64,512]{1,0:T(8,128)S(1)}, f32[64,512]{1,0:T(8,128)}, u32[]{:S(2)}) copy-start(f32[64,512]{1,0:T(8,128)} %get-tuple-element.79) | copy-start | bytes 393220
  271.3 20.4 %copy-start.4 = (f32[384,512]{1,0:T(8,128)S(1)}, f32[384,512]{1,0:T(8,128)}, u32[]{:S(2)}) copy-start(f32[384,512]{1,0:T(8,128)} %get-tuple-element.80) | copy-start | bytes 2359300
  293.4 21.4 %all-to-all-start.4 = ((f32[8,64,256]{2,1,0:T(8,128)}), f32[8,64,256]{2,1,0:T(8,128)S(1)}, u32[]{:S(2)}, u32[]{:S(2)}) async-start(f32[8,64,256]{2,1,0:T(8,128)} %broadcast_in_dim.66), calls=%async_computation.4 | async-start | bytes 1048576 | tf_op jit(solution)/shard_map/all_to_all | solution.py:16
  296.9 17.9 %copy-start.7 = (f32[64,512]{1,0:T(8,128)S(1)}, f32[64,512]{1,0:T(8,128)}, u32[]{:S(2)}) copy-start(f32[64,512]{1,0:T(8,128)} %get-tuple-element.81) | copy-start | bytes 393220
  315.2 20.4 %copy-start.1 = (f32[512,256]{1,0:T(8,128)}, f32[512,256]{1,0:T(8,128)S(1)}, u32[]{:S(2)}) copy-start(f32[512,256]{1,0:T(8,128)S(1)} %get-tuple-element.95) | copy-start | bytes 1572868
  315.2 20.4 %copy-start.5 = (f32[320,512]{1,0:T(8,128)S(1)}, f32[320,512]{1,0:T(8,128)}, u32[]{:S(2)}) copy-start(f32[320,512]{1,0:T(8,128)} %get-tuple-element.82) | copy-start | bytes 1966084
Sparse Core Ops, SparseCore 0:
  14.9 207.1 all-reduce.2
where the time goes:
time: 345 us
  waiting for transfers between devices  218 us (63%)
  blocking collectives  87.9 us (25%)
  between operations  15.5 us (4%)
  starting transfers between devices  6.99 us (2%)
  matrix products  6.09 us (2%)
  local copies, waits for them, and re-layouts  5.65 us (2%)
  other arithmetic  5.01 us (1%)
    psum x1, waiting for transfers between devices, broadcast(): return lax.psum(block, axis)  182 us
    all_to_all x4, blocking collectives, sent_to_all(): lax.all_to_all(jnp.broadcast_to(x[None], (count, *x.shape)), axis, 0, 0,...  87.9 us
    all_to_all x2, waiting for transfers between devices, sent_to_all(): lax.all_to_all(jnp.broadcast_to(x[None], (count, *x.shape)), axis, 0, 0,...  35.7 us
    all_to_all x2, starting transfers between devices, sent_to_all(): lax.all_to_all(jnp.broadcast_to(x[None], (count, *x.shape)), axis, 0, 0,...  6.99 us
  transfers between devices with their start and end apart: 3, of which 3 were waited for; matrix products, arithmetic and copies ran while one was open for 1% of the time, Pallas kernels for 0%

commit v1 on v0

v1 whole, which is shorter than its diff:
```python
import jax
import jax.numpy as jnp
from jax import lax
from jax.sharding import Mesh, PartitionSpec as P

PANELS = 3
ROW = "row"
PLANE = ("core", "x", "z")


def sent_to_all(x, axis):
    count = lax.axis_size(axis)
    return lax.all_to_all(jnp.broadcast_to(x[None], (count, *x.shape)), axis, 0, 0, tiled=True)


def dot(a, b):
    return jnp.dot(a, b, precision=lax.Precision.HIGHEST, preferred_element_type=jnp.float32)


def per_device(rhs_block, below, inverse, owner_map, row_perm):
    rows_dev, columns = rhs_block.shape
    slab = inverse.shape[1]
    pivots = inverse.shape[2]
    position = lax.axis_index(ROW)
    nx, nz, nc = lax.axis_size("x"), lax.axis_size("z"), lax.axis_size("core")
    plane = nx * nz * nc
    me = (lax.axis_index("x") * nz + lax.axis_index("z")) * nc + lax.axis_index("core")

    working = rhs_block.at[row_perm - position * rows_dev].get(mode="promise_in_bounds")
    pivot = sent_to_all(working[:slab], ROW).reshape(pivots, columns)

    whole_inverse = sent_to_all(inverse[0], ROW).reshape(pivots, pivots)
    operator = -dot(below[0], whole_inverse)
    panel_of_me = sum(jnp.where(owner_map[k] == me, k, 0) for k in range(PANELS))
    operator = lax.dynamic_update_slice(operator, inverse[0], (panel_of_me * slab, 0))

    piece = rows_dev // plane
    pieces = lax.all_to_all(operator.reshape(plane, piece, pivots), PLANE, 0, 0, tiled=True)
    kept = []
    for k in range(PANELS):
        o = owner_map[k]
        core, z, x = o % nc, (o // nc) % nz, o // (nc * nz)
        kept.append(lax.dynamic_index_in_dim(pieces, (core * nx + x) * nz + z, 0, keepdims=False))
    kept = jnp.stack(kept)
    kept = sent_to_all(kept, "z")
    kept = sent_to_all(kept, "x")
    mine = kept
    other = lax.ppermute(kept, "core", [(0, 1), (1, 0)])
    first = lax.axis_index("core") == 0
    halves = [jnp.where(first, mine, other), jnp.where(first, other, mine)]

    for k in range(PANELS):
        start, end = k * slab, (k + 1) * slab
        panel = jnp.concatenate([h[:, :, k].reshape(rows_dev // 2, pivots) for h in halves], axis=0)
        if k:
            pivot = sent_to_all(working[start:end], ROW).reshape(pivots, columns)
        moved = dot(panel[start:], pivot)
        working = jnp.concatenate(
            [working[:start], moved[:slab], working[end:] + moved[slab:]], axis=0
        )
    return working


def solution(mesh):
    mesh = Mesh(mesh.devices.reshape(4, 8, 2, 8), ("x", "z", "core", "row"))
    rhs = ("x", "z", "core")
    return jax.shard_map(
        per_device,
        mesh=mesh,
        in_specs=(P("row", rhs), P(rhs, "row", None), P(rhs, "row", None), P(), P("row")),
        out_specs=P("row", rhs),
        check_vma=False,
    )
```

time: 345 us -> 204 us (0.59)
  the two profiles are of different devices: /device:TPU:65 before, /device:TPU:1 now
where the time goes in v1:
time: 204 us; the launch traced here: 203 us
  waiting for transfers between devices  80.1 us (39%)
  blocking collectives  57.5 us (28%)
  starting transfers between devices  36.3 us (18%)
  local copies, waits for them, and re-layouts  10.5 us (5%)
  between operations  9.23 us (5%)
  matrix products  6.85 us (3%)
  other arithmetic  2.77 us (1%)
    all_to_all x3, waiting for transfers between devices, sent_to_all(): lax.all_to_all(jnp.broadcast_to(x[None], (count, *x.shape)), axis, 0, 0,...  58.2 us
    all_to_all x3, blocking collectives, sent_to_all(): lax.all_to_all(jnp.broadcast_to(x[None], (count, *x.shape)), axis, 0, 0,...  57.5 us
    all_to_all x1, waiting for transfers between devices, per_device(): lax.all_to_all(operator.reshape(plane, piece, pivots), PLANE, 0, 0, tiled...  21.9 us
    all_to_all x1, starting transfers between devices, per_device(): lax.all_to_all(operator.reshape(plane, piece, pivots), PLANE, 0, 0, tiled...  15.8 us
    all_to_all x3, starting transfers between devices, sent_to_all(): lax.all_to_all(jnp.broadcast_to(x[None], (count, *x.shape)), axis, 0, 0,...  15.3 us
    dot_general x4, matrix products, dot(): jnp.dot(a, b, precision=lax.Precision.HIGHEST, preferred_element_type=jnp...  6.85 us
    ppermute x1, starting transfers between devices, per_device(): other = lax.ppermute(kept, 'core', [(0, 1), (1, 0)])  5.15 us
    broadcast_in_dim x6, local copies, waits for them, and re-layouts, sent_to_all(): jnp.broadcast_to(x[None], (count, *x.shape))  4.09 us
  transfers between devices with their start and end apart: 5, of which 4 were waited for; matrix products, arithmetic and copies ran while one was open for 4% of the time, Pallas kernels for 0%

profile of v1, /device:TPU:1, one launch (start us, length us, event | category | flops | bytes accessed | tf_op | source)
XLA Modules:
  0.0 203.2 jit_solution(14387606891561533739)
XLA Ops:
  0.0 2.1 %broadcast_in_dim.17 = f32[8,64,512]{2,1,0:T(8,128)} broadcast(f32[64,512]{1,0:T(8,128)} %bitcast.32), dimensions={1,2} | broadcast | bytes 1179648 | tf_op jit(solution)/shard_map/broadcast_in_dim | solution.py:13
  2.1 7.6 %all-to-all-start = ((f32[8,64,512]{2,1,0:T(8,128)}), f32[8,64,512]{2,1,0:T(8,128)S(1)}, u32[]{:S(2)}, u32[]{:S(2)}) async-start(f32[8,64,512]{2,1,0:T(8,128)} %broadcast_in_dim.17), calls=%async_computation | async-start | bytes 2097152 | tf_op jit(solution)/shard_map/all_to_all | solution.py:13
  11.7 25.4 %all-to-all-done = f32[8,64,512]{2,1,0:T(8,128)S(1)} async-done(((f32[8,64,512]{2,1,0:T(8,128)}), f32[8,64,512]{2,1,0:T(8,128)S(1)}, u32[]{:S(2)}, u32[]{:S(2)}) %all-to-all-start) | async-done | bytes 1048608 | tf_op jit(solution)/shard_map/all_to_all | solution.py:13
  37.1 2.9 %convolution_negate_fusion = f32[512,512]{1,0:T(8,128)} fusion(f32[512,512]{1,0:T(8,128)S(1)} %bitcast.23, f32[1,512,512]{2,1,0:T(8,128)S(1)} %copy-done), kind=kOutput, calls=%fused_computation.1 | convolution fusion | flops 1610874880 | bytes 3145728 | tf_op jit(solution)/shard_map/dot_general | solution.py:17
  40.6 15.8 %all-to-all-start.1 = ((f32[64,8,512]{2,1,0:T(8,128)}), f32[64,8,512]{2,1,0:T(8,128)S(1)}, u32[]{:S(2)}, u32[]{:S(2)}) async-start(f32[64,8,512]{2,1,0:T(8,128)} %bitcast.5), calls=%async_computation.1 | async-start | bytes 2097152 | tf_op jit(solution)/shard_map/all_to_all | solution.py:38
  64.1 21.9 %all-to-all-done.1 = f32[64,8,512]{2,1,0:T(8,128)S(1)} async-done(((f32[64,8,512]{2,1,0:T(8,128)}), f32[64,8,512]{2,1,0:T(8,128)S(1)}, u32[]{:S(2)}, u32[]{:S(2)}) %all-to-all-start.1) | async-done | bytes 1048608 | tf_op jit(solution)/shard_map/all_to_all | solution.py:38
  86.1 16.2 %all_to_all.35 = f32[8,3,8,512]{3,2,1,0:T(8,128)S(1)} all-to-all(f32[8,3,8,512]{3,2,1,0:T(8,128)S(1)} %broadcast_in_dim.18), channel_id=1, replica_groups=mesh['x'=4,'z'=8,'core'=2,'row'=8] {'z'}, dimensions={0} | all-to-all | bytes 786432 | tf_op jit(solution)/shard_map/all_to_all | solution.py:13
  102.5 21.0 %all_to_all.36 = f32[4,8,3,8,512]{4,3,2,1,0:T(8,128)S(1)} all-to-all(f32[4,8,3,8,512]{4,3,2,1,0:T(8,128)S(1)} %broadcast_in_dim.19), channel_id=1, replica_groups=mesh['x'=4,'z'=8,'core'=2,'row'=8] {'x'}, dimensions={0} | all-to-all | bytes 3145728 | tf_op jit(solution)/shard_map/all_to_all | solution.py:13
  123.5 5.2 %collective-permute-start = (f32[4,8,3,8,512]{4,3,2,1,0:T(8,128)S(1)}, f32[4,8,3,8,512]{4,3,2,1,0:T(8,128)}, u32[]{:S(2)}, u32[]{:S(2)}) collective-permute-start(f32[4,8,3,8,512]{4,3,2,1,0:T(8,128)S(1)} %all_to_all.36), channel_id=1, source_target_pairs={{0,8},{8,0},{1,9},{9,1},{2,10},{10,2},{3,11},{11,3},{4,12},{12,4},... | collective-permute-start | bytes 4718600 | tf_op jit(solution)/shard_map/ppermute | solution.py:48
  128.7 2.2 %gather_fusion = f32[512,256]{1,0:T(8,128)} fusion(f32[512,256]{1,0:T(8,128)S(1)} %copy-done.1, s32[1024]{0:T(1024)S(1)} %pad_clamp_fusion), kind=kCustom, calls=%fused_computation | custom fusion | bytes 1050624 | tf_op jit(solution)/shard_map/gather | solution.py:29
  131.0 0.8 slice.99
  131.8 0.8 broadcast_in_dim.21
  132.6 4.1 %all-to-all-start.4 = ((f32[8,64,256]{2,1,0:T(8,128)}), f32[8,64,256]{2,1,0:T(8,128)}, u32[]{:S(2)}, u32[]{:S(2)}) async-start(f32[8,64,256]{2,1,0:T(8,128)} %broadcast_in_dim.21), calls=%async_computation.4 | async-start | bytes 1048576 | tf_op jit(solution)/shard_map/all_to_all | solution.py:13
  136.8 1.8 broadcast_select_fusion.1
  138.6 1.3 fusion.12
  139.9 15.0 %all-to-all-done.4 = f32[8,64,256]{2,1,0:T(8,128)} async-done(((f32[8,64,256]{2,1,0:T(8,128)}), f32[8,64,256]{2,1,0:T(8,128)}, u32[]{:S(2)}, u32[]{:S(2)}) %all-to-all-start.4) | async-done | bytes 524320 | tf_op jit(solution)/shard_map/all_to_all | solution.py:13
  154.8 2.3 %fusion = f32[512,256]{1,0:T(8,128)S(1)} fusion(f32[512,256]{1,0:T(8,128)} %bitcast.9, f32[256,512]{1,0:T(8,128)} %bitcast.29, f32[256,512]{1,0:T(8,128)} %bitcast.28), kind=kOutput, calls=%fused_computation.2 | convolution fusion | flops 805568512 | bytes 2097152 | tf_op jit(solution)/shard_map/dot_general | solution.py:17
  158.0 20.3 %all_to_all.37 = f32[8,64,256]{2,1,0:T(8,128)S(1)} all-to-all(f32[8,64,256]{2,1,0:T(8,128)S(1)} %broadcast_in_dim.22), channel_id=1, replica_groups=mesh['x'=4,'z'=8,'core'=2,'row'=8] {'row'}, dimensions={0} | all-to-all | bytes 1048576 | tf_op jit(solution)/shard_map/all_to_all | solution.py:13
  178.3 0.9 fusion.5
  179.3 0.9 broadcast_in_dim.23
  180.2 3.5 %all-to-all-start.6 = ((f32[8,64,256]{2,1,0:T(8,128)}), f32[8,64,256]{2,1,0:T(8,128)S(1)}, u32[]{:S(2)}, u32[]{:S(2)}) async-start(f32[8,64,256]{2,1,0:T(8,128)} %broadcast_in_dim.23), calls=%async_computation.6 | async-start | bytes 1048576 | tf_op jit(solution)/shard_map/all_to_all | solution.py:13
  183.7 17.8 %all-to-all-done.6 = f32[8,64,256]{2,1,0:T(8,128)S(1)} async-done(((f32[8,64,256]{2,1,0:T(8,128)}), f32[8,64,256]{2,1,0:T(8,128)S(1)}, u32[]{:S(2)}, u32[]{:S(2)}) %all-to-all-start.6) | async-done | bytes 524320 | tf_op jit(solution)/shard_map/all_to_all | solution.py:13
  201.5 0.8 fusion.7
  202.4 0.8 pad_maximum_fusion.4
  (38 shorter events, 2.5 us)
Async XLA Ops:
  0.0 37.1 %copy-start = (f32[1,512,512]{2,1,0:T(8,128)S(1)}, f32[1,512,512]{2,1,0:T(8,128)}, u32[]{:S(2)}) copy-start(f32[1,512,512]{2,1,0:T(8,128)} %param.6) | copy-start | bytes 3145732
  0.0 9.8 %copy-start.7 = (s32[64]{0:T(128)S(1)}, s32[64]{0:T(128)}, u32[]{:S(2)}) copy-start(s32[64]{0:T(128)} %param.8) | copy-start | bytes 772
  2.1 34.9 %all-to-all-start = ((f32[8,64,512]{2,1,0:T(8,128)}), f32[8,64,512]{2,1,0:T(8,128)S(1)}, u32[]{:S(2)}, u32[]{:S(2)}) async-start(f32[8,64,512]{2,1,0:T(8,128)} %broadcast_in_dim.17), calls=%async_computation | async-start | bytes 2097152 | tf_op jit(solution)/shard_map/all_to_all | solution.py:13
  37.1 2.9 %copy-start.6 = (f32[1,64,512]{2,1,0:T(8,128)S(1)}, f32[1,64,512]{2,1,0:T(8,128)}, u32[]{:S(2)}) copy-start(f32[1,64,512]{2,1,0:T(8,128)} %param.7) | copy-start | bytes 393220
  40.6 45.5 %all-to-all-start.1 = ((f32[64,8,512]{2,1,0:T(8,128)}), f32[64,8,512]{2,1,0:T(8,128)S(1)}, u32[]{:S(2)}, u32[]{:S(2)}) async-start(f32[64,8,512]{2,1,0:T(8,128)} %bitcast.5), calls=%async_computation.1 | async-start | bytes 2097152 | tf_op jit(solution)/shard_map/all_to_all | solution.py:38
  102.5 26.2 %copy-start.8 = (s32[512]{0:T(512)S(1)}, s32[512]{0:T(512)}, u32[]{:S(2)}) copy-start(s32[512]{0:T(512)} %param.9) | copy-start | bytes 6148
  102.5 26.2 %copy-start.1 = (f32[512,256]{1,0:T(8,128)S(1)}, f32[512,256]{1,0:T(8,128)}, u32[]{:S(2)}) copy-start(f32[512,256]{1,0:T(8,128)} %param.5) | copy-start | bytes 1572868
  123.5 13.3 %collective-permute-start = (f32[4,8,3,8,512]{4,3,2,1,0:T(8,128)S(1)}, f32[4,8,3,8,512]{4,3,2,1,0:T(8,128)}, u32[]{:S(2)}, u32[]{:S(2)}) collective-permute-start(f32[4,8,3,8,512]{4,3,2,1,0:T(8,128)S(1)} %all_to_all.36), channel_id=1, source_target_pairs={{0,8},{8,0},{1,9},{9,1},{2,10},{10,2},{3,11},{11,3},{4,12},{12,4},... | collective-permute-start | bytes 4718600 | tf_op jit(solution)/shard_map/ppermute | solution.py:48
  132.6 22.2 %all-to-all-start.4 = ((f32[8,64,256]{2,1,0:T(8,128)}), f32[8,64,256]{2,1,0:T(8,128)}, u32[]{:S(2)}, u32[]{:S(2)}) async-start(f32[8,64,256]{2,1,0:T(8,128)} %broadcast_in_dim.21), calls=%async_computation.4 | async-start | bytes 1048576 | tf_op jit(solution)/shard_map/all_to_all | solution.py:13
  139.9 17.3 %copy-start.2 = (f32[512,256]{1,0:T(8,128)S(1)}, f32[512,256]{1,0:T(8,128)}, u32[]{:S(2)}) copy-start(f32[512,256]{1,0:T(8,128)} %gather_fusion) | copy-start | bytes 1572868
  157.2 0.8 copy-start.4
  157.2 21.1 %copy-start.3 = (f32[4,8,1,8,512]{4,3,2,1,0:T(8,128)S(1)}, f32[4,8,1,8,512]{4,3,2,1,0:T(8,128)}, u32[]{:S(2)}) copy-start(f32[4,8,1,8,512]{4,3,2,1,0:T(8,128)} %get-tuple-element.20) | copy-start | bytes 1572868
  179.2 4.4 %copy-start.5 = (f32[448,256]{1,0:T(8,128)}, f32[448,256]{1,0:T(8,128)S(1)}, u32[]{:S(2)}) copy-start(f32[448,256]{1,0:T(8,128)S(1)} %fusion.5) | copy-start | bytes 1376260
  180.2 21.4 %all-to-all-start.6 = ((f32[8,64,256]{2,1,0:T(8,128)}), f32[8,64,256]{2,1,0:T(8,128)S(1)}, u32[]{:S(2)}, u32[]{:S(2)}) async-start(f32[8,64,256]{2,1,0:T(8,128)} %broadcast_in_dim.23), calls=%async_computation.6 | async-start | bytes 1048576 | tf_op jit(solution)/shard_map/all_to_all | solution.py:13
  183.7 18.7 %slice-start = ((f32[512,256]{1,0:T(8,128)}), f32[64,256]{1,0:T(8,128)S(1)}, s32[]{:S(2)}) async-start(f32[512,256]{1,0:T(8,128)} %copy-done.4), calls=%async_computation.7 | async-start | bytes 131072 | tf_op jit(solution)/shard_map/slice | solution.py:59
  201.5 0.9 slice-start.1

commit v2 on v1

v2 whole, which is shorter than its diff:
```python
import jax
import jax.numpy as jnp
from jax import lax
from jax.sharding import Mesh, PartitionSpec as P

PANELS = 3
ROW = "row"
CHIP = ("x", "z")
PLANE = ("core", "x", "z")
SWAP = [(0, 1), (1, 0)]


def sent_to_all(x, axis):
    count = lax.axis_size(axis)
    return lax.all_to_all(jnp.broadcast_to(x[None], (count, *x.shape)), axis, 0, 0, tiled=True)


def dot(a, b):
    return jnp.dot(a, b, precision=lax.Precision.HIGHEST, preferred_element_type=jnp.float32)


def spread(operator, axes, sources):
    rows, pivots = operator.shape
    count = lax.axis_size(axes)
    operator, sources = lax.optimization_barrier((operator, sources))
    pieces = lax.all_to_all(operator.reshape(count, rows // count, pivots), axes, 0, 0, tiled=True)
    return jnp.stack([lax.dynamic_index_in_dim(pieces, s, 0, keepdims=False) for s in sources])


def shared_slots(below, inverse, core, own_core, panel, chips, sources):
    slab, pivots = inverse.shape
    rows = below.shape[0] // 2
    kept_rows = lax.dynamic_slice_in_dim(below, core * rows, rows, 0)
    sent_rows = lax.dynamic_slice_in_dim(below, (1 - core) * rows, rows, 0)
    got = lax.ppermute(jnp.concatenate([sent_rows, inverse]), "core", SWAP)
    mine = core == own_core
    lower = jnp.where(mine, kept_rows, got[:rows])
    slab_rows = jnp.where(mine, inverse, got[rows:])
    part = lax.dynamic_slice_in_dim(slab_rows, core * (slab // 2), slab // 2, 0)
    part = sent_to_all(part, ROW)
    other = lax.ppermute(part, "core", SWAP)
    first = core == 0
    whole = jnp.stack([jnp.where(first, part, other), jnp.where(first, other, part)], axis=1)
    operator = -dot(lower, whole.reshape(pivots, pivots))
    operator = jnp.where(
        first, lax.dynamic_update_slice(operator, slab_rows, (panel * slab, 0)), operator
    )
    return spread(operator, CHIP, chips)


def own_slots(below, inverse, core, own_core, panel, chips, sources):
    slab, pivots = inverse.shape
    whole = sent_to_all(inverse, ROW).reshape(pivots, pivots)
    operator = -dot(below, whole)
    operator = lax.dynamic_update_slice(operator, inverse, (panel * slab, 0))
    return spread(operator, PLANE, sources)


def per_device(rhs_block, below, inverse, owner_map, row_perm):
    rows_dev, columns = rhs_block.shape
    slab = inverse.shape[1]
    pivots = inverse.shape[2]
    position = lax.axis_index(ROW)
    core = lax.axis_index("core")
    chip = lax.axis_index(CHIP)
    count = lax.axis_size(CHIP)

    working = rhs_block.at[row_perm - position * rows_dev].get(mode="promise_in_bounds")
    pivot = sent_to_all(working[:slab], ROW).reshape(pivots, columns)

    owners = [owner_map[k] for k in range(PANELS)]
    chips = [o // 2 for o in owners]
    cores = [o % 2 for o in owners]
    sources = [(c * count + h).astype(jnp.uint32) for c, h in zip(cores, chips)]
    chip_sources = [h.astype(jnp.uint32) for h in chips]
    twice = (chips[0] == chips[1]) | (chips[0] == chips[2]) | (chips[1] == chips[2])
    own_core = sum(jnp.where(h == chip, c, 0) for c, h in zip(cores, chips))
    panel_chip = sum(jnp.where(h == chip, k, 0) for k, h in enumerate(chips))
    panel_core = sum(
        jnp.where((h == chip) & (c == core), k, 0) for k, (c, h) in enumerate(zip(cores, chips))
    )
    panel = jnp.where(twice, panel_core, panel_chip)
    kept = lax.cond(
        twice,
        own_slots,
        shared_slots,
        below[0],
        inverse[0],
        core,
        own_core,
        panel,
        chip_sources,
        sources,
    )

    kept = sent_to_all(kept, "z")
    kept = sent_to_all(kept, "x")
    other = lax.ppermute(kept, "core", SWAP)
    first = core == 0
    halves = [jnp.where(first, kept, other), jnp.where(first, other, kept)]

    for k in range(PANELS):
        start, end = k * slab, (k + 1) * slab
        panel = jnp.concatenate([h[:, :, k].reshape(rows_dev // 2, pivots) for h in halves], axis=0)
        if k:
            pivot = sent_to_all(working[start:end], ROW).reshape(pivots, columns)
        moved = dot(panel[start:], pivot)
        working = jnp.concatenate(
            [working[:start], moved[:slab], working[end:] + moved[slab:]], axis=0
        )
    return working


def solution(mesh):
    mesh = Mesh(mesh.devices.reshape(4, 8, 2, 8), ("x", "z", "core", "row"))
    rhs = ("x", "z", "core")
    return jax.shard_map(
        per_device,
        mesh=mesh,
        in_specs=(P("row", rhs), P(rhs, "row", None), P(rhs, "row", None), P(), P("row")),
        out_specs=P("row", rhs),
        check_vma=False,
    )
```

time: 204 us -> 194 us (0.951)
  blocking collectives: 57.5 us -> 107 us
  waiting for transfers between devices: 80.1 us -> 36 us
  starting transfers between devices: 36.3 us -> 24 us
    all_to_all x0 -> x1, blocking collectives: none -> 25.7 us  [spread(): lax.all_to_all(operator.reshape(count, rows // count, pivots), axes, 0, 0...]
    all_to_all x3 -> x2, waiting for transfers between devices: 58.2 us -> 32.8 us  [sent_to_all(): lax.all_to_all(jnp.broadcast_to(x[None], (count, *x.shape)), axis, 0, 0,...]
    all_to_all x3 -> x4, blocking collectives: 57.5 us -> 81.4 us  [sent_to_all(): lax.all_to_all(jnp.broadcast_to(x[None], (count, *x.shape)), axis, 0, 0,...]
    all_to_all x1 -> x0, waiting for transfers between devices: 21.9 us -> none  [per_device(): lax.all_to_all(operator.reshape(plane, piece, pivots), PLANE, 0, 0, tiled...]
    all_to_all x1 -> x0, starting transfers between devices: 15.8 us -> none  [per_device(): lax.all_to_all(operator.reshape(plane, piece, pivots), PLANE, 0, 0, tiled...]
    ppermute x1 -> x3, starting transfers between devices: 5.15 us -> 16.3 us  [the longest x1 8.75 us: shared_slots(): got = lax.ppermute(jnp.concatenate([sent_rows, inverse]), 'core', SWAP)]
    all_to_all x3 -> x2, starting transfers between devices: 15.3 us -> 7.64 us  [sent_to_all(): lax.all_to_all(jnp.broadcast_to(x[None], (count, *x.shape)), axis, 0, 0,...]
    ppermute x1 -> x3, waiting for transfers between devices: 0.01 us -> 3.19 us  [the longest x1 1.68 us: shared_slots(): got = lax.ppermute(jnp.concatenate([sent_rows, inverse]), 'core', SWAP)]
  transfers between devices with their start and end apart: 5 -> 5, of which waited for: 4 -> 4; matrix products, arithmetic and copies ran while one was open for 4% -> 3% of each run, Pallas kernels for 0% -> 0%
where the time goes in v2:
time: 194 us; the launch traced here: 193 us
  blocking collectives  107 us (55%)
  waiting for transfers between devices  36 us (19%)
  starting transfers between devices  24 us (12%)
  local copies, waits for them, and re-layouts  9.29 us (5%)
  between operations  7.94 us (4%)
  matrix products  5.07 us (3%)
  other arithmetic  4 us (2%)
    all_to_all x4, blocking collectives, sent_to_all(): lax.all_to_all(jnp.broadcast_to(x[None], (count, *x.shape)), axis, 0, 0,...  81.4 us
    all_to_all x2, waiting for transfers between devices, sent_to_all(): lax.all_to_all(jnp.broadcast_to(x[None], (count, *x.shape)), axis, 0, 0,...  32.8 us
    all_to_all x1, blocking collectives, spread(): lax.all_to_all(operator.reshape(count, rows // count, pivots), axes, 0, 0...  25.7 us
    ppermute x1, starting transfers between devices, shared_slots(): got = lax.ppermute(jnp.concatenate([sent_rows, inverse]), 'core', SWAP)  8.75 us
    all_to_all x2, starting transfers between devices, sent_to_all(): lax.all_to_all(jnp.broadcast_to(x[None], (count, *x.shape)), axis, 0, 0,...  7.64 us
    ppermute x1, starting transfers between devices, per_device(): other = lax.ppermute(kept, 'core', SWAP)  5.18 us
    dot_general x4, matrix products, dot(): jnp.dot(a, b, precision=lax.Precision.HIGHEST, preferred_element_type=jnp...  5.07 us
  transfers between devices with their start and end apart: 5, of which 4 were waited for; matrix products, arithmetic and copies ran while one was open for 3% of the time, Pallas kernels for 0%

profile of v2, /device:TPU:1, one launch (start us, length us, event | category | flops | bytes accessed | tf_op | source)
XLA Modules:
  0.0 193.5 jit_solution(9515863758905405178)
XLA Ops:
  0.0 1.4 fusion.16
  9.1 65.2 %conditional.1 = (f32[3,8,512]{2,1,0:T(8,128)S(1)}) conditional(s32[]{:T(128)} %convert_element_type.21, (s32[]{:T(128)}, s32[]{:T(128)}, s32[]{:T(128)}, pred[]{:T(512)}, s32[]{:T(128)}, /*index=5*/pred[]{:T(512)}, s32[]{:T(128)}, s32[]{:T(128)}, f32[512,512]{1,0:T(8,128)}, f32[64,512]{1,0:T(8,128)}, /*index=10*/s32[]{:T(128)}, u32[]{:T(128)}, ...), branch_computations={%region_0.1_spmd, %region_1.2_spmd} | conditional | flops 1610899456 | bytes 22413768 | solution.py:83
  9.1 1.1 constant_dynamic-slice_fusion.1
  10.2 1.0 pad_maximum_fusion.1
  11.2 8.7 %collective-permute-start = (f32[320,512]{1,0:T(8,128)S(1)}, f32[320,512]{1,0:T(8,128)S(1)}, u32[]{:S(2)}, u32[]{:S(2)}) collective-permute-start(f32[320,512]{1,0:T(8,128)S(1)} %pad_maximum_fusion.1), channel_id=1, source_target_pairs={{0,8},{8,0},{1,9},{9,1},{2,10},{10,2},{3,11},{11,3},{4,12},{12,4},... | collective-permute-start | bytes 1966088 | tf_op jit(solution)/shard_map/cond/branch_0_fun/ppermute | solution.py:35
  19.9 1.7 collective-permute-done
  21.7 20.3 %all_to_all.41 = f32[8,32,512]{2,1,0:T(8,128)S(1)} all-to-all(f32[8,32,512]{2,1,0:T(8,128)S(1)} %broadcast_in_dim.6), channel_id=1, replica_groups=mesh['x'=4,'z'=8,'core'=2,'row'=8] {'row'}, dimensions={0} | all-to-all | bytes 1048576 | tf_op jit(solution)/shard_map/cond/branch_0_fun/all_to_all | solution.py:15
  42.1 2.4 %collective-permute-start.1 = (f32[8,32,512]{2,1,0:T(8,128)S(1)}, f32[8,32,512]{2,1,0:T(8,128)S(1)}, u32[]{:S(2)}, u32[]{:S(2)}) collective-permute-start(f32[8,32,512]{2,1,0:T(8,128)S(1)} %all_to_all.41), channel_id=1, source_target_pairs={{0,8},{8,0},{1,9},{9,1},{2,10},{10,2},{3,11},{11,3},{4,12},{12,4},... | collective-permute-start | bytes 1572872 | tf_op jit(solution)/shard_map/cond/branch_0_fun/ppermute | solution.py:41
  44.5 1.5 collective-permute-done.1
  46.3 1.1 copy-done.1
  47.4 1.1 convolution_negate_fusion
  48.5 25.7 %all_to_all.42 = f32[32,8,512]{2,1,0:T(8,128)S(1)} all-to-all(f32[32,8,512]{2,1,0:T(8,128)S(1)} %bitcast.36), channel_id=1, replica_groups=mesh['x'=4,'z'=8,'core'=2,'row'=8] {'x','z'}, dimensions={0} | all-to-all | bytes 1048576 | tf_op jit(solution)/shard_map/cond/branch_0_fun/all_to_all | solution.py:26
  74.3 18.6 %all_to_all.44 = f32[8,3,8,512]{3,2,1,0:T(8,128)S(1)} all-to-all(f32[8,3,8,512]{3,2,1,0:T(8,128)S(1)} %broadcast_in_dim.25), channel_id=1, replica_groups=mesh['x'=4,'z'=8,'core'=2,'row'=8] {'z'}, dimensions={0} | all-to-all | bytes 786432 | tf_op jit(solution)/shard_map/all_to_all | solution.py:15
  93.1 22.1 %all_to_all.45 = f32[4,8,3,8,512]{4,3,2,1,0:T(8,128)S(1)} all-to-all(f32[4,8,3,8,512]{4,3,2,1,0:T(8,128)S(1)} %broadcast_in_dim.26), channel_id=1, replica_groups=mesh['x'=4,'z'=8,'core'=2,'row'=8] {'x'}, dimensions={0} | all-to-all | bytes 3145728 | tf_op jit(solution)/shard_map/all_to_all | solution.py:15
  115.2 5.2 %collective-permute-start.2 = (f32[4,8,3,8,512]{4,3,2,1,0:T(8,128)S(1)}, f32[4,8,3,8,512]{4,3,2,1,0:T(8,128)}, u32[]{:S(2)}, u32[]{:S(2)}) collective-permute-start(f32[4,8,3,8,512]{4,3,2,1,0:T(8,128)S(1)} %all_to_all.45), channel_id=1, source_target_pairs={{0,8},{8,0},{1,9},{9,1},{2,10},{10,2},{3,11},{11,3},{4,12},{12,4},... | collective-permute-start | bytes 4718600 | tf_op jit(solution)/shard_map/ppermute | solution.py:98
  120.5 1.6 gather_fusion
  122.9 4.1 %all-to-all-start.6 = ((f32[8,64,256]{2,1,0:T(8,128)}), f32[8,64,256]{2,1,0:T(8,128)}, u32[]{:S(2)}, u32[]{:S(2)}) async-start(f32[8,64,256]{2,1,0:T(8,128)} %broadcast_in_dim.28), calls=%async_computation.6 | async-start | bytes 1048576 | tf_op jit(solution)/shard_map/all_to_all | solution.py:15
  127.1 1.8 broadcast_select_fusion.1
  128.8 1.3 fusion.14
  130.1 15.0 %all-to-all-done.6 = f32[8,64,256]{2,1,0:T(8,128)} async-done(((f32[8,64,256]{2,1,0:T(8,128)}), f32[8,64,256]{2,1,0:T(8,128)}, u32[]{:S(2)}, u32[]{:S(2)}) %all-to-all-start.6) | async-done | bytes 524320 | tf_op jit(solution)/shard_map/all_to_all | solution.py:15
  145.1 2.3 %fusion.3 = f32[512,256]{1,0:T(8,128)S(1)} fusion(f32[512,256]{1,0:T(8,128)} %bitcast.15, f32[256,512]{1,0:T(8,128)} %bitcast.44, f32[256,512]{1,0:T(8,128)} %bitcast.43), kind=kOutput, calls=%fused_computation.24 | convolution fusion | flops 805568512 | bytes 2097152 | tf_op jit(solution)/shard_map/dot_general | solution.py:19
  148.3 20.3 %all_to_all.46 = f32[8,64,256]{2,1,0:T(8,128)S(1)} all-to-all(f32[8,64,256]{2,1,0:T(8,128)S(1)} %broadcast_in_dim.29), channel_id=1, replica_groups=mesh['x'=4,'z'=8,'core'=2,'row'=8] {'row'}, dimensions={0} | all-to-all | bytes 1048576 | tf_op jit(solution)/shard_map/all_to_all | solution.py:15
  170.4 3.5 %all-to-all-start.8 = ((f32[8,64,256]{2,1,0:T(8,128)}), f32[8,64,256]{2,1,0:T(8,128)S(1)}, u32[]{:S(2)}, u32[]{:S(2)}) async-start(f32[8,64,256]{2,1,0:T(8,128)} %broadcast_in_dim.30), calls=%async_computation.8 | async-start | bytes 1048576 | tf_op jit(solution)/shard_map/all_to_all | solution.py:15
  173.9 17.8 %all-to-all-done.8 = f32[8,64,256]{2,1,0:T(8,128)S(1)} async-done(((f32[8,64,256]{2,1,0:T(8,128)}), f32[8,64,256]{2,1,0:T(8,128)S(1)}, u32[]{:S(2)}, u32[]{:S(2)}) %all-to-all-start.8) | async-done | bytes 524320 | tf_op jit(solution)/shard_map/all_to_all | solution.py:15
  (41 shorter events, 5.7 us)
Async XLA Ops:
  0.0 120.4 %copy-start = (f32[512,256]{1,0:T(8,128)S(1)}, f32[512,256]{1,0:T(8,128)}, u32[]{:S(2)}) copy-start(f32[512,256]{1,0:T(8,128)} %param.7) | copy-start | bytes 1572868
  9.1 12.5 %copy-start.3 = (f32[64,512]{1,0:T(8,128)S(1)}, f32[64,512]{1,0:T(8,128)}, u32[]{:S(2)}) copy-start(f32[64,512]{1,0:T(8,128)} %get-tuple-element.68) | copy-start | bytes 393220 | tf_op jit(solution)/shard_map/cond
  11.2 10.5 %collective-permute-start = (f32[320,512]{1,0:T(8,128)S(1)}, f32[320,512]{1,0:T(8,128)S(1)}, u32[]{:S(2)}, u32[]{:S(2)}) collective-permute-start(f32[320,512]{1,0:T(8,128)S(1)} %pad_maximum_fusion.1), channel_id=1, source_target_pairs={{0,8},{8,0},{1,9},{9,1},{2,10},{10,2},{3,11},{11,3},{4,12},{12,4},... | collective-permute-start | bytes 1966088 | tf_op jit(solution)/shard_map/cond/branch_0_fun/ppermute | solution.py:35
  42.1 3.9 %collective-permute-start.1 = (f32[8,32,512]{2,1,0:T(8,128)S(1)}, f32[8,32,512]{2,1,0:T(8,128)S(1)}, u32[]{:S(2)}, u32[]{:S(2)}) collective-permute-start(f32[8,32,512]{2,1,0:T(8,128)S(1)} %all_to_all.41), channel_id=1, source_target_pairs={{0,8},{8,0},{1,9},{9,1},{2,10},{10,2},{3,11},{11,3},{4,12},{12,4},... | collective-permute-start | bytes 1572872 | tf_op jit(solution)/shard_map/cond/branch_0_fun/ppermute | solution.py:41
  46.1 1.2 copy-start.1
  93.1 27.4 %copy-start.7 = (s32[512]{0:T(512)S(1)}, s32[512]{0:T(512)}, u32[]{:S(2)}) copy-start(s32[512]{0:T(512)} %param.11) | copy-start | bytes 6148
  115.2 11.8 %collective-permute-start.2 = (f32[4,8,3,8,512]{4,3,2,1,0:T(8,128)S(1)}, f32[4,8,3,8,512]{4,3,2,1,0:T(8,128)}, u32[]{:S(2)}, u32[]{:S(2)}) collective-permute-start(f32[4,8,3,8,512]{4,3,2,1,0:T(8,128)S(1)} %all_to_all.45), channel_id=1, source_target_pairs={{0,8},{8,0},{1,9},{9,1},{2,10},{10,2},{3,11},{11,3},{4,12},{12,4},... | collective-permute-start | bytes 4718600 | tf_op jit(solution)/shard_map/ppermute | solution.py:98
  122.9 22.2 %all-to-all-start.6 = ((f32[8,64,256]{2,1,0:T(8,128)}), f32[8,64,256]{2,1,0:T(8,128)}, u32[]{:S(2)}, u32[]{:S(2)}) async-start(f32[8,64,256]{2,1,0:T(8,128)} %broadcast_in_dim.28), calls=%async_computation.6 | async-start | bytes 1048576 | tf_op jit(solution)/shard_map/all_to_all | solution.py:15
  147.4 0.8 copy-start.5
  169.5 4.4 %copy-start.6 = (f32[448,256]{1,0:T(8,128)}, f32[448,256]{1,0:T(8,128)S(1)}, u32[]{:S(2)}) copy-start(f32[448,256]{1,0:T(8,128)S(1)} %fusion.7) | copy-start | bytes 1376260
  170.4 21.4 %all-to-all-start.8 = ((f32[8,64,256]{2,1,0:T(8,128)}), f32[8,64,256]{2,1,0:T(8,128)S(1)}, u32[]{:S(2)}, u32[]{:S(2)}) async-start(f32[8,64,256]{2,1,0:T(8,128)} %broadcast_in_dim.30), calls=%async_computation.8 | async-start | bytes 1048576 | tf_op jit(solution)/shard_map/all_to_all | solution.py:15
  173.9 18.7 %slice-start = ((f32[512,256]{1,0:T(8,128)}), f32[64,256]{1,0:T(8,128)S(1)}, s32[]{:S(2)}) async-start(f32[512,256]{1,0:T(8,128)} %copy-done.5), calls=%async_computation.9 | async-start | bytes 131072 | tf_op jit(solution)/shard_map/slice | solution.py:109
  191.8 0.9 slice-start.1

commit v3 on v1

v3 whole, which is shorter than its diff:
```python
import jax
import jax.numpy as jnp
from jax import lax
from jax.sharding import Mesh, PartitionSpec as P


PANELS = 3
ROW = "row"
CHIP = ("z", "x")
SWAP = [(0, 1), (1, 0)]


def sent_to_all(x, axis):
    count = lax.axis_size(axis)
    return lax.all_to_all(jnp.broadcast_to(x[None], (count, *x.shape)), axis, 0, 0, tiled=True)


def dot(a, b):
    return jnp.dot(a, b, precision=lax.Precision.HIGHEST, preferred_element_type=jnp.float32)


def both_cores(x, on_first):
    other = lax.ppermute(x, "core", SWAP)
    return jnp.where(on_first, x, other), jnp.where(on_first, other, x)


def spread(operator, sources, pivot):
    groups, across, piece, pivots = operator.shape
    operator, sources, pivot = lax.optimization_barrier((operator, sources, pivot))
    pieces = lax.all_to_all(
        operator.reshape(groups * across, piece, pivots), CHIP, 0, 0, tiled=True
    )
    kept = [lax.dynamic_index_in_dim(pieces, s, 0, keepdims=False) for s in sources]
    return jnp.stack(kept), pivot


def gathered(rows, pivot_rows):
    n, columns = rows.shape[0], pivot_rows.shape[1]
    both = jnp.concatenate([rows[:, :columns], rows[:, columns:], pivot_rows])
    both = sent_to_all(both, ROW)
    rows = jnp.concatenate([both[:, :n], both[:, n : 2 * n]], axis=2)
    return rows, both[:, 2 * n :].reshape(-1, columns)


def with_inverse(operator, rows, panel):
    group = lax.broadcasted_iota(jnp.int32, operator.shape, 0)
    return jnp.where(group == panel, rows[None], operator)


def shared_slots(below, inverse, pivot_rows, core, own_core, panel, panel_core, chips, cores):
    groups, _, half, pivots = below.shape
    inverse = inverse.reshape(1, 2, half, pivots)
    mixed = jnp.concatenate([below, inverse])
    on_first = core == 0
    kept = jnp.where(on_first, mixed[:, 0], mixed[:, 1])
    sent = jnp.where(on_first, mixed[:, 1], mixed[:, 0])
    got = lax.ppermute(sent, "core", SWAP)
    mixed = jnp.where(core == own_core, kept, got)
    part = mixed[groups]
    parts, pivot = gathered(part, pivot_rows)
    low, high = both_cores(parts, on_first)
    whole = jnp.stack([low, high], axis=1).reshape(pivots, pivots)
    operator = -dot(mixed[:groups].reshape(groups * half, pivots), whole)
    operator = with_inverse(operator.reshape(groups, half, pivots), part, panel)
    return spread(operator.reshape(groups, half // 8, 8, pivots), chips, pivot)


def own_slots(below, inverse, pivot_rows, core, own_core, panel, panel_core, chips, cores):
    groups, _, half, pivots = below.shape
    whole, pivot = gathered(inverse, pivot_rows)
    whole = whole.reshape(pivots, pivots)
    operator = -dot(below.reshape(groups * 2 * half, pivots), whole)
    operator = with_inverse(operator.reshape(groups, 2 * half, pivots), inverse, panel_core)
    operator = operator.reshape(groups, 2, half, pivots)
    on_first = core == 0
    mine = jnp.where(on_first, operator[:, 0], operator[:, 1])
    other = jnp.where(on_first, operator[:, 1], operator[:, 0])
    other = lax.ppermute(other, "core", SWAP)
    shape = (groups, half // 8, 8, pivots)
    mine, pivot = spread(mine.reshape(shape), chips, pivot)
    other, pivot = spread(other.reshape(shape), chips, pivot)
    kept = jnp.stack([jnp.where(c == core, mine[k], other[k]) for k, c in enumerate(cores)])
    return kept, pivot


def per_device(rhs_block, below, inverse, owner_map, row_perm):
    rows_dev, columns = rhs_block.shape
    slab, pivots = inverse.shape[1:]
    groups = rows_dev // slab
    position = lax.axis_index(ROW)
    core = lax.axis_index("core")
    nz, nx = lax.axis_size("z"), lax.axis_size("x")
    chip = (lax.axis_index("x") * nz + lax.axis_index("z")).astype(jnp.uint32)

    owners = [owner_map[k].astype(jnp.uint32) for k in range(PANELS)]
    chips = [o >> 1 for o in owners]
    cores = [(o & 1).astype(jnp.int32) for o in owners]
    twice = (chips[0] == chips[1]) | (chips[0] == chips[2]) | (chips[1] == chips[2])
    held = [h == chip for h in chips]
    own_core = jnp.where(held[0], cores[0], jnp.where(held[1], cores[1], cores[2]))
    panel = jnp.where(held[0], 0, jnp.where(held[1], 1, 2))
    panel_core = jnp.where(
        held[0] & (cores[0] == core), 0, jnp.where(held[1] & (cores[1] == core), 1, 2)
    )
    sources = [(h % nz) * nx + h // nz for h in chips]

    working = rhs_block.at[row_perm - position * rows_dev].get(mode="promise_in_bounds")
    kept, pivot = lax.cond(
        twice,
        own_slots,
        shared_slots,
        below[0].reshape(groups, 2, slab // 2, pivots),
        inverse[0],
        working[:slab],
        core,
        own_core,
        panel,
        panel_core,
        sources,
        cores,
    )

    pivot = [pivot]
    kept, on_first = lax.optimization_barrier((kept, core == 0))

    kept = sent_to_all(kept, "z")
    pairs = [(g, k) for g in range(PANELS) for k in range(g)] + [(k, k) for k in range(PANELS)]
    first = sent_to_all(jnp.stack([kept[g, k] for g, k in pairs]), "x")
    first = jnp.concatenate(both_cores(first, on_first))
    first = {at: first[:, n].reshape(slab, pivots) for n, at in enumerate(pairs)}
    rest = lax.all_gather(kept[PANELS:], "x")
    rest = jnp.concatenate(both_cores(rest, on_first))

    for g in range(1, PANELS):
        rows = working[g * slab : (g + 1) * slab]
        for k in range(g):
            rows = rows + dot(first[g, k], pivot[k])
        pivot.append(sent_to_all(rows, ROW).reshape(pivots, columns))

    tail = working[PANELS * slab :]
    pieces, left = rest.shape[:2]
    moved = sum(dot(rest[:, :, k].reshape(-1, pivots), pivot[k]) for k in range(PANELS))
    moved = moved.reshape(pieces, left, -1, columns).swapaxes(0, 1).reshape(tail.shape)
    solved = [dot(first[k, k], pivot[k]) for k in range(PANELS)]
    return jnp.concatenate([*solved, tail + moved])


def solution(mesh):
    mesh4 = Mesh(mesh.devices.reshape(4, 8, 2, 8), ("x", "z", "core", "row"))
    rhs = ("x", "z", "core")

    def step(*args):
        return per_device(*args)

    step = jax.shard_map(
        step,
        mesh=mesh4,
        in_specs=(P("row", rhs), P(rhs, "row", None), P(rhs, "row", None), P(), P("row")),
        out_specs=P("row", rhs),
        check_vma=False,
    )
    return step
```

time: 204 us -> 183 us (0.90)
  waiting for transfers between devices: 80.1 us -> 28.9 us
  blocking collectives: 57.5 us -> 98.4 us
  starting transfers between devices: 36.3 us -> 27.7 us
  between operations: 9.23 us -> 2.25 us
  other arithmetic: 2.77 us -> 9.68 us
  local copies, waits for them, and re-layouts: 10.5 us -> 6.94 us
    all_to_all x3 -> x2, waiting for transfers between devices: 58.2 us -> 25.4 us  [sent_to_all(): lax.all_to_all(jnp.broadcast_to(x[None], (count, *x.shape)), axis, 0, 0,...]
    all_to_all x0 -> x1, blocking collectives: none -> 28.4 us  [spread(): lax.all_to_all(operator.reshape(groups * across, piece, pivots), CHIP, 0,...]
    all_to_all x1 -> x0, waiting for transfers between devices: 21.9 us -> none  [per_device(): lax.all_to_all(operator.reshape(plane, piece, pivots), PLANE, 0, 0, tiled...]
    all_to_all x1 -> x0, starting transfers between devices: 15.8 us -> none  [per_device(): lax.all_to_all(operator.reshape(plane, piece, pivots), PLANE, 0, 0, tiled...]
    ppermute x1 -> x4, starting transfers between devices: 5.15 us -> 20.6 us  [the longest x3 11.8 us: both_cores(): other = lax.ppermute(x, 'core', SWAP)]
    all_gather x0 -> x1, blocking collectives: none -> 12.9 us  [per_device(): rest = lax.all_gather(kept[PANELS:], 'x')]
    all_to_all x3 -> x2, starting transfers between devices: 15.3 us -> 7.16 us  [sent_to_all(): lax.all_to_all(jnp.broadcast_to(x[None], (count, *x.shape)), axis, 0, 0,...]
    ppermute x1 -> x4, waiting for transfers between devices: 0.01 us -> 3.51 us  [the longest x3 1.79 us: both_cores(): other = lax.ppermute(x, 'core', SWAP)]
  transfers between devices with their start and end apart: 5 -> 6, of which waited for: 4 -> 4; matrix products, arithmetic and copies ran while one was open for 4% -> 6% of each run, Pallas kernels for 0% -> 0%
where the time goes in v3:
time: 183 us; the launch traced here: 182 us
  blocking collectives  98.4 us (54%)
  waiting for transfers between devices  28.9 us (16%)
  starting transfers between devices  27.7 us (15%)
  other arithmetic  9.68 us (5%)
  matrix products  8.32 us (5%)
  local copies, waits for them, and re-layouts  6.94 us (4%)
  between operations  2.25 us (1%)
    all_to_all x3, blocking collectives, sent_to_all(): lax.all_to_all(jnp.broadcast_to(x[None], (count, *x.shape)), axis, 0, 0,...  57.1 us
    all_to_all x1, blocking collectives, spread(): lax.all_to_all(operator.reshape(groups * across, piece, pivots), CHIP, 0,...  28.4 us
    all_to_all x2, waiting for transfers between devices, sent_to_all(): lax.all_to_all(jnp.broadcast_to(x[None], (count, *x.shape)), axis, 0, 0,...  25.4 us
    all_gather x1, blocking collectives, per_device(): rest = lax.all_gather(kept[PANELS:], 'x')  12.9 us
    ppermute x3, starting transfers between devices, both_cores(): other = lax.ppermute(x, 'core', SWAP)  11.8 us
    ppermute x1, starting transfers between devices, shared_slots(): got = lax.ppermute(sent, 'core', SWAP)  8.75 us
    dot_general x10, matrix products, dot(): jnp.dot(a, b, precision=lax.Precision.HIGHEST, preferred_element_type=jnp...  8.32 us
    all_to_all x2, starting transfers between devices, sent_to_all(): lax.all_to_all(jnp.broadcast_to(x[None], (count, *x.shape)), axis, 0, 0,...  7.16 us
  transfers between devices with their start and end apart: 6, of which 4 were waited for; matrix products, arithmetic and copies ran while one was open for 6% of the time, Pallas kernels for 0%

profile of v3, /device:TPU:1, one launch (start us, length us, event | category | flops | bytes accessed | tf_op | source)
XLA Modules:
  0.0 182.3 jit_solution(13269353531622338848)
XLA Ops:
  0.0 1.4 fusion.43
  4.0 1.6 gather_fusion
  6.4 80.4 %conditional.1 = (f32[3,8,512]{2,1,0:T(8,128)S(1)}, f32[512,256]{1,0:T(8,128)S(1)}) conditional(s32[]{:T(128)} %convert_element_type.47, (pred[]{:T(512)}, s32[]{:T(128)}, pred[]{:T(512)}, f32[1,64,512]{2,1,0:T(8,128)S(1)}, f32[1,512,512]{2,1,0:T(8,128)S(1)}, /*index=5*/f32[64,256]{1,0:T(8,128)S(1)}, u32[]{:T(128)}, u32[]{:T(128)}, u32[]{:T(128)}, ...), branch_computations={%region_0.1_spmd, %region_1.2_spmd} | conditional | flops 1611796480 | bytes 28180732 | solution.py:108
  6.5 8.7 %collective-permute-start.1 = (f32[9,32,512]{2,1,0:T(8,128)S(1)}, f32[9,32,512]{2,1,0:T(8,128)}, u32[]{:S(2)}, u32[]{:S(2)}) collective-permute-start(f32[9,32,512]{2,1,0:T(8,128)S(1)} %select_bitcast_fusion), channel_id=1, source_target_pairs={{0,8},{8,0},{1,9},{9,1},{2,10},{10,2},{3,11},{11,3},{4,12},{12,4},... | collective-permute-start | bytes 1769480 | tf_op jit(solution)/shard_map/cond/branch_0_fun/ppermute | solution.py:57
  15.3 1.7 collective-permute-done.1
  17.0 1.2 fusion.2
  18.4 31.5 %all_to_all.40 = f32[8,128,256]{2,1,0:T(8,128)S(1)} all-to-all(f32[8,128,256]{2,1,0:T(8,128)S(1)} %broadcast_in_dim.33), channel_id=1, replica_groups=mesh['x'=4,'z'=8,'core'=2,'row'=8] {'row'}, dimensions={0} | all-to-all | bytes 2097152 | tf_op jit(solution)/shard_map/cond/branch_0_fun/all_to_all | solution.py:15
  50.8 2.3 %collective-permute-start.2 = (f32[8,32,512]{2,1,0:T(8,128)}, f32[8,32,512]{2,1,0:T(8,128)}, u32[]{:S(2)}, u32[]{:S(2)}) collective-permute-start(f32[8,32,512]{2,1,0:T(8,128)} %pad_maximum_fusion.2), channel_id=1, source_target_pairs={{0,8},{8,0},{1,9},{9,1},{2,10},{10,2},{3,11},{11,3},{4,12},{12,4},... | collective-permute-start | bytes 1572872 | tf_op jit(solution)/shard_map/cond/branch_0_fun/ppermute | solution.py:23
  53.2 1.8 collective-permute-done.2
  54.9 1.2 select_bitcast_fusion.2
  58.4 28.4 %all_to_all.41 = f32[32,8,512]{2,1,0:T(8,128)S(1)} all-to-all(f32[32,8,512]{2,1,0:T(8,128)S(1)} %bitcast.144), channel_id=1, replica_groups=mesh['x'=4,'z'=8,'core'=2,'row'=8] {'z','x'}, dimensions={0} | all-to-all | bytes 1048576 | tf_op jit(solution)/shard_map/cond/branch_0_fun/all_to_all | solution.py:30
  86.8 17.0 %all_to_all.42 = f32[8,3,8,512]{3,2,1,0:T(8,128)S(1)} all-to-all(f32[8,3,8,512]{3,2,1,0:T(8,128)S(1)} %broadcast_in_dim.43), channel_id=1, replica_groups=mesh['x'=4,'z'=8,'core'=2,'row'=8] {'z'}, dimensions={0} | all-to-all | bytes 786432 | tf_op jit(solution)/shard_map/all_to_all | solution.py:15
  104.0 8.6 %all_to_all.43 = f32[4,6,8,512]{3,2,1,0:T(8,128)S(1)} all-to-all(f32[4,6,8,512]{3,2,1,0:T(8,128)S(1)} %broadcast_in_dim.44), channel_id=1, replica_groups=mesh['x'=4,'z'=8,'core'=2,'row'=8] {'x'}, dimensions={0} | all-to-all | bytes 786432 | tf_op jit(solution)/shard_map/all_to_all | solution.py:15
  112.6 5.3 %collective-permute-start.3 = (f32[4,6,8,512]{3,2,1,0:T(8,128)S(1)}, f32[4,6,8,512]{3,2,1,0:T(8,128)S(1)}, u32[]{:S(2)}, u32[]{:S(2)}) collective-permute-start(f32[4,6,8,512]{3,2,1,0:T(8,128)S(1)} %all_to_all.43), channel_id=1, source_target_pairs={{0,8},{8,0},{1,9},{9,1},{2,10},{10,2},{3,11},{11,3},{4,12},{12,4},... | collective-permute-start | bytes 1179656 | tf_op jit(solution)/shard_map/ppermute | solution.py:23
  117.9 12.9 %all-gather = f32[20,3,8,512]{3,2,1,0:T(8,128)S(1)} all-gather(f32[5,3,8,512]{3,2,1,0:T(8,128)S(1)} %slice.182), channel_id=2, replica_groups=mesh['x'=4,'z'=8,'core'=2,'row'=8] {'x'}, dimensions={0}, use_global_device_ids=true | all-gather | bytes 1228800 | tf_op jit(solution)/shard_map/all_gather | solution.py:131
  130.8 4.2 %collective-permute-start.4 = (f32[4,5,3,8,512]{4,3,2,1,0:T(8,128)S(1)}, f32[4,5,3,8,512]{4,3,2,1,0:T(8,128)}, u32[]{:S(2)}, u32[]{:S(2)}) collective-permute-start(f32[4,5,3,8,512]{4,3,2,1,0:T(8,128)S(1)} %bitcast.138), channel_id=1, source_target_pairs={{0,8},{8,0},{1,9},{9,1},{2,10},{10,2},{3,11},{11,3},{4,12},{12,4},... | collective-permute-start | bytes 2949128 | tf_op jit(solution)/shard_map/ppermute | solution.py:23
  135.1 1.2 convolution_add_fusion.4
  137.2 3.5 %all-to-all-start.7 = ((f32[8,64,256]{2,1,0:T(8,128)}), f32[8,64,256]{2,1,0:T(8,128)S(1)}, u32[]{:S(2)}, u32[]{:S(2)}) async-start(f32[8,64,256]{2,1,0:T(8,128)} %broadcast_in_dim.62), calls=%async_computation.7 | async-start | bytes 1048576 | tf_op jit(solution)/shard_map/all_to_all | solution.py:15
  141.7 1.2 convolution_add_fusion.3
  142.9 2.8 %broadcast_select_fusion.2 = (f32[4,5,3,8,512]{4,3,2,1,0:T(8,128)}, f32[4,5,3,8,512]{4,3,2,1,0:T(8,128)}) fusion(f32[4,5,3,8,512]{4,3,2,1,0:T(8,128)} %collective-permute-done.4, f32[4,5,3,8,512]{4,3,2,1,0:T(8,128)S(1)} %bitcast.139, pred[]{:T(512)S(6)} %eq.67), kind=kLoop, calls=%fused_computation.58 | loop fusion | flops 491520 | bytes 3932161 | tf_op jit(solution)/shard_map/jit(_where)/select_n | solution.py:24
  145.7 13.0 %all-to-all-done.7 = f32[8,64,256]{2,1,0:T(8,128)S(1)} async-done(((f32[8,64,256]{2,1,0:T(8,128)}), f32[8,64,256]{2,1,0:T(8,128)S(1)}, u32[]{:S(2)}, u32[]{:S(2)}) %all-to-all-start.7) | async-done | bytes 524320 | tf_op jit(solution)/shard_map/all_to_all | solution.py:15
  159.9 3.7 %all-to-all-start.8 = ((f32[8,64,256]{2,1,0:T(8,128)}), f32[8,64,256]{2,1,0:T(8,128)S(1)}, u32[]{:S(2)}, u32[]{:S(2)}) async-start(f32[8,64,256]{2,1,0:T(8,128)} %broadcast_in_dim.63), calls=%async_computation.8 | async-start | bytes 1048576 | tf_op jit(solution)/shard_map/all_to_all | solution.py:15
  163.6 1.6 pad_maximum_fusion.8
  167.6 12.4 %all-to-all-done.8 = f32[8,64,256]{2,1,0:T(8,128)S(1)} async-done(((f32[8,64,256]{2,1,0:T(8,128)}), f32[8,64,256]{2,1,0:T(8,128)S(1)}, u32[]{:S(2)}, u32[]{:S(2)}) %all-to-all-start.8) | async-done | bytes 524320 | tf_op jit(solution)/shard_map/all_to_all | solution.py:15
  (59 shorter events, 12.7 us)
Async XLA Ops:
  0.0 4.0 %copy-start = (f32[512,256]{1,0:T(8,128)S(1)}, f32[512,256]{1,0:T(8,128)}, u32[]{:S(2)}) copy-start(f32[512,256]{1,0:T(8,128)} %param.7) | copy-start | bytes 1572868
  4.0 1.7 copy-start.1
  4.0 1.7 copy-start.5
  5.6 0.8 copy-start.3
  6.5 10.5 %collective-permute-start.1 = (f32[9,32,512]{2,1,0:T(8,128)S(1)}, f32[9,32,512]{2,1,0:T(8,128)}, u32[]{:S(2)}, u32[]{:S(2)}) collective-permute-start(f32[9,32,512]{2,1,0:T(8,128)S(1)} %select_bitcast_fusion), channel_id=1, source_target_pairs={{0,8},{8,0},{1,9},{9,1},{2,10},{10,2},{3,11},{11,3},{4,12},{12,4},... | collective-permute-start | bytes 1769480 | tf_op jit(solution)/shard_map/cond/branch_0_fun/ppermute | solution.py:57
  18.2 34.9 %copy-start.2 = (f32[9,32,512]{2,1,0:T(8,128)}, f32[9,32,512]{2,1,0:T(8,128)S(1)}, u32[]{:S(2)}) copy-start(f32[9,32,512]{2,1,0:T(8,128)S(1)} %fusion.2) | copy-start | bytes 1769476 | tf_op jit(solution)/shard_map/cond
  50.8 4.2 %collective-permute-start.2 = (f32[8,32,512]{2,1,0:T(8,128)}, f32[8,32,512]{2,1,0:T(8,128)}, u32[]{:S(2)}, u32[]{:S(2)}) collective-permute-start(f32[8,32,512]{2,1,0:T(8,128)} %pad_maximum_fusion.2), channel_id=1, source_target_pairs={{0,8},{8,0},{1,9},{9,1},{2,10},{10,2},{3,11},{11,3},{4,12},{12,4},... | collective-permute-start | bytes 1572872 | tf_op jit(solution)/shard_map/cond/branch_0_fun/ppermute | solution.py:23
  56.1 1.0 slice-start
  112.6 22.4 %collective-permute-start.3 = (f32[4,6,8,512]{3,2,1,0:T(8,128)S(1)}, f32[4,6,8,512]{3,2,1,0:T(8,128)S(1)}, u32[]{:S(2)}, u32[]{:S(2)}) collective-permute-start(f32[4,6,8,512]{3,2,1,0:T(8,128)S(1)} %all_to_all.43), channel_id=1, source_target_pairs={{0,8},{8,0},{1,9},{9,1},{2,10},{10,2},{3,11},{11,3},{4,12},{12,4},... | collective-permute-start | bytes 1179656 | tf_op jit(solution)/shard_map/ppermute | solution.py:23
  130.8 12.2 %collective-permute-start.4 = (f32[4,5,3,8,512]{4,3,2,1,0:T(8,128)S(1)}, f32[4,5,3,8,512]{4,3,2,1,0:T(8,128)}, u32[]{:S(2)}, u32[]{:S(2)}) collective-permute-start(f32[4,5,3,8,512]{4,3,2,1,0:T(8,128)S(1)} %bitcast.138), channel_id=1, source_target_pairs={{0,8},{8,0},{1,9},{9,1},{2,10},{10,2},{3,11},{11,3},{4,12},{12,4},... | collective-permute-start | bytes 2949128 | tf_op jit(solution)/shard_map/ppermute | solution.py:23
  137.2 21.5 %all-to-all-start.7 = ((f32[8,64,256]{2,1,0:T(8,128)}), f32[8,64,256]{2,1,0:T(8,128)S(1)}, u32[]{:S(2)}, u32[]{:S(2)}) async-start(f32[8,64,256]{2,1,0:T(8,128)} %broadcast_in_dim.62), calls=%async_computation.7 | async-start | bytes 1048576 | tf_op jit(solution)/shard_map/all_to_all | solution.py:15
  159.9 20.1 %all-to-all-start.8 = ((f32[8,64,256]{2,1,0:T(8,128)}), f32[8,64,256]{2,1,0:T(8,128)S(1)}, u32[]{:S(2)}, u32[]{:S(2)}) async-start(f32[8,64,256]{2,1,0:T(8,128)} %broadcast_in_dim.63), calls=%async_computation.8 | async-start | bytes 1048576 | tf_op jit(solution)/shard_map/all_to_all | solution.py:15
  180.4 1.0 copy-start.4
  180.4 1.1 copy-start.6
  180.4 1.1 copy-start.7

commit v4 on v3

--- a/solution.py
+++ b/solution.py
@@ -34,12 +34,10 @@
     return jnp.stack(kept), pivot
 
 
-def gathered(rows, pivot_rows):
-    n, columns = rows.shape[0], pivot_rows.shape[1]
-    both = jnp.concatenate([rows[:, :columns], rows[:, columns:], pivot_rows])
-    both = sent_to_all(both, ROW)
-    rows = jnp.concatenate([both[:, :n], both[:, n : 2 * n]], axis=2)
-    return rows, both[:, 2 * n :].reshape(-1, columns)
+def permuted(rhs_block, row_perm):
+    position = lax.axis_index(ROW)
+    rows = row_perm - position * rhs_block.shape[0]
+    return rhs_block.at[rows].get(mode="promise_in_bounds")
 
 
 def with_inverse(operator, rows, panel):
@@ -47,28 +45,32 @@
     return jnp.where(group == panel, rows[None], operator)
 
 
-def shared_slots(below, inverse, pivot_rows, core, own_core, panel, panel_core, chips, cores):
+def shared_slots(below, inverse, rhs_block, row_perm, core, own_core, panel, panel_core, chips, cores):
     groups, _, half, pivots = below.shape
-    inverse = inverse.reshape(1, 2, half, pivots)
-    mixed = jnp.concatenate([below, inverse])
-    on_first = core == 0
-    kept = jnp.where(on_first, mixed[:, 0], mixed[:, 1])
-    sent = jnp.where(on_first, mixed[:, 1], mixed[:, 0])
-    got = lax.ppermute(sent, "core", SWAP)
-    mixed = jnp.where(core == own_core, kept, got)
-    part = mixed[groups]
-    parts, pivot = gathered(part, pivot_rows)
+    inverse = inverse.reshape(2, half, pivots)
+    on_first, mine = core == 0, core == own_core
+    sent = jnp.where(on_first, inverse[1], inverse[0])
+    kept = jnp.where(on_first, inverse[0], inverse[1])
+    part = jnp.where(mine, kept, lax.ppermute(sent, "core", SWAP))
+    sent = jnp.where(on_first, below[:, 1], below[:, 0])
+    kept = jnp.where(on_first, below[:, 0], below[:, 1])
+    lower = jnp.where(mine, kept, lax.ppermute(sent, "core", SWAP))
+    working = permuted(rhs_block, row_perm)
+    pivot = sent_to_all(working[: 2 * half], ROW).reshape(pivots, -1)
+    parts = lax.all_gather(part, ROW)
     low, high = both_cores(parts, on_first)
     whole = jnp.stack([low, high], axis=1).reshape(pivots, pivots)
-    operator = -dot(mixed[:groups].reshape(groups * half, pivots), whole)
+    operator = -dot(lower.reshape(groups * half, pivots), whole)
     operator = with_inverse(operator.reshape(groups, half, pivots), part, panel)
-    return spread(operator.reshape(groups, half // 8, 8, pivots), chips, pivot)
+    kept, pivot = spread(operator.reshape(groups, half // 8, 8, pivots), chips, pivot)
+    return kept, pivot, working
 
 
-def own_slots(below, inverse, pivot_rows, core, own_core, panel, panel_core, chips, cores):
+def own_slots(below, inverse, rhs_block, row_perm, core, own_core, panel, panel_core, chips, cores):
     groups, _, half, pivots = below.shape
-    whole, pivot = gathered(inverse, pivot_rows)
-    whole = whole.reshape(pivots, pivots)
+    working = permuted(rhs_block, row_perm)
+    pivot = sent_to_all(working[: 2 * half], ROW).reshape(pivots, -1)
+    whole = sent_to_all(inverse, ROW).reshape(pivots, pivots)
     operator = -dot(below.reshape(groups * 2 * half, pivots), whole)
     operator = with_inverse(operator.reshape(groups, 2 * half, pivots), inverse, panel_core)
     operator = operator.reshape(groups, 2, half, pivots)
@@ -80,14 +82,13 @@
     mine, pivot = spread(mine.reshape(shape), chips, pivot)
     other, pivot = spread(other.reshape(shape), chips, pivot)
     kept = jnp.stack([jnp.where(c == core, mine[k], other[k]) for k, c in enumerate(cores)])
-    return kept, pivot
+    return kept, pivot, working
 
 
 def per_device(rhs_block, below, inverse, owner_map, row_perm):
     rows_dev, columns = rhs_block.shape
     slab, pivots = inverse.shape[1:]
     groups = rows_dev // slab
-    position = lax.axis_index(ROW)
     core = lax.axis_index("core")
     nz, nx = lax.axis_size("z"), lax.axis_size("x")
     chip = (lax.axis_index("x") * nz + lax.axis_index("z")).astype(jnp.uint32)
@@ -104,14 +105,14 @@
     )
     sources = [(h % nz) * nx + h // nz for h in chips]
 
-    working = rhs_block.at[row_perm - position * rows_dev].get(mode="promise_in_bounds")
-    kept, pivot = lax.cond(
+    kept, pivot, working = lax.cond(
         twice,
         own_slots,
         shared_slots,
         below[0].reshape(groups, 2, slab // 2, pivots),
         inverse[0],
-        working[:slab],
+        rhs_block,
+        row_perm,
         core,
         own_core,
         panel,
@@ -129,7 +130,7 @@
     first = jnp.concatenate(both_cores(first, on_first))
     first = {at: first[:, n].reshape(slab, pivots) for n, at in enumerate(pairs)}
     rest = lax.all_gather(kept[PANELS:], "x")
-    rest = jnp.concatenate(both_cores(rest, on_first))
+    rest = rest, lax.ppermute(rest, "core", SWAP)
 
     for g in range(1, PANELS):
         rows = working[g * slab : (g + 1) * slab]
@@ -138,9 +139,12 @@
         pivot.append(sent_to_all(rows, ROW).reshape(pivots, columns))
 
     tail = working[PANELS * slab :]
-    pieces, left = rest.shape[:2]
-    moved = sum(dot(rest[:, :, k].reshape(-1, pivots), pivot[k]) for k in range(PANELS))
-    moved = moved.reshape(pieces, left, -1, columns).swapaxes(0, 1).reshape(tail.shape)
+    here, there = (
+        sum(dot(r[:, :, k].reshape(-1, pivots), pivot[k]) for k in range(PANELS)) for r in rest
+    )
+    moved = jnp.stack([jnp.where(on_first, here, there), jnp.where(on_first, there, here)])
+    pieces, left = rest[0].shape[:2]
+    moved = moved.reshape(2 * pieces, left, -1, columns).swapaxes(0, 1).reshape(tail.shape)
     solved = [dot(first[k, k], pivot[k]) for k in range(PANELS)]
     return jnp.concatenate([*solved, tail + moved])
 

time: 183 us -> 197 us (1.077)
  blocking collectives: 98.4 us -> 84.6 us
  waiting for transfers between devices: 28.9 us -> 41.5 us
  starting transfers between devices: 27.7 us -> 40 us
  local copies, waits for them, and re-layouts: 6.94 us -> 12.1 us
  other arithmetic: 9.68 us -> 5.55 us
    all_to_all x3 -> x2, blocking collectives: 57.1 us -> 25.2 us  [sent_to_all(): lax.all_to_all(jnp.broadcast_to(x[None], (count, *x.shape)), axis, 0, 0,...]
    all_gather x0 -> x1, blocking collectives: none -> 19.3 us  [shared_slots(): parts = lax.all_gather(part, ROW)]
    all_to_all x2 -> x3, waiting for transfers between devices: 25.4 us -> 41.5 us  [sent_to_all(): lax.all_to_all(jnp.broadcast_to(x[None], (count, *x.shape)), axis, 0, 0,...]
    ppermute x1 -> x3, starting transfers between devices: 8.75 us -> 15 us  [the longest x1 8.75 us: shared_slots(): part = jnp.where(mine, kept, lax.ppermute(sent, 'core', SWAP))]
    all_to_all x2 -> x3, starting transfers between devices: 7.16 us -> 10.7 us  [sent_to_all(): lax.all_to_all(jnp.broadcast_to(x[None], (count, *x.shape)), axis, 0, 0,...]
    unnamed x19 -> x23, local copies, waits for them, and re-layouts: 1.06 us -> 4.2 us
    select_n x2 -> x1, other arithmetic: 2.85 us -> 0.08 us  [both_cores(): return (jnp.where(on_first, x, other), jnp.where(on_first, other, x))]
    concatenate x3 -> x0, other arithmetic: 2.53 us -> none  [the longest x1 1.64 us: per_device(): rest = jnp.concatenate(both_cores(rest, on_first))]
  transfers between devices with their start and end apart: 6 -> 8, of which waited for: 4 -> 3; matrix products, arithmetic and copies ran while one was open for 6% -> 10% of each run, Pallas kernels for 0% -> 0%
where the time goes in v4:
time: 197 us; the launch traced here: 196 us
  blocking collectives  84.6 us (43%)
  waiting for transfers between devices  41.5 us (21%)
  starting transfers between devices  40 us (20%)
  local copies, waits for them, and re-layouts  12.1 us (6%)
  matrix products  9.64 us (5%)
  other arithmetic  5.55 us (3%)
  between operations  2.19 us (1%)
    all_to_all x3, waiting for transfers between devices, sent_to_all(): lax.all_to_all(jnp.broadcast_to(x[None], (count, *x.shape)), axis, 0, 0,...  41.5 us
    all_to_all x1, blocking collectives, spread(): lax.all_to_all(operator.reshape(groups * across, piece, pivots), CHIP, 0,...  27.1 us
    all_to_all x2, blocking collectives, sent_to_all(): lax.all_to_all(jnp.broadcast_to(x[None], (count, *x.shape)), axis, 0, 0,...  25.2 us
    all_gather x1, blocking collectives, shared_slots(): parts = lax.all_gather(part, ROW)  19.3 us
    ppermute x2, starting transfers between devices, both_cores(): other = lax.ppermute(x, 'core', SWAP)  14.3 us
    all_gather x1, blocking collectives, per_device(): rest = lax.all_gather(kept[PANELS:], 'x')  12.9 us
    all_to_all x3, starting transfers between devices, sent_to_all(): lax.all_to_all(jnp.broadcast_to(x[None], (count, *x.shape)), axis, 0, 0,...  10.7 us
    dot_general x13, matrix products, dot(): jnp.dot(a, b, precision=lax.Precision.HIGHEST, preferred_element_type=jnp...  9.64 us
  transfers between devices with their start and end apart: 8, of which 3 were waited for; matrix products, arithmetic and copies ran while one was open for 10% of the time, Pallas kernels for 0%

profile of v4, /device:TPU:1, one launch (start us, length us, event | category | flops | bytes accessed | tf_op | source)
XLA Modules:
  0.0 195.7 jit_solution(4473786903332980369)
XLA Ops:
  3.9 93.0 %conditional.1 = (f32[3,8,512]{2,1,0:T(8,128)S(1)}, f32[512,256]{1,0:T(8,128)S(1)}, f32[512,256]{1,0:T(8,128)}) conditional(s32[]{:T(128)} %convert_element_type.47, (pred[]{:T(512)}, s32[]{:T(128)}, pred[]{:T(512)}, f32[1,64,512]{2,1,0:T(8,128)}, f32[1,512,512]{2,1,0:T(8,128)}, /*index=5*/s32[512]{0:T(512)S(1)}, f32[512,256]{1,0:T(8,128)}, ...), branch_computations={%region_0.1_spmd, %region_1.2_spmd} | conditional | flops 1611439104 | bytes 33747460 | solution.py:108
  4.8 8.7 %collective-permute-start = (f32[32,512]{1,0:T(8,128)S(1)}, f32[32,512]{1,0:T(8,128)S(1)}, u32[]{:S(2)}, u32[]{:S(2)}) collective-permute-start(f32[32,512]{1,0:T(8,128)S(1)} %select_bitcast_fusion.3), channel_id=1, source_target_pairs={{0,8},{8,0},{1,9},{9,1},{2,10},{10,2},{3,11},{11,3},{4,12},{12,4},... | collective-permute-start | bytes 196616 | tf_op jit(solution)/shard_map/cond/branch_0_fun/ppermute | solution.py:54
  13.6 2.1 %select_bitcast_fusion.2 = f32[8,32,512]{2,1,0:T(8,128)} fusion(f32[8,2,32,512]{3,2,1,0:T(8,128)} %bitcast.144, pred[]{:T(512)S(6)} %eq.45), kind=kLoop, calls=%fused_computation.9 | loop fusion | flops 131072 | bytes 1572865 | tf_op jit(solution)/shard_map/cond/branch_0_fun/jit(_where)/select_n | solution.py:55
  15.7 2.0 %collective-permute-start.1 = (f32[8,32,512]{2,1,0:T(8,128)}, f32[8,32,512]{2,1,0:T(8,128)}, u32[]{:S(2)}, u32[]{:S(2)}) collective-permute-start(f32[8,32,512]{2,1,0:T(8,128)} %select_bitcast_fusion.2), channel_id=1, source_target_pairs={{0,8},{8,0},{1,9},{9,1},{2,10},{10,2},{3,11},{11,3},{4,12},{12,4},... | collective-permute-start | bytes 1572872 | tf_op jit(solution)/shard_map/cond/branch_0_fun/ppermute | solution.py:57
  17.8 19.3 %all-gather = f32[256,512]{1,0:T(8,128)S(1)} all-gather(f32[32,512]{1,0:T(8,128)S(1)} %bitcast_select_fusion.1), channel_id=2, replica_groups=mesh['x'=4,'z'=8,'core'=2,'row'=8] {'row'}, dimensions={0}, use_global_device_ids=true | all-gather | bytes 589824 | tf_op jit(solution)/shard_map/cond/branch_0_fun/all_gather | solution.py:60
  37.2 8.6 %collective-permute-start.2 = (f32[8,32,512]{2,1,0:T(8,128)S(1)}, f32[8,32,512]{2,1,0:T(8,128)S(1)}, u32[]{:S(2)}, u32[]{:S(2)}) collective-permute-start(f32[8,32,512]{2,1,0:T(8,128)S(1)} %bitcast.154), channel_id=1, source_target_pairs={{0,8},{8,0},{1,9},{9,1},{2,10},{10,2},{3,11},{11,3},{4,12},{12,4},... | collective-permute-start | bytes 1572872 | tf_op jit(solution)/shard_map/cond/branch_0_fun/ppermute | solution.py:23
  45.8 1.6 gather_fusion
  48.4 3.5 %all-to-all-start = ((f32[8,64,256]{2,1,0:T(8,128)}), f32[8,64,256]{2,1,0:T(8,128)S(1)}, u32[]{:S(2)}, u32[]{:S(2)}) async-start(f32[8,64,256]{2,1,0:T(8,128)} %broadcast_in_dim.45), calls=%async_computation | async-start | bytes 1048576 | tf_op jit(solution)/shard_map/cond/branch_0_fun/all_to_all | solution.py:15
  51.9 1.2 fusion.1
  54.6 15.3 %all-to-all-done = f32[8,64,256]{2,1,0:T(8,128)S(1)} async-done(((f32[8,64,256]{2,1,0:T(8,128)}), f32[8,64,256]{2,1,0:T(8,128)S(1)}, u32[]{:S(2)}, u32[]{:S(2)}) %all-to-all-start) | async-done | bytes 524320 | tf_op jit(solution)/shard_map/cond/branch_0_fun/all_to_all | solution.py:15
  69.9 27.1 %all_to_all.44 = f32[32,8,512]{2,1,0:T(8,128)S(1)} all-to-all(f32[32,8,512]{2,1,0:T(8,128)S(1)} %bitcast.158), channel_id=1, replica_groups=mesh['x'=4,'z'=8,'core'=2,'row'=8] {'z','x'}, dimensions={0} | all-to-all | bytes 1048576 | tf_op jit(solution)/shard_map/cond/branch_0_fun/all_to_all | solution.py:30
  97.0 16.6 %all_to_all.45 = f32[8,3,8,512]{3,2,1,0:T(8,128)S(1)} all-to-all(f32[8,3,8,512]{3,2,1,0:T(8,128)S(1)} %broadcast_in_dim.72), channel_id=1, replica_groups=mesh['x'=4,'z'=8,'core'=2,'row'=8] {'z'}, dimensions={0} | all-to-all | bytes 786432 | tf_op jit(solution)/shard_map/all_to_all | solution.py:15
  113.7 8.6 %all_to_all.46 = f32[4,6,8,512]{3,2,1,0:T(8,128)S(1)} all-to-all(f32[4,6,8,512]{3,2,1,0:T(8,128)S(1)} %broadcast_in_dim.73), channel_id=1, replica_groups=mesh['x'=4,'z'=8,'core'=2,'row'=8] {'x'}, dimensions={0} | all-to-all | bytes 786432 | tf_op jit(solution)/shard_map/all_to_all | solution.py:15
  122.4 5.6 %collective-permute-start.4 = (f32[4,6,8,512]{3,2,1,0:T(8,128)S(1)}, f32[4,6,8,512]{3,2,1,0:T(8,128)S(1)}, u32[]{:S(2)}, u32[]{:S(2)}) collective-permute-start(f32[4,6,8,512]{3,2,1,0:T(8,128)S(1)} %all_to_all.46), channel_id=1, source_target_pairs={{0,8},{8,0},{1,9},{9,1},{2,10},{10,2},{3,11},{11,3},{4,12},{12,4},... | collective-permute-start | bytes 1179656 | tf_op jit(solution)/shard_map/ppermute | solution.py:23
  128.0 12.9 %all-gather.1 = f32[20,3,8,512]{3,2,1,0:T(8,128)S(1)} all-gather(f32[5,3,8,512]{3,2,1,0:T(8,128)S(1)} %slice.158), channel_id=3, replica_groups=mesh['x'=4,'z'=8,'core'=2,'row'=8] {'x'}, dimensions={0}, use_global_device_ids=true | all-gather | bytes 1228800 | tf_op jit(solution)/shard_map/all_gather | solution.py:132
  140.9 4.2 %collective-permute-start.5 = (f32[4,5,3,8,512]{4,3,2,1,0:T(8,128)S(1)}, f32[4,5,3,8,512]{4,3,2,1,0:T(8,128)}, u32[]{:S(2)}, u32[]{:S(2)}) collective-permute-start(f32[4,5,3,8,512]{4,3,2,1,0:T(8,128)S(1)} %bitcast.152), channel_id=1, source_target_pairs={{0,8},{8,0},{1,9},{9,1},{2,10},{10,2},{3,11},{11,3},{4,12},{12,4},... | collective-permute-start | bytes 2949128 | tf_op jit(solution)/shard_map/ppermute | solution.py:133
  145.3 1.2 convolution_add_fusion.5
  147.3 3.5 %all-to-all-start.8 = ((f32[8,64,256]{2,1,0:T(8,128)}), f32[8,64,256]{2,1,0:T(8,128)S(1)}, u32[]{:S(2)}, u32[]{:S(2)}) async-start(f32[8,64,256]{2,1,0:T(8,128)} %broadcast_in_dim.74), calls=%async_computation.8 | async-start | bytes 1048576 | tf_op jit(solution)/shard_map/all_to_all | solution.py:15
  153.2 1.2 convolution_add_fusion.4
  154.4 14.4 %all-to-all-done.8 = f32[8,64,256]{2,1,0:T(8,128)S(1)} async-done(((f32[8,64,256]{2,1,0:T(8,128)}), f32[8,64,256]{2,1,0:T(8,128)S(1)}, u32[]{:S(2)}, u32[]{:S(2)}) %all-to-all-start.8) | async-done | bytes 524320 | tf_op jit(solution)/shard_map/all_to_all | solution.py:15
  170.0 3.7 %all-to-all-start.9 = ((f32[8,64,256]{2,1,0:T(8,128)}), f32[8,64,256]{2,1,0:T(8,128)S(1)}, u32[]{:S(2)}, u32[]{:S(2)}) async-start(f32[8,64,256]{2,1,0:T(8,128)} %broadcast_in_dim.75), calls=%async_computation.9 | async-start | bytes 1048576 | tf_op jit(solution)/shard_map/all_to_all | solution.py:15
  173.7 2.0 %fusion.38 = (f32[4,5,1,8,512]{4,3,2,1,0:T(8,128)}, f32[4,5,1,8,512]{4,3,2,1,0:T(8,128)S(1)}, f32[4,5,1,8,512]{4,3,2,1,0:T(8,128)S(1)}) fusion(f32[4,5,3,8,512]{4,3,2,1,0:T(8,128)} %collective-permute-done.5), kind=kLoop, calls=%fused_computation.91 | loop fusion | bytes 1966080 | tf_op jit(solution)/shard_map/slice | solution.py:143
  176.7 1.1 fusion.41
  178.3 11.8 %all-to-all-done.9 = f32[8,64,256]{2,1,0:T(8,128)S(1)} async-done(((f32[8,64,256]{2,1,0:T(8,128)}), f32[8,64,256]{2,1,0:T(8,128)S(1)}, u32[]{:S(2)}, u32[]{:S(2)}) %all-to-all-start.9) | async-done | bytes 524320 | tf_op jit(solution)/shard_map/all_to_all | solution.py:15
  (71 shorter events, 16.8 us)
Async XLA Ops:
  0.0 0.7 copy-start.18
  3.2 0.7 copy-start.17
  4.8 13.0 %collective-permute-start = (f32[32,512]{1,0:T(8,128)S(1)}, f32[32,512]{1,0:T(8,128)S(1)}, u32[]{:S(2)}, u32[]{:S(2)}) collective-permute-start(f32[32,512]{1,0:T(8,128)S(1)} %select_bitcast_fusion.3), channel_id=1, source_target_pairs={{0,8},{8,0},{1,9},{9,1},{2,10},{10,2},{3,11},{11,3},{4,12},{12,4},... | collective-permute-start | bytes 196616 | tf_op jit(solution)/shard_map/cond/branch_0_fun/ppermute | solution.py:54
  13.6 4.2 %copy-start.9 = (f32[1,64,512]{2,1,0:T(8,128)S(1)}, f32[1,64,512]{2,1,0:T(8,128)}, u32[]{:S(2)}) copy-start(f32[1,64,512]{2,1,0:T(8,128)} %get-tuple-element.52) | copy-start | bytes 393220 | tf_op jit(solution)/shard_map/cond
  15.7 30.1 %copy-start = (f32[512,256]{1,0:T(8,128)S(1)}, f32[512,256]{1,0:T(8,128)}, u32[]{:S(2)}) copy-start(f32[512,256]{1,0:T(8,128)} %get-tuple-element.57) | copy-start | bytes 1572868 | tf_op jit(solution)/shard_map/cond
  15.7 36.2 %collective-permute-start.1 = (f32[8,32,512]{2,1,0:T(8,128)}, f32[8,32,512]{2,1,0:T(8,128)}, u32[]{:S(2)}, u32[]{:S(2)}) collective-permute-start(f32[8,32,512]{2,1,0:T(8,128)} %select_bitcast_fusion.2), channel_id=1, source_target_pairs={{0,8},{8,0},{1,9},{9,1},{2,10},{10,2},{3,11},{11,3},{4,12},{12,4},... | collective-permute-start | bytes 1572872 | tf_op jit(solution)/shard_map/cond/branch_0_fun/ppermute | solution.py:57
  37.2 16.0 %collective-permute-start.2 = (f32[8,32,512]{2,1,0:T(8,128)S(1)}, f32[8,32,512]{2,1,0:T(8,128)S(1)}, u32[]{:S(2)}, u32[]{:S(2)}) collective-permute-start(f32[8,32,512]{2,1,0:T(8,128)S(1)} %bitcast.154), channel_id=1, source_target_pairs={{0,8},{8,0},{1,9},{9,1},{2,10},{10,2},{3,11},{11,3},{4,12},{12,4},... | collective-permute-start | bytes 1572872 | tf_op jit(solution)/shard_map/cond/branch_0_fun/ppermute | solution.py:23
  47.4 1.0 copy-start.6
  47.4 4.5 %copy-start.4 = (f32[1,512,512]{2,1,0:T(8,128)S(1)}, f32[1,512,512]{2,1,0:T(8,128)}, u32[]{:S(2)}) copy-start(f32[1,512,512]{2,1,0:T(8,128)} %get-tuple-element.102) | copy-start | bytes 3145732 | tf_op jit(solution)/shard_map/cond
  48.4 21.5 %all-to-all-start = ((f32[8,64,256]{2,1,0:T(8,128)}), f32[8,64,256]{2,1,0:T(8,128)S(1)}, u32[]{:S(2)}, u32[]{:S(2)}) async-start(f32[8,64,256]{2,1,0:T(8,128)} %broadcast_in_dim.45), calls=%async_computation | async-start | bytes 1048576 | tf_op jit(solution)/shard_map/cond/branch_0_fun/all_to_all | solution.py:15
  122.4 22.8 %collective-permute-start.4 = (f32[4,6,8,512]{3,2,1,0:T(8,128)S(1)}, f32[4,6,8,512]{3,2,1,0:T(8,128)S(1)}, u32[]{:S(2)}, u32[]{:S(2)}) collective-permute-start(f32[4,6,8,512]{3,2,1,0:T(8,128)S(1)} %all_to_all.46), channel_id=1, source_target_pairs={{0,8},{8,0},{1,9},{9,1},{2,10},{10,2},{3,11},{11,3},{4,12},{12,4},... | collective-permute-start | bytes 1179656 | tf_op jit(solution)/shard_map/ppermute | solution.py:23
  140.9 32.8 %collective-permute-start.5 = (f32[4,5,3,8,512]{4,3,2,1,0:T(8,128)S(1)}, f32[4,5,3,8,512]{4,3,2,1,0:T(8,128)}, u32[]{:S(2)}, u32[]{:S(2)}) collective-permute-start(f32[4,5,3,8,512]{4,3,2,1,0:T(8,128)S(1)} %bitcast.152), channel_id=1, source_target_pairs={{0,8},{8,0},{1,9},{9,1},{2,10},{10,2},{3,11},{11,3},{4,12},{12,4},... | collective-permute-start | bytes 2949128 | tf_op jit(solution)/shard_map/ppermute | solution.py:133
  147.3 21.5 %all-to-all-start.8 = ((f32[8,64,256]{2,1,0:T(8,128)}), f32[8,64,256]{2,1,0:T(8,128)S(1)}, u32[]{:S(2)}, u32[]{:S(2)}) async-start(f32[8,64,256]{2,1,0:T(8,128)} %broadcast_in_dim.74), calls=%async_computation.8 | async-start | bytes 1048576 | tf_op jit(solution)/shard_map/all_to_all | solution.py:15
  170.0 20.1 %all-to-all-start.9 = ((f32[8,64,256]{2,1,0:T(8,128)}), f32[8,64,256]{2,1,0:T(8,128)S(1)}, u32[]{:S(2)}, u32[]{:S(2)}) async-start(f32[8,64,256]{2,1,0:T(8,128)} %broadcast_in_dim.75), calls=%async_computation.9 | async-start | bytes 1048576 | tf_op jit(solution)/shard_map/all_to_all | solution.py:15
  176.7 1.1 copy-start.12
  190.5 1.0 copy-start.11
  191.5 1.0 copy-start.13
  191.5 1.0 copy-start.14
  193.0 1.0 copy-start.8
  194.0 0.8 copy-start.15
  194.0 0.9 copy-start.16

commit v5 on v3

v5 whole, which is shorter than its diff:
```python
import jax
import jax.numpy as jnp
from jax import lax
from jax.sharding import Mesh, PartitionSpec as P


PANELS = 3
ROW = "row"
CHIP = ("z", "x")
SWAP = [(0, 1), (1, 0)]


def sent_to_all(x, axis):
    count = lax.axis_size(axis)
    return lax.all_to_all(jnp.broadcast_to(x[None], (count, *x.shape)), axis, 0, 0, tiled=True)


def dot(a, b):
    return jnp.dot(a, b, precision=lax.Precision.HIGHEST, preferred_element_type=jnp.float32)


def both_cores(x, on_first):
    other = lax.ppermute(x, "core", SWAP)
    return jnp.where(on_first, x, other), jnp.where(on_first, other, x)


def spread(operator, sources):
    groups, across, piece, pivots = operator.shape
    operator, sources = lax.optimization_barrier((operator, sources))
    pieces = lax.all_to_all(
        operator.reshape(groups * across, piece, pivots), CHIP, 0, 0, tiled=True
    )
    return jnp.stack([lax.dynamic_index_in_dim(pieces, s, 0, keepdims=False) for s in sources])


def with_inverse(operator, rows, panel):
    group = lax.broadcasted_iota(jnp.int32, operator.shape, 0)
    return jnp.where(group == panel, rows[None], operator)


def shared_slots(below, inverse, core, own_core, panel, panel_core, chips, cores):
    groups, _, half, pivots = below.shape
    inverse = inverse.reshape(1, 2, half, pivots)
    mixed = jnp.concatenate([below, inverse])
    on_first = core == 0
    kept = jnp.where(on_first, mixed[:, 0], mixed[:, 1])
    sent = jnp.where(on_first, mixed[:, 1], mixed[:, 0])
    got = lax.ppermute(sent, "core", SWAP)
    mixed = jnp.where(core == own_core, kept, got)
    part = mixed[groups]
    low, high = both_cores(sent_to_all(part, ROW), on_first)
    whole = jnp.stack([low, high], axis=1).reshape(pivots, pivots)
    operator = -dot(mixed[:groups].reshape(groups * half, pivots), whole)
    operator = with_inverse(operator.reshape(groups, half, pivots), part, panel)
    return spread(operator.reshape(groups, half // 8, 8, pivots), chips)


def own_slots(below, inverse, core, own_core, panel, panel_core, chips, cores):
    groups, _, half, pivots = below.shape
    whole = sent_to_all(inverse, ROW).reshape(pivots, pivots)
    operator = -dot(below.reshape(groups * 2 * half, pivots), whole)
    operator = with_inverse(operator.reshape(groups, 2 * half, pivots), inverse, panel_core)
    operator = operator.reshape(groups, 2, half, pivots)
    on_first = core == 0
    mine = jnp.where(on_first, operator[:, 0], operator[:, 1])
    other = jnp.where(on_first, operator[:, 1], operator[:, 0])
    other = lax.ppermute(other, "core", SWAP)
    shape = (groups, half // 8, 8, pivots)
    mine = spread(mine.reshape(shape), chips)
    other = spread(other.reshape(shape), chips)
    return jnp.stack([jnp.where(c == core, mine[k], other[k]) for k, c in enumerate(cores)])


def per_device(rhs_block, below, inverse, owner_map, row_perm):
    rows_dev, columns = rhs_block.shape
    slab, pivots = inverse.shape[1:]
    groups = rows_dev // slab
    position = lax.axis_index(ROW)
    core = lax.axis_index("core")
    nz, nx = lax.axis_size("z"), lax.axis_size("x")
    chip = (lax.axis_index("x") * nz + lax.axis_index("z")).astype(jnp.uint32)

    owners = [owner_map[k].astype(jnp.uint32) for k in range(PANELS)]
    chips = [o >> 1 for o in owners]
    cores = [(o & 1).astype(jnp.int32) for o in owners]
    twice = (chips[0] == chips[1]) | (chips[0] == chips[2]) | (chips[1] == chips[2])
    held = [h == chip for h in chips]
    own_core = jnp.where(held[0], cores[0], jnp.where(held[1], cores[1], cores[2]))
    panel = jnp.where(held[0], 0, jnp.where(held[1], 1, 2))
    panel_core = jnp.where(
        held[0] & (cores[0] == core), 0, jnp.where(held[1] & (cores[1] == core), 1, 2)
    )
    sources = [(h % nz) * nx + h // nz for h in chips]

    kept = lax.cond(
        twice,
        own_slots,
        shared_slots,
        below[0].reshape(groups, 2, slab // 2, pivots),
        inverse[0],
        core,
        own_core,
        panel,
        panel_core,
        sources,
        cores,
    )

    kept, on_first = lax.optimization_barrier((kept, core == 0))

    def permuted(start, end):
        rows = row_perm[start:end] - position * rows_dev
        return rhs_block.at[rows].get(mode="promise_in_bounds")

    def to_all_rows(rows):
        return sent_to_all(rows, ROW).reshape(pivots, columns)

    kept = sent_to_all(kept, "z")
    pivot = [to_all_rows(permuted(0, slab))]
    working = permuted(slab, rows_dev)
    pairs = [(g, k) for g in range(PANELS) for k in range(g + 1)]
    first = lax.all_gather(jnp.stack([kept[g, k] for g, k in pairs]), "x")
    first = jnp.concatenate(both_cores(first, on_first))
    first = {at: first[:, n].reshape(slab, pivots) for n, at in enumerate(pairs)}
    parts = []
    for start, end in [(PANELS, groups - 2), (groups - 2, groups)]:
        rest = lax.all_gather(kept[start:end], "x")
        parts.append(jnp.concatenate(both_cores(rest, on_first)))

    for g in range(1, PANELS):
        rows = working[(g - 1) * slab : g * slab]
        for k in range(g):
            rows = rows + dot(first[g, k], pivot[k])
        pivot.append(to_all_rows(rows))

    tail = []
    for rest in parts:
        pieces, left = rest.shape[:2]
        moved = sum(dot(rest[:, :, k].reshape(-1, pivots), pivot[k]) for k in range(PANELS))
        moved = moved.reshape(pieces, left, -1, columns).swapaxes(0, 1)
        tail.append(moved.reshape(left * slab, columns))
    tail = working[(PANELS - 1) * slab :] + jnp.concatenate(tail)
    solved = [dot(first[k, k], pivot[k]) for k in range(PANELS)]
    return jnp.concatenate([*solved, tail])


def solution(mesh):
    mesh4 = Mesh(mesh.devices.reshape(4, 8, 2, 8), ("x", "z", "core", "row"))
    rhs = ("x", "z", "core")

    def step(*args):
        return per_device(*args)

    step = jax.shard_map(
        step,
        mesh=mesh4,
        in_specs=(P("row", rhs), P(rhs, "row", None), P(rhs, "row", None), P(), P("row")),
        out_specs=P("row", rhs),
        check_vma=False,
    )
    return step
```

time: 183 us -> 194 us (1.060)
  blocking collectives: 98.4 us -> 79.8 us
  starting transfers between devices: 27.7 us -> 45.5 us
  waiting for transfers between devices: 28.9 us -> 38.8 us
    all_to_all x3 -> x1, blocking collectives: 57.1 us -> 20.3 us  [sent_to_all(): lax.all_to_all(jnp.broadcast_to(x[None], (count, *x.shape)), axis, 0, 0,...]
    all_gather x1 -> x3, blocking collectives: 12.9 us -> 31.3 us  [the longest x2 21.4 us: per_device(): rest = lax.all_gather(kept[start:end], 'x')]
    all_to_all x2 -> x4, starting transfers between devices: 7.16 us -> 17.8 us  [sent_to_all(): lax.all_to_all(jnp.broadcast_to(x[None], (count, *x.shape)), axis, 0, 0,...]
    all_to_all x2 -> x4, waiting for transfers between devices: 25.4 us -> 35.7 us  [sent_to_all(): lax.all_to_all(jnp.broadcast_to(x[None], (count, *x.shape)), axis, 0, 0,...]
    ppermute x3 -> x4, starting transfers between devices: 11.8 us -> 19 us  [both_cores(): other = lax.ppermute(x, 'core', SWAP)]
    dot_general x10 -> x13, matrix products: 8.32 us -> 9.26 us  [dot(): jnp.dot(a, b, precision=lax.Precision.HIGHEST, preferred_element_type=jnp...]
  transfers between devices with their start and end apart: 6 -> 9, of which waited for: 4 -> 5; matrix products, arithmetic and copies ran while one was open for 6% -> 8% of each run, Pallas kernels for 0% -> 0%
where the time goes in v5:
time: 194 us; the launch traced here: 193 us
  blocking collectives  79.8 us (41%)
  starting transfers between devices  45.5 us (23%)
  waiting for transfers between devices  38.8 us (20%)
  matrix products  9.26 us (5%)
  local copies, waits for them, and re-layouts  8.7 us (4%)
  other arithmetic  8.34 us (4%)
  between operations  2.23 us (1%)
    all_to_all x4, waiting for transfers between devices, sent_to_all(): lax.all_to_all(jnp.broadcast_to(x[None], (count, *x.shape)), axis, 0, 0,...  35.7 us
    all_to_all x1, blocking collectives, spread(): lax.all_to_all(operator.reshape(groups * across, piece, pivots), CHIP, 0,...  28.2 us
    all_gather x2, blocking collectives, per_device(): rest = lax.all_gather(kept[start:end], 'x')  21.4 us
    all_to_all x1, blocking collectives, sent_to_all(): lax.all_to_all(jnp.broadcast_to(x[None], (count, *x.shape)), axis, 0, 0,...  20.3 us
    ppermute x4, starting transfers between devices, both_cores(): other = lax.ppermute(x, 'core', SWAP)  19 us
    all_to_all x4, starting transfers between devices, sent_to_all(): lax.all_to_all(jnp.broadcast_to(x[None], (count, *x.shape)), axis, 0, 0,...  17.8 us
    all_gather x1, blocking collectives, per_device(): first = lax.all_gather(jnp.stack([kept[g, k] for g, k in pairs]), 'x')  9.93 us
    dot_general x13, matrix products, dot(): jnp.dot(a, b, precision=lax.Precision.HIGHEST, preferred_element_type=jnp...  9.26 us
  transfers between devices with their start and end apart: 9, of which 5 were waited for; matrix products, arithmetic and copies ran while one was open for 8% of the time, Pallas kernels for 0%

profile of v5, /device:TPU:1, one launch (start us, length us, event | category | flops | bytes accessed | tf_op | source)
XLA Modules:
  0.0 192.8 jit_solution(1940191779362974041)
XLA Ops:
  0.0 1.4 fusion.39
  3.3 67.0 %conditional.1 = (f32[3,8,512]{2,1,0:T(8,128)S(1)}) conditional(s32[]{:T(128)} %convert_element_type.47, (pred[]{:T(512)}, s32[]{:T(128)}, pred[]{:T(512)}, f32[1,64,512]{2,1,0:T(8,128)}, f32[1,512,512]{2,1,0:T(8,128)}, /*index=5*/u32[]{:T(128)}, u32[]{:T(128)}, u32[]{:T(128)}, s32[]{:T(128)}, pred[]{:T(512)}, /*index=10*/s32[]{:T(128)}, pred[]{:T(512)}, ...), branch_computations={%region_0.1_spmd, %region_1.2_spmd} | conditional | flops 1611436032 | bytes 27722028 | solution.py:95
  3.3 1.5 select_bitcast_fusion
  4.8 8.7 %collective-permute-start.1 = (f32[9,32,512]{2,1,0:T(8,128)S(1)}, f32[9,32,512]{2,1,0:T(8,128)S(1)}, u32[]{:S(2)}, u32[]{:S(2)}) collective-permute-start(f32[9,32,512]{2,1,0:T(8,128)S(1)} %select_bitcast_fusion), channel_id=1, source_target_pairs={{0,8},{8,0},{1,9},{9,1},{2,10},{10,2},{3,11},{11,3},{4,12},{12,4},... | collective-permute-start | bytes 1769480 | tf_op jit(solution)/shard_map/cond/branch_0_fun/ppermute | solution.py:48
  13.6 1.6 collective-permute-done.1
  15.4 20.3 %all_to_all.40 = f32[8,32,512]{2,1,0:T(8,128)S(1)} all-to-all(f32[8,32,512]{2,1,0:T(8,128)S(1)} %broadcast_in_dim.35), channel_id=1, replica_groups=mesh['x'=4,'z'=8,'core'=2,'row'=8] {'row'}, dimensions={0} | all-to-all | bytes 1048576 | tf_op jit(solution)/shard_map/cond/branch_0_fun/all_to_all | solution.py:15
  35.8 2.4 %collective-permute-start.2 = (f32[8,32,512]{2,1,0:T(8,128)S(1)}, f32[8,32,512]{2,1,0:T(8,128)S(1)}, u32[]{:S(2)}, u32[]{:S(2)}) collective-permute-start(f32[8,32,512]{2,1,0:T(8,128)S(1)} %all_to_all.40), channel_id=1, source_target_pairs={{0,8},{8,0},{1,9},{9,1},{2,10},{10,2},{3,11},{11,3},{4,12},{12,4},... | collective-permute-start | bytes 1572872 | tf_op jit(solution)/shard_map/cond/branch_0_fun/ppermute | solution.py:23
  38.2 1.5 collective-permute-done.2
  42.1 28.2 %all_to_all.41 = f32[32,8,512]{2,1,0:T(8,128)S(1)} all-to-all(f32[32,8,512]{2,1,0:T(8,128)S(1)} %bitcast.145), channel_id=1, replica_groups=mesh['x'=4,'z'=8,'core'=2,'row'=8] {'z','x'}, dimensions={0} | all-to-all | bytes 1048576 | tf_op jit(solution)/shard_map/cond/branch_0_fun/all_to_all | solution.py:30
  71.0 3.8 %all-to-all-start.5 = ((f32[8,3,8,512]{3,2,1,0:T(8,128)}), f32[8,3,8,512]{3,2,1,0:T(8,128)S(1)}, u32[]{:S(2)}, u32[]{:S(2)}) async-start(f32[8,3,8,512]{3,2,1,0:T(8,128)} %broadcast_in_dim.64), calls=%async_computation.5 | async-start | bytes 786432 | tf_op jit(solution)/shard_map/all_to_all | solution.py:15
  75.7 11.8 %all-to-all-done.5 = f32[8,3,8,512]{3,2,1,0:T(8,128)S(1)} async-done(((f32[8,3,8,512]{3,2,1,0:T(8,128)}), f32[8,3,8,512]{3,2,1,0:T(8,128)S(1)}, u32[]{:S(2)}, u32[]{:S(2)}) %all-to-all-start.5) | async-done | bytes 393248 | tf_op jit(solution)/shard_map/all_to_all | solution.py:15
  88.3 3.5 %all-to-all-start.6 = ((f32[8,64,256]{2,1,0:T(8,128)}), f32[8,64,256]{2,1,0:T(8,128)S(1)}, u32[]{:S(2)}, u32[]{:S(2)}) async-start(f32[8,64,256]{2,1,0:T(8,128)} %broadcast_in_dim.66), calls=%async_computation.6 | async-start | bytes 1048576 | tf_op jit(solution)/shard_map/all_to_all | solution.py:15
  91.9 9.9 %all-gather = f32[24,8,512]{2,1,0:T(8,128)S(1)} all-gather(f32[6,8,512]{2,1,0:T(8,128)S(1)} %fusion.27), channel_id=2, replica_groups=mesh['x'=4,'z'=8,'core'=2,'row'=8] {'x'}, dimensions={0}, use_global_device_ids=true | all-gather | bytes 491520 | tf_op jit(solution)/shard_map/all_gather | solution.py:122
  101.8 7.5 %collective-permute-start.3 = (f32[4,6,8,512]{3,2,1,0:T(8,128)S(1)}, f32[4,6,8,512]{3,2,1,0:T(8,128)}, u32[]{:S(2)}, u32[]{:S(2)}) collective-permute-start(f32[4,6,8,512]{3,2,1,0:T(8,128)S(1)} %bitcast.154), channel_id=1, source_target_pairs={{0,8},{8,0},{1,9},{9,1},{2,10},{10,2},{3,11},{11,3},{4,12},{12,4},... | collective-permute-start | bytes 1179656 | tf_op jit(solution)/shard_map/ppermute | solution.py:23
  109.4 1.7 gather_fusion.1
  111.1 10.7 %all-gather.2 = f32[8,3,8,512]{3,2,1,0:T(8,128)} all-gather(f32[2,3,8,512]{3,2,1,0:T(8,128)S(1)} %slice.168), channel_id=4, replica_groups=mesh['x'=4,'z'=8,'core'=2,'row'=8] {'x'}, dimensions={0}, use_global_device_ids=true | all-gather | bytes 491520 | tf_op jit(solution)/shard_map/all_gather | solution.py:127
  121.8 4.5 %collective-permute-start.5 = (f32[4,2,3,8,512]{4,3,2,1,0:T(8,128)}, f32[4,2,3,8,512]{4,3,2,1,0:T(8,128)}, u32[]{:S(2)}, u32[]{:S(2)}) collective-permute-start(f32[4,2,3,8,512]{4,3,2,1,0:T(8,128)} %bitcast.53), channel_id=1, source_target_pairs={{0,8},{8,0},{1,9},{9,1},{2,10},{10,2},{3,11},{11,3},{4,12},{12,4},... | collective-permute-start | bytes 1179656 | tf_op jit(solution)/shard_map/ppermute | solution.py:23
  126.4 10.6 %all-gather.1 = f32[12,3,8,512]{3,2,1,0:T(8,128)S(1)} all-gather(f32[3,3,8,512]{3,2,1,0:T(8,128)S(1)} %slice.163), channel_id=3, replica_groups=mesh['x'=4,'z'=8,'core'=2,'row'=8] {'x'}, dimensions={0}, use_global_device_ids=true | all-gather | bytes 737280 | tf_op jit(solution)/shard_map/all_gather | solution.py:127
  137.0 4.5 %collective-permute-start.4 = (f32[4,3,3,8,512]{4,3,2,1,0:T(8,128)S(1)}, f32[4,3,3,8,512]{4,3,2,1,0:T(8,128)}, u32[]{:S(2)}, u32[]{:S(2)}) collective-permute-start(f32[4,3,3,8,512]{4,3,2,1,0:T(8,128)S(1)} %bitcast.142), channel_id=1, source_target_pairs={{0,8},{8,0},{1,9},{9,1},{2,10},{10,2},{3,11},{11,3},{4,12},{12,4},... | collective-permute-start | bytes 1769480 | tf_op jit(solution)/shard_map/ppermute | solution.py:23
  143.8 6.8 %all-to-all-start.7 = ((f32[8,64,256]{2,1,0:T(8,128)}), f32[8,64,256]{2,1,0:T(8,128)S(1)}, u32[]{:S(2)}, u32[]{:S(2)}) async-start(f32[8,64,256]{2,1,0:T(8,128)} %broadcast_in_dim.68), calls=%async_computation.7 | async-start | bytes 1048576 | tf_op jit(solution)/shard_map/all_to_all | solution.py:15
  155.2 1.2 broadcast_select_fusion.2
  157.5 11.2 %all-to-all-done.7 = f32[8,64,256]{2,1,0:T(8,128)S(1)} async-done(((f32[8,64,256]{2,1,0:T(8,128)}), f32[8,64,256]{2,1,0:T(8,128)S(1)}, u32[]{:S(2)}, u32[]{:S(2)}) %all-to-all-start.7) | async-done | bytes 524320 | tf_op jit(solution)/shard_map/all_to_all | solution.py:15
  169.9 3.7 %all-to-all-start.8 = ((f32[8,64,256]{2,1,0:T(8,128)}), f32[8,64,256]{2,1,0:T(8,128)S(1)}, u32[]{:S(2)}, u32[]{:S(2)}) async-start(f32[8,64,256]{2,1,0:T(8,128)} %broadcast_in_dim.69), calls=%async_computation.8 | async-start | bytes 1048576 | tf_op jit(solution)/shard_map/all_to_all | solution.py:15
  177.4 12.6 %all-to-all-done.8 = f32[8,64,256]{2,1,0:T(8,128)S(1)} async-done(((f32[8,64,256]{2,1,0:T(8,128)}), f32[8,64,256]{2,1,0:T(8,128)S(1)}, u32[]{:S(2)}, u32[]{:S(2)}) %all-to-all-start.8) | async-done | bytes 524320 | tf_op jit(solution)/shard_map/all_to_all | solution.py:15
  (83 shorter events, 20.5 us)
Async XLA Ops:
  0.0 74.9 %copy-start = (f32[512,256]{1,0:T(8,128)S(1)}, f32[512,256]{1,0:T(8,128)}, u32[]{:S(2)}) copy-start(f32[512,256]{1,0:T(8,128)} %param.7) | copy-start | bytes 1572868
  3.3 11.9 %copy-start.1 = (f32[1,512,512]{2,1,0:T(8,128)S(1)}, f32[1,512,512]{2,1,0:T(8,128)}, u32[]{:S(2)}) copy-start(f32[1,512,512]{2,1,0:T(8,128)} %get-tuple-element.84) | copy-start | bytes 3145732 | tf_op jit(solution)/shard_map/cond
  3.3 11.9 %copy-start.4 = (f32[1,64,512]{2,1,0:T(8,128)S(1)}, f32[1,64,512]{2,1,0:T(8,128)}, u32[]{:S(2)}) copy-start(f32[1,64,512]{2,1,0:T(8,128)} %get-tuple-element.48) | copy-start | bytes 393220 | tf_op jit(solution)/shard_map/cond
  4.8 10.4 %collective-permute-start.1 = (f32[9,32,512]{2,1,0:T(8,128)S(1)}, f32[9,32,512]{2,1,0:T(8,128)S(1)}, u32[]{:S(2)}, u32[]{:S(2)}) collective-permute-start(f32[9,32,512]{2,1,0:T(8,128)S(1)} %select_bitcast_fusion), channel_id=1, source_target_pairs={{0,8},{8,0},{1,9},{9,1},{2,10},{10,2},{3,11},{11,3},{4,12},{12,4},... | collective-permute-start | bytes 1769480 | tf_op jit(solution)/shard_map/cond/branch_0_fun/ppermute | solution.py:48
  15.3 22.9 %copy-start.3 = (f32[9,32,512]{2,1,0:T(8,128)}, f32[9,32,512]{2,1,0:T(8,128)S(1)}, u32[]{:S(2)}) copy-start(f32[9,32,512]{2,1,0:T(8,128)S(1)} %bitcast_select_fusion) | copy-start | bytes 1769476 | tf_op jit(solution)/shard_map/cond
  35.8 3.9 %collective-permute-start.2 = (f32[8,32,512]{2,1,0:T(8,128)S(1)}, f32[8,32,512]{2,1,0:T(8,128)S(1)}, u32[]{:S(2)}, u32[]{:S(2)}) collective-permute-start(f32[8,32,512]{2,1,0:T(8,128)S(1)} %all_to_all.40), channel_id=1, source_target_pairs={{0,8},{8,0},{1,9},{9,1},{2,10},{10,2},{3,11},{11,3},{4,12},{12,4},... | collective-permute-start | bytes 1572872 | tf_op jit(solution)/shard_map/cond/branch_0_fun/ppermute | solution.py:23
  39.8 1.0 slice-start
  70.2 4.6 %copy-start.16 = (s32[512]{0:T(512)S(1)}, s32[512]{0:T(512)}, u32[]{:S(2)}) copy-start(s32[512]{0:T(512)} %param.11) | copy-start | bytes 6148
  71.0 16.4 %all-to-all-start.5 = ((f32[8,3,8,512]{3,2,1,0:T(8,128)}), f32[8,3,8,512]{3,2,1,0:T(8,128)S(1)}, u32[]{:S(2)}, u32[]{:S(2)}) async-start(f32[8,3,8,512]{3,2,1,0:T(8,128)} %broadcast_in_dim.64), calls=%async_computation.5 | async-start | bytes 786432 | tf_op jit(solution)/shard_map/all_to_all | solution.py:15
  88.3 54.3 %all-to-all-start.6 = ((f32[8,64,256]{2,1,0:T(8,128)}), f32[8,64,256]{2,1,0:T(8,128)S(1)}, u32[]{:S(2)}, u32[]{:S(2)}) async-start(f32[8,64,256]{2,1,0:T(8,128)} %broadcast_in_dim.66), calls=%async_computation.6 | async-start | bytes 1048576 | tf_op jit(solution)/shard_map/all_to_all | solution.py:15
  101.8 39.7 %collective-permute-start.3 = (f32[4,6,8,512]{3,2,1,0:T(8,128)S(1)}, f32[4,6,8,512]{3,2,1,0:T(8,128)}, u32[]{:S(2)}, u32[]{:S(2)}) collective-permute-start(f32[4,6,8,512]{3,2,1,0:T(8,128)S(1)} %bitcast.154), channel_id=1, source_target_pairs={{0,8},{8,0},{1,9},{9,1},{2,10},{10,2},{3,11},{11,3},{4,12},{12,4},... | collective-permute-start | bytes 1179656 | tf_op jit(solution)/shard_map/ppermute | solution.py:23
  121.8 29.9 %collective-permute-start.5 = (f32[4,2,3,8,512]{4,3,2,1,0:T(8,128)}, f32[4,2,3,8,512]{4,3,2,1,0:T(8,128)}, u32[]{:S(2)}, u32[]{:S(2)}) collective-permute-start(f32[4,2,3,8,512]{4,3,2,1,0:T(8,128)} %bitcast.53), channel_id=1, source_target_pairs={{0,8},{8,0},{1,9},{9,1},{2,10},{10,2},{3,11},{11,3},{4,12},{12,4},... | collective-permute-start | bytes 1179656 | tf_op jit(solution)/shard_map/ppermute | solution.py:23
  137.0 18.2 %collective-permute-start.4 = (f32[4,3,3,8,512]{4,3,2,1,0:T(8,128)S(1)}, f32[4,3,3,8,512]{4,3,2,1,0:T(8,128)}, u32[]{:S(2)}, u32[]{:S(2)}) collective-permute-start(f32[4,3,3,8,512]{4,3,2,1,0:T(8,128)S(1)} %bitcast.142), channel_id=1, source_target_pairs={{0,8},{8,0},{1,9},{9,1},{2,10},{10,2},{3,11},{11,3},{4,12},{12,4},... | collective-permute-start | bytes 1769480 | tf_op jit(solution)/shard_map/ppermute | solution.py:23
  143.8 24.9 %all-to-all-start.7 = ((f32[8,64,256]{2,1,0:T(8,128)}), f32[8,64,256]{2,1,0:T(8,128)S(1)}, u32[]{:S(2)}, u32[]{:S(2)}) async-start(f32[8,64,256]{2,1,0:T(8,128)} %broadcast_in_dim.68), calls=%async_computation.7 | async-start | bytes 1048576 | tf_op jit(solution)/shard_map/all_to_all | solution.py:15
  156.4 12.3 %copy-start.13 = (f32[64,256]{1,0:T(8,128)S(1)}, f32[64,256]{1,0:T(8,128)}, u32[]{:S(2)}) copy-start(f32[64,256]{1,0:T(8,128)} %convolution_add_fusion.5) | copy-start | bytes 196612
  169.9 20.1 %all-to-all-start.8 = ((f32[8,64,256]{2,1,0:T(8,128)}), f32[8,64,256]{2,1,0:T(8,128)S(1)}, u32[]{:S(2)}, u32[]{:S(2)}) async-start(f32[8,64,256]{2,1,0:T(8,128)} %broadcast_in_dim.69), calls=%async_computation.8 | async-start | bytes 1048576 | tf_op jit(solution)/shard_map/all_to_all | solution.py:15
  173.6 1.0 copy-start.10
  173.6 2.1 %copy-start.8 = (f32[8,3,1,8,512]{4,3,2,1,0:T(8,128)S(1)}, f32[8,3,1,8,512]{4,3,2,1,0:T(8,128)}, u32[]{:S(2)}) copy-start(f32[8,3,1,8,512]{4,3,2,1,0:T(8,128)} %get-tuple-element.119) | copy-start | bytes 1179652
  174.6 1.6 copy-start.7
  176.2 14.2 %copy-start.12 = (f32[128,256]{1,0:T(8,128)S(1)}, f32[128,256]{1,0:T(8,128)}, u32[]{:S(2)}) copy-start(f32[128,256]{1,0:T(8,128)} %convolution_add_fusion.3) | copy-start | bytes 393220
  177.4 13.0 %copy-start.9 = (f32[8,2,1,8,512]{4,3,2,1,0:T(8,128)S(1)}, f32[8,2,1,8,512]{4,3,2,1,0:T(8,128)}, u32[]{:S(2)}) copy-start(f32[8,2,1,8,512]{4,3,2,1,0:T(8,128)} %get-tuple-element.122) | copy-start | bytes 786436
  190.0 1.0 copy-start.6
  190.0 1.0 copy-start.11
  191.1 0.9 copy-start.15
  (1 other events, 0.8 us)

commit v6 on v5

v6 whole, which is shorter than its diff:
```python
import jax
import jax.numpy as jnp
from jax import lax
from jax.sharding import Mesh, PartitionSpec as P


PANELS = 3
ROW = "row"
CHIP = ("z", "x")
SWAP = [(0, 1), (1, 0)]


def sent_to_all(x, axis):
    count = lax.axis_size(axis)
    return lax.all_to_all(jnp.broadcast_to(x[None], (count, *x.shape)), axis, 0, 0, tiled=True)


def swapped(x):
    return lax.ppermute(x, "core", SWAP)


def dot(a, b):
    return jnp.dot(a, b, precision=lax.Precision.HIGHEST, preferred_element_type=jnp.float32)


def halves(x, on_first, axis):
    low, high = jnp.split(x, 2, axis)
    return jnp.where(on_first, low, high), jnp.where(on_first, high, low)


def spread(operator, sources):
    rows, columns = operator.shape
    count = lax.axis_size(CHIP)
    operator, sources = lax.optimization_barrier((operator, sources))
    pieces = lax.all_to_all(
        operator.reshape(count, rows // count, columns), CHIP, 0, 0, tiled=True
    )
    return jnp.stack([lax.dynamic_index_in_dim(pieces, s, 0, keepdims=False) for s in sources])


def operator_of(below, inverse, own_rows, panel):
    slab = own_rows.shape[0]
    product = -dot(below, inverse)
    group = lax.broadcasted_iota(jnp.int32, product.shape, 0) // slab
    return jnp.where(group == panel, jnp.tile(own_rows, (below.shape[0] // slab, 1)), product)


def shared_slots(lower, whole, part, below, inverse, on_first, panel, panel_core, sources, cores):
    return spread(operator_of(lower, whole, part, panel), sources)


def own_slots(lower, whole, part, below, inverse, on_first, panel, panel_core, sources, cores):
    whole = sent_to_all(inverse, ROW).reshape(-1, inverse.shape[1])
    mine, other = halves(operator_of(below, whole, inverse, panel_core), on_first, 1)
    mine, other = spread(mine, sources), spread(swapped(other), sources)
    here = [(c == 0) == on_first for c in cores]
    return jnp.stack([jnp.where(h, mine[k], other[k]) for k, h in enumerate(here)])


def per_device(rhs_block, below, inverse, owner_map, row_perm):
    rows_dev, columns = rhs_block.shape
    below, inverse = below[0], inverse[0]
    slab, pivots = inverse.shape
    position = lax.axis_index(ROW)
    core = lax.axis_index("core")
    on_first = core == 0
    nz, nx = lax.axis_size("z"), lax.axis_size("x")
    chip = (lax.axis_index("x") * nz + lax.axis_index("z")).astype(jnp.uint32)

    owners = [owner_map[k].astype(jnp.uint32) for k in range(PANELS)]
    chips = [o >> 1 for o in owners]
    cores = [(o & 1).astype(jnp.int32) for o in owners]
    twice = (chips[0] == chips[1]) | (chips[0] == chips[2]) | (chips[1] == chips[2])
    held = [h == chip for h in chips]
    own_core = jnp.where(held[0], cores[0], jnp.where(held[1], cores[1], cores[2]))
    panel = jnp.where(held[0], 0, jnp.where(held[1], 1, 2))
    panel_core = jnp.where(
        held[0] & (cores[0] == core), 0, jnp.where(held[1] & (cores[1] == core), 1, 2)
    )
    sources = [(h % nz) * nx + h // nz for h in chips]

    kept, sent = halves(inverse, on_first, 1)
    part = jnp.where(own_core == core, kept, swapped(sent))
    lower = jnp.where(own_core == core, below, swapped(below))
    whole = sent_to_all(part, ROW).reshape(pivots, -1)
    kept = lax.cond(
        twice,
        own_slots,
        shared_slots,
        lower,
        whole,
        part,
        below,
        inverse,
        on_first,
        panel,
        panel_core,
        sources,
        cores,
    )

    def permuted(start, end):
        rows = row_perm[start:end] - position * rows_dev
        return rhs_block.at[rows].get(mode="promise_in_bounds")

    def to_all_rows(rows):
        return halves(sent_to_all(rows, ROW).reshape(pivots, columns), on_first, 0)

    def product(a, b):
        return dot(a[0], b[0]) + dot(a[1], b[1])

    kept = sent_to_all(kept, "z")
    pivot = [to_all_rows(permuted(0, slab))]
    working = permuted(slab, rows_dev)
    pairs = [(g, k) for g in range(PANELS) for k in range(g + 1)]
    first = lax.all_gather(jnp.stack([kept[g, k] for g, k in pairs]), "x")
    first = first, swapped(first)
    first = {
        at: [f[:, n].reshape(slab, pivots // 2) for f in first] for n, at in enumerate(pairs)
    }
    rest = lax.all_gather(kept[PANELS:], "x")
    rest = rest, swapped(rest)

    for g in range(1, PANELS):
        rows = working[(g - 1) * slab : g * slab]
        for k in range(g):
            rows = rows + product(first[g, k], pivot[k])
        pivot.append(to_all_rows(rows))

    moved = sum(
        product([r[:, :, k].reshape(-1, pivots // 2) for r in rest], pivot[k])
        for k in range(PANELS)
    )
    pieces, left = rest[0].shape[:2]
    moved = moved.reshape(pieces, left, -1, columns).swapaxes(0, 1).reshape(-1, columns)
    solved = [product(first[k, k], pivot[k]) for k in range(PANELS)]
    return jnp.concatenate([*solved, working[(PANELS - 1) * slab :] + moved])


def solution(mesh):
    mesh4 = Mesh(mesh.devices.reshape(4, 8, 2, 8), ("x", "z", "core", "row"))
    rhs = ("x", "z", "core")

    def step(*args):
        return per_device(*args)

    step = jax.shard_map(
        step,
        mesh=mesh4,
        in_specs=(P("row", rhs), P(rhs, "row", None), P(rhs, "row", None), P(), P("row")),
        out_specs=P("row", rhs),
        check_vma=False,
    )
    return step
```

time: 194 us -> 190 us (0.979)
  waiting for transfers between devices: 38.8 us -> 53 us
  blocking collectives: 79.8 us -> 67.6 us
  local copies, waits for them, and re-layouts: 8.7 us -> 15.7 us
  starting transfers between devices: 45.5 us -> 39.2 us
  other arithmetic: 8.34 us -> 2.07 us
    all_to_all x4, waiting for transfers between devices: 35.7 us -> 53 us  [sent_to_all(): lax.all_to_all(jnp.broadcast_to(x[None], (count, *x.shape)), axis, 0, 0,...]
    all_gather x2 -> x1, blocking collectives: 21.4 us -> 12.9 us  [per_device(): rest = lax.all_gather(kept[PANELS:], 'x')]
    unnamed x29 -> x41, local copies, waits for them, and re-layouts: 0.56 us -> 4.93 us
    select_n x6 -> x5, other arithmetic: 5.22 us -> 1.08 us  [the longest x4 1.07 us: halves(): return (jnp.where(on_first, low, high), jnp.where(on_first, high, low))]
    ppermute x5 -> x4, starting transfers between devices: 27.7 us -> 23.7 us  [swapped(): return lax.ppermute(x, 'core', SWAP)]
    slice x4 -> x5, local copies, waits for them, and re-layouts: 0.96 us -> 4.35 us  [the longest x2 2.95 us: per_device(): r[:, :, k].reshape(-1, pivots // 2)]
    all_to_all x1, blocking collectives: 20.3 us -> 17.1 us  [sent_to_all(): lax.all_to_all(jnp.broadcast_to(x[None], (count, *x.shape)), axis, 0, 0,...]
    ppermute x5 -> x4, waiting for transfers between devices: 3.08 us -> 0.01 us  [swapped(): return lax.ppermute(x, 'core', SWAP)]
  transfers between devices with their start and end apart: 9 -> 8, of which waited for: 5 -> 4; matrix products, arithmetic and copies ran while one was open for 8% -> 7% of each run, Pallas kernels for 0% -> 0%
where the time goes in v6:
time: 190 us; the launch traced here: 189 us
  blocking collectives  67.6 us (36%)
  waiting for transfers between devices  53 us (28%)
  starting transfers between devices  39.2 us (21%)
  local copies, waits for them, and re-layouts  15.7 us (8%)
  matrix products  8.82 us (5%)
  between operations  2.32 us (1%)
  other arithmetic  2.07 us (1%)
    all_to_all x4, waiting for transfers between devices, sent_to_all(): lax.all_to_all(jnp.broadcast_to(x[None], (count, *x.shape)), axis, 0, 0,...  53 us
    all_to_all x1, blocking collectives, spread(): lax.all_to_all(operator.reshape(count, rows // count, columns), CHIP, 0,...  27.3 us
    ppermute x4, starting transfers between devices, swapped(): return lax.ppermute(x, 'core', SWAP)  23.7 us
    all_to_all x1, blocking collectives, sent_to_all(): lax.all_to_all(jnp.broadcast_to(x[None], (count, *x.shape)), axis, 0, 0,...  17.1 us
    all_to_all x4, starting transfers between devices, sent_to_all(): lax.all_to_all(jnp.broadcast_to(x[None], (count, *x.shape)), axis, 0, 0,...  15.6 us
    all_gather x1, blocking collectives, per_device(): rest = lax.all_gather(kept[PANELS:], 'x')  12.9 us
    all_gather x1, blocking collectives, per_device(): first = lax.all_gather(jnp.stack([kept[g, k] for g, k in pairs]), 'x')  10.3 us
    dot_general x19, matrix products, dot(): jnp.dot(a, b, precision=lax.Precision.HIGHEST, preferred_element_type=jnp...  8.82 us
  transfers between devices with their start and end apart: 8, of which 4 were waited for; matrix products, arithmetic and copies ran while one was open for 7% of the time, Pallas kernels for 0%

profile of v6, /device:TPU:1, one launch (start us, length us, event | category | flops | bytes accessed | tf_op | source)
XLA Modules:
  0.0 188.7 jit_solution(65022263065055357)
XLA Ops:
  0.0 0.9 slice_select_fusion.8
  1.0 8.7 %collective-permute-start.1 = (f32[64,256]{1,0:T(8,128)S(1)}, f32[64,256]{1,0:T(8,128)S(1)}, u32[]{:S(2)}, u32[]{:S(2)}) collective-permute-start(f32[64,256]{1,0:T(8,128)S(1)} %slice_select_fusion.8), channel_id=1, source_target_pairs={{0,8},{8,0},{1,9},{9,1},{2,10},{10,2},{3,11},{11,3},{4,12},{12,4},... | collective-permute-start | bytes 196616 | tf_op jit(solution)/shard_map/ppermute | solution.py:19
  9.7 1.9 %collective-permute-start.2 = (f32[512,512]{1,0:T(8,128)}, f32[512,512]{1,0:T(8,128)S(1)}, u32[]{:S(2)}, u32[]{:S(2)}) collective-permute-start(f32[512,512]{1,0:T(8,128)} %bitcast.118), channel_id=1, source_target_pairs={{0,8},{8,0},{1,9},{9,1},{2,10},{10,2},{3,11},{11,3},{4,12},{12,4},... | collective-permute-start | bytes 3145736 | tf_op jit(solution)/shard_map/ppermute | solution.py:19
  15.1 3.5 %all-to-all-start.4 = ((f32[8,64,256]{2,1,0:T(8,128)}), f32[8,64,256]{2,1,0:T(8,128)S(1)}, u32[]{:S(2)}, u32[]{:S(2)}) async-start(f32[8,64,256]{2,1,0:T(8,128)} %broadcast_in_dim.17), calls=%async_computation.4 | async-start | bytes 1048576 | tf_op jit(solution)/shard_map/all_to_all | solution.py:15
  19.9 16.5 %all-to-all-done.4 = f32[8,64,256]{2,1,0:T(8,128)S(1)} async-done(((f32[8,64,256]{2,1,0:T(8,128)}), f32[8,64,256]{2,1,0:T(8,128)S(1)}, u32[]{:S(2)}, u32[]{:S(2)}) %all-to-all-start.4) | async-done | bytes 524320 | tf_op jit(solution)/shard_map/all_to_all | solution.py:15
  36.4 28.7 %conditional.1 = (f32[3,16,256]{2,1,0:T(8,128)S(1)}) conditional(s32[]{:T(128)} %convert_element_type.47, (pred[]{:T(512)}, pred[]{:T(512)}, f32[64,256]{1,0:T(8,128)S(1)}, pred[]{:T(512)}, f32[512,512]{1,0:T(8,128)S(1)}, /*index=5*/f32[512,512]{1,0:T(8,128)S(1)}, f32[8,64,256]{2,1,0:T(8,128)S(1)}, u32[]{:T(128)}, u32[]{:T(128)}, ...), branch_computations={%region_0.1_spmd, %region_1.2_spmd} | conditional | flops 1611963904 | bytes 16114938 | solution.py:86
  36.5 1.3 fusion
  37.8 27.3 %all_to_all.41 = f32[32,16,256]{2,1,0:T(8,128)S(1)} all-to-all(f32[32,16,256]{2,1,0:T(8,128)S(1)} %bitcast.135), channel_id=1, replica_groups=mesh['x'=4,'z'=8,'core'=2,'row'=8] {'z','x'}, dimensions={0} | all-to-all | bytes 1048576 | tf_op jit(solution)/shard_map/cond/branch_0_fun/all_to_all | solution.py:35
  65.2 17.1 %all_to_all.42 = f32[8,64,256]{2,1,0:T(8,128)S(1)} all-to-all(f32[8,64,256]{2,1,0:T(8,128)S(1)} %broadcast_in_dim.20), channel_id=1, replica_groups=mesh['x'=4,'z'=8,'core'=2,'row'=8] {'row'}, dimensions={0} | all-to-all | bytes 1048576 | tf_op jit(solution)/shard_map/all_to_all | solution.py:15
  83.1 4.8 %all-to-all-start.5 = ((f32[8,3,16,256]{3,2,1,0:T(8,128)}), f32[8,3,16,256]{3,2,1,0:T(8,128)S(1)}, u32[]{:S(2)}, u32[]{:S(2)}) async-start(f32[8,3,16,256]{3,2,1,0:T(8,128)} %broadcast_in_dim.18), calls=%async_computation.5 | async-start | bytes 786432 | tf_op jit(solution)/shard_map/all_to_all | solution.py:15
  87.9 1.7 gather_fusion.1
  89.7 9.5 %all-to-all-done.5 = f32[8,3,16,256]{3,2,1,0:T(8,128)S(1)} async-done(((f32[8,3,16,256]{3,2,1,0:T(8,128)}), f32[8,3,16,256]{3,2,1,0:T(8,128)S(1)}, u32[]{:S(2)}, u32[]{:S(2)}) %all-to-all-start.5) | async-done | bytes 393248 | tf_op jit(solution)/shard_map/all_to_all | solution.py:15
  99.2 10.3 %all-gather = f32[24,16,256]{2,1,0:T(8,128)S(1)} all-gather(f32[6,16,256]{2,1,0:T(8,128)S(1)} %fusion.15), channel_id=2, replica_groups=mesh['x'=4,'z'=8,'core'=2,'row'=8] {'x'}, dimensions={0}, use_global_device_ids=true | all-gather | bytes 491520 | tf_op jit(solution)/shard_map/all_gather | solution.py:116
  110.2 8.9 %collective-permute-start.3 = (f32[4,6,16,256]{3,2,1,0:T(8,128)S(1)}, f32[4,6,16,256]{3,2,1,0:T(8,128)S(1)}, u32[]{:S(2)}, u32[]{:S(2)}) collective-permute-start(f32[4,6,16,256]{3,2,1,0:T(8,128)S(1)} %bitcast.138), channel_id=1, source_target_pairs={{0,8},{8,0},{1,9},{9,1},{2,10},{10,2},{3,11},{11,3},{4,12},{12,4},... | collective-permute-start | bytes 1179656 | tf_op jit(solution)/shard_map/ppermute | solution.py:19
  119.1 12.9 %all-gather.1 = f32[20,3,16,256]{3,2,1,0:T(8,128)S(1)} all-gather(f32[5,3,16,256]{3,2,1,0:T(8,128)S(1)} %slice.163), channel_id=3, replica_groups=mesh['x'=4,'z'=8,'core'=2,'row'=8] {'x'}, dimensions={0}, use_global_device_ids=true | all-gather | bytes 1228800 | tf_op jit(solution)/shard_map/all_gather | solution.py:121
  132.8 4.1 %collective-permute-start.4 = (f32[4,5,3,16,256]{4,3,2,1,0:T(8,128)S(1)}, f32[4,5,3,16,256]{4,3,2,1,0:T(8,128)}, u32[]{:S(2)}, u32[]{:S(2)}) collective-permute-start(f32[4,5,3,16,256]{4,3,2,1,0:T(8,128)S(1)} %bitcast.129), channel_id=1, source_target_pairs={{0,8},{8,0},{1,9},{9,1},{2,10},{10,2},{3,11},{11,3},{4,12},{12,4},... | collective-permute-start | bytes 2949128 | tf_op jit(solution)/shard_map/ppermute | solution.py:19
  137.2 0.9 fusion.29
  138.1 1.1 fusion.32
  141.0 3.5 %all-to-all-start.7 = ((f32[8,64,256]{2,1,0:T(8,128)}), f32[8,64,256]{2,1,0:T(8,128)S(1)}, u32[]{:S(2)}, u32[]{:S(2)}) async-start(f32[8,64,256]{2,1,0:T(8,128)} %broadcast_in_dim.22), calls=%async_computation.7 | async-start | bytes 1048576 | tf_op jit(solution)/shard_map/all_to_all | solution.py:15
  146.2 0.9 fusion.13
  147.1 2.1 %fusion.21 = (f32[4,5,1,16,256]{4,3,2,1,0:T(8,128)}, f32[4,5,1,16,256]{4,3,2,1,0:T(8,128)}, f32[4,5,1,16,256]{4,3,2,1,0:T(8,128)}) fusion(f32[4,5,3,16,256]{4,3,2,1,0:T(8,128)} %collective-permute-done.4), kind=kLoop, calls=%fused_computation.74 | loop fusion | bytes 1966080 | tf_op jit(solution)/shard_map/slice | solution.py:131
  149.2 13.2 %all-to-all-done.7 = f32[8,64,256]{2,1,0:T(8,128)S(1)} async-done(((f32[8,64,256]{2,1,0:T(8,128)}), f32[8,64,256]{2,1,0:T(8,128)S(1)}, u32[]{:S(2)}, u32[]{:S(2)}) %all-to-all-start.7) | async-done | bytes 524320 | tf_op jit(solution)/shard_map/all_to_all | solution.py:15
  164.5 3.8 %all-to-all-start.8 = ((f32[8,64,256]{2,1,0:T(8,128)}), f32[8,64,256]{2,1,0:T(8,128)S(1)}, u32[]{:S(2)}, u32[]{:S(2)}) async-start(f32[8,64,256]{2,1,0:T(8,128)} %broadcast_in_dim.23), calls=%async_computation.8 | async-start | bytes 1048576 | tf_op jit(solution)/shard_map/all_to_all | solution.py:15
  171.0 13.8 %all-to-all-done.8 = f32[8,64,256]{2,1,0:T(8,128)S(1)} async-done(((f32[8,64,256]{2,1,0:T(8,128)}), f32[8,64,256]{2,1,0:T(8,128)S(1)}, u32[]{:S(2)}, u32[]{:S(2)}) %all-to-all-start.8) | async-done | bytes 524320 | tf_op jit(solution)/shard_map/all_to_all | solution.py:15
  (88 shorter events, 17.6 us)
Async XLA Ops:
  0.0 19.3 %copy-start = (f32[512,256]{1,0:T(8,128)S(1)}, f32[512,256]{1,0:T(8,128)}, u32[]{:S(2)}) copy-start(f32[512,256]{1,0:T(8,128)} %param.7) | copy-start | bytes 1572868
  0.0 14.2 %copy-start.7 = (f32[1,64,512]{2,1,0:T(8,128)S(1)}, f32[1,64,512]{2,1,0:T(8,128)}, u32[]{:S(2)}) copy-start(f32[1,64,512]{2,1,0:T(8,128)} %param.9) | copy-start | bytes 393220
  1.0 10.7 %copy-start.16 = (s32[64]{0:T(128)S(1)}, s32[64]{0:T(128)}, u32[]{:S(2)}) copy-start(s32[64]{0:T(128)} %param.10) | copy-start | bytes 772
  1.0 13.2 %collective-permute-start.1 = (f32[64,256]{1,0:T(8,128)S(1)}, f32[64,256]{1,0:T(8,128)S(1)}, u32[]{:S(2)}, u32[]{:S(2)}) collective-permute-start(f32[64,256]{1,0:T(8,128)S(1)} %slice_select_fusion.8), channel_id=1, source_target_pairs={{0,8},{8,0},{1,9},{9,1},{2,10},{10,2},{3,11},{11,3},{4,12},{12,4},... | collective-permute-start | bytes 196616 | tf_op jit(solution)/shard_map/ppermute | solution.py:19
  9.7 26.7 %collective-permute-start.2 = (f32[512,512]{1,0:T(8,128)}, f32[512,512]{1,0:T(8,128)S(1)}, u32[]{:S(2)}, u32[]{:S(2)}) collective-permute-start(f32[512,512]{1,0:T(8,128)} %bitcast.118), channel_id=1, source_target_pairs={{0,8},{8,0},{1,9},{9,1},{2,10},{10,2},{3,11},{11,3},{4,12},{12,4},... | collective-permute-start | bytes 3145736 | tf_op jit(solution)/shard_map/ppermute | solution.py:19
  14.2 22.2 %copy-start.1 = (f32[1,512,512]{2,1,0:T(8,128)S(1)}, f32[1,512,512]{2,1,0:T(8,128)}, u32[]{:S(2)}) copy-start(f32[1,512,512]{2,1,0:T(8,128)} %param.8) | copy-start | bytes 3145732
  15.1 21.4 %all-to-all-start.4 = ((f32[8,64,256]{2,1,0:T(8,128)}), f32[8,64,256]{2,1,0:T(8,128)S(1)}, u32[]{:S(2)}, u32[]{:S(2)}) async-start(f32[8,64,256]{2,1,0:T(8,128)} %broadcast_in_dim.17), calls=%async_computation.4 | async-start | bytes 1048576 | tf_op jit(solution)/shard_map/all_to_all | solution.py:15
  83.1 16.1 %all-to-all-start.5 = ((f32[8,3,16,256]{3,2,1,0:T(8,128)}), f32[8,3,16,256]{3,2,1,0:T(8,128)S(1)}, u32[]{:S(2)}, u32[]{:S(2)}) async-start(f32[8,3,16,256]{3,2,1,0:T(8,128)} %broadcast_in_dim.18), calls=%async_computation.5 | async-start | bytes 786432 | tf_op jit(solution)/shard_map/all_to_all | solution.py:15
  110.2 29.0 %collective-permute-start.3 = (f32[4,6,16,256]{3,2,1,0:T(8,128)S(1)}, f32[4,6,16,256]{3,2,1,0:T(8,128)S(1)}, u32[]{:S(2)}, u32[]{:S(2)}) collective-permute-start(f32[4,6,16,256]{3,2,1,0:T(8,128)S(1)} %bitcast.138), channel_id=1, source_target_pairs={{0,8},{8,0},{1,9},{9,1},{2,10},{10,2},{3,11},{11,3},{4,12},{12,4},... | collective-permute-start | bytes 1179656 | tf_op jit(solution)/shard_map/ppermute | solution.py:19
  132.8 14.3 %collective-permute-start.4 = (f32[4,5,3,16,256]{4,3,2,1,0:T(8,128)S(1)}, f32[4,5,3,16,256]{4,3,2,1,0:T(8,128)}, u32[]{:S(2)}, u32[]{:S(2)}) collective-permute-start(f32[4,5,3,16,256]{4,3,2,1,0:T(8,128)S(1)} %bitcast.129), channel_id=1, source_target_pairs={{0,8},{8,0},{1,9},{9,1},{2,10},{10,2},{3,11},{11,3},{4,12},{12,4},... | collective-permute-start | bytes 2949128 | tf_op jit(solution)/shard_map/ppermute | solution.py:19
  141.0 21.5 %all-to-all-start.7 = ((f32[8,64,256]{2,1,0:T(8,128)}), f32[8,64,256]{2,1,0:T(8,128)S(1)}, u32[]{:S(2)}, u32[]{:S(2)}) async-start(f32[8,64,256]{2,1,0:T(8,128)} %broadcast_in_dim.22), calls=%async_computation.7 | async-start | bytes 1048576 | tf_op jit(solution)/shard_map/all_to_all | solution.py:15
  144.5 0.8 copy-start.8
  145.3 0.9 copy-start.14
  149.2 13.3 %copy-start.11 = (f32[4,1,16,256]{3,2,1,0:T(8,128)S(1)}, f32[4,1,16,256]{3,2,1,0:T(8,128)}, u32[]{:S(2)}) copy-start(f32[4,1,16,256]{3,2,1,0:T(8,128)} %get-tuple-element.133) | copy-start | bytes 196612
  162.5 0.8 copy-start.12
  162.5 0.9 copy-start.15
  164.5 3.8 %copy-start.10 = (f32[4,1,16,256]{3,2,1,0:T(8,128)S(1)}, f32[4,1,16,256]{3,2,1,0:T(8,128)}, u32[]{:S(2)}) copy-start(f32[4,1,16,256]{3,2,1,0:T(8,128)} %get-tuple-element.137) | copy-start | bytes 196612
  164.5 20.2 %all-to-all-start.8 = ((f32[8,64,256]{2,1,0:T(8,128)}), f32[8,64,256]{2,1,0:T(8,128)S(1)}, u32[]{:S(2)}, u32[]{:S(2)}) async-start(f32[8,64,256]{2,1,0:T(8,128)} %broadcast_in_dim.23), calls=%async_computation.8 | async-start | bytes 1048576 | tf_op jit(solution)/shard_map/all_to_all | solution.py:15
  168.6 1.0 copy-start.3
  169.5 1.0 copy-start.5
  170.9 13.8 %copy-start.9 = (f32[4,1,16,256]{3,2,1,0:T(8,128)S(1)}, f32[4,1,16,256]{3,2,1,0:T(8,128)}, u32[]{:S(2)}) copy-start(f32[4,1,16,256]{3,2,1,0:T(8,128)} %get-tuple-element.135) | copy-start | bytes 196612
  185.0 1.0 copy-start.4
  186.0 1.0 copy-start.2
  186.0 1.1 copy-start.6
  (2 other events, 1.5 us)

commit v7 on v6

--- a/solution.py
+++ b/solution.py
@@ -113,28 +113,35 @@
     pivot = [to_all_rows(permuted(0, slab))]
     working = permuted(slab, rows_dev)
     pairs = [(g, k) for g in range(PANELS) for k in range(g + 1)]
-    first = lax.all_gather(jnp.stack([kept[g, k] for g, k in pairs]), "x")
+    first = jnp.stack([kept[g, k] for g, k in pairs])
+    first = lax.all_gather(first, "x", axis=1, tiled=True)
     first = first, swapped(first)
-    first = {
-        at: [f[:, n].reshape(slab, pivots // 2) for f in first] for n, at in enumerate(pairs)
-    }
-    rest = lax.all_gather(kept[PANELS:], "x")
+
+    def own_group(g, k):
+        return [f[pairs.index((g, k))] for f in first]
+
+    rest = lax.all_gather(kept[PANELS:].swapaxes(0, 1), "x", axis=2, tiled=True)
+    rest = rest.reshape(PANELS, -1, pivots // 2)
     rest = rest, swapped(rest)
 
-    for g in range(1, PANELS):
-        rows = working[(g - 1) * slab : g * slab]
-        for k in range(g):
-            rows = rows + product(first[g, k], pivot[k])
-        pivot.append(to_all_rows(rows))
+    rows = [working[g * slab : (g + 1) * slab] for g in range(PANELS - 1)]
+    tail = working[(PANELS - 1) * slab :]
+    solved = []
 
-    moved = sum(
-        product([r[:, :, k].reshape(-1, pivots // 2) for r in rest], pivot[k])
-        for k in range(PANELS)
-    )
-    pieces, left = rest[0].shape[:2]
-    moved = moved.reshape(pieces, left, -1, columns).swapaxes(0, 1).reshape(-1, columns)
-    solved = [product(first[k, k], pivot[k]) for k in range(PANELS)]
-    return jnp.concatenate([*solved, working[(PANELS - 1) * slab :] + moved])
+    rows[0] = rows[0] + product(own_group(1, 0), pivot[0])
+    rows, first, pivot = lax.optimization_barrier((rows, first, pivot))
+    pivot.append(to_all_rows(rows[0]))
+    solved.append(product(own_group(0, 0), pivot[0]))
+    rows[1] = rows[1] + product(own_group(2, 0), pivot[0])
+    tail = tail + product([r[0] for r in rest], pivot[0])
+    rows[1] = rows[1] + product(own_group(2, 1), pivot[1])
+    rows, tail, solved = lax.optimization_barrier((rows, tail, solved))
+    pivot.append(to_all_rows(rows[1]))
+    pivot, first, rest, tail = lax.optimization_barrier((pivot, first, rest, tail))
+    for k in range(1, PANELS):
+        solved.append(product(own_group(k, k), pivot[k]))
+        tail = tail + product([r[k] for r in rest], pivot[k])
+    return jnp.concatenate([*solved, tail])
 
 
 def solution(mesh):

time: 190 us -> 192 us (1.011)
  blocking collectives: 67.6 us -> 93.9 us
  waiting for transfers between devices: 53 us -> 40.7 us
  starting transfers between devices: 39.2 us -> 29.3 us
  local copies, waits for them, and re-layouts: 15.7 us -> 9.94 us
  matrix products: 8.82 us -> 13.2 us
    all_to_all x1 -> x2, blocking collectives: 17.1 us -> 39.9 us  [sent_to_all(): lax.all_to_all(jnp.broadcast_to(x[None], (count, *x.shape)), axis, 0, 0,...]
    all_to_all x4 -> x3, waiting for transfers between devices: 53 us -> 40.7 us  [sent_to_all(): lax.all_to_all(jnp.broadcast_to(x[None], (count, *x.shape)), axis, 0, 0,...]
    ppermute x4, starting transfers between devices: 23.7 us -> 18.6 us  [swapped(): return lax.ppermute(x, 'core', SWAP)]
    all_to_all x4 -> x3, starting transfers between devices: 15.6 us -> 10.7 us  [sent_to_all(): lax.all_to_all(jnp.broadcast_to(x[None], (count, *x.shape)), axis, 0, 0,...]
    dot_general x19, matrix products: 8.82 us -> 13.2 us  [dot(): jnp.dot(a, b, precision=lax.Precision.HIGHEST, preferred_element_type=jnp...]
    slice x5 -> x3, local copies, waits for them, and re-layouts: 4.35 us -> 0.75 us  [the longest x1 0.74 us: per_device(): tail = tail + product([r[0] for r in rest], pivot[0])]
    all_gather x2, blocking collectives: 23.1 us -> 25.9 us  [the longest x1 13.5 us: per_device(): rest = lax.all_gather(kept[PANELS:].swapaxes(0, 1), 'x', axis=2, tiled=True)]
    unnamed x41 -> x25, local copies, waits for them, and re-layouts: 4.93 us -> 2.67 us
  transfers between devices with their start and end apart: 8 -> 7, of which waited for: 4 -> 3; matrix products, arithmetic and copies ran while one was open for 7% -> 6% of each run, Pallas kernels for 0% -> 0%
where the time goes in v7:
time: 192 us; the launch traced here: 191 us
  blocking collectives  93.9 us (49%)
  waiting for transfers between devices  40.7 us (21%)
  starting transfers between devices  29.3 us (15%)
  matrix products  13.2 us (7%)
  local copies, waits for them, and re-layouts  9.94 us (5%)
  between operations  2.31 us (1%)
  other arithmetic  2.02 us (1%)
    all_to_all x3, waiting for transfers between devices, sent_to_all(): lax.all_to_all(jnp.broadcast_to(x[None], (count, *x.shape)), axis, 0, 0,...  40.7 us
    all_to_all x2, blocking collectives, sent_to_all(): lax.all_to_all(jnp.broadcast_to(x[None], (count, *x.shape)), axis, 0, 0,...  39.9 us
    all_to_all x1, blocking collectives, spread(): lax.all_to_all(operator.reshape(count, rows // count, columns), CHIP, 0,...  28.1 us
    ppermute x4, starting transfers between devices, swapped(): return lax.ppermute(x, 'core', SWAP)  18.6 us
    all_gather x1, blocking collectives, per_device(): rest = lax.all_gather(kept[PANELS:].swapaxes(0, 1), 'x', axis=2, tiled=True)  13.5 us
    dot_general x19, matrix products, dot(): jnp.dot(a, b, precision=lax.Precision.HIGHEST, preferred_element_type=jnp...  13.2 us
    all_gather x1, blocking collectives, per_device(): first = lax.all_gather(first, 'x', axis=1, tiled=True)  12.5 us
    all_to_all x3, starting transfers between devices, sent_to_all(): lax.all_to_all(jnp.broadcast_to(x[None], (count, *x.shape)), axis, 0, 0,...  10.7 us
  transfers between devices with their start and end apart: 7, of which 3 were waited for; matrix products, arithmetic and copies ran while one was open for 6% of the time, Pallas kernels for 0%

profile of v7, /device:TPU:1, one launch (start us, length us, event | category | flops | bytes accessed | tf_op | source)
XLA Modules:
  0.0 191.4 jit_solution(14932535368176685976)
XLA Ops:
  1.0 8.7 %collective-permute-start.1 = (f32[64,256]{1,0:T(8,128)S(1)}, f32[64,256]{1,0:T(8,128)S(1)}, u32[]{:S(2)}, u32[]{:S(2)}) collective-permute-start(f32[64,256]{1,0:T(8,128)S(1)} %slice_select_fusion.8), channel_id=1, source_target_pairs={{0,8},{8,0},{1,9},{9,1},{2,10},{10,2},{3,11},{11,3},{4,12},{12,4},... | collective-permute-start | bytes 196616 | tf_op jit(solution)/shard_map/ppermute | solution.py:19
  9.7 1.9 %collective-permute-start.2 = (f32[512,512]{1,0:T(8,128)}, f32[512,512]{1,0:T(8,128)S(1)}, u32[]{:S(2)}, u32[]{:S(2)}) collective-permute-start(f32[512,512]{1,0:T(8,128)} %bitcast.135), channel_id=1, source_target_pairs={{0,8},{8,0},{1,9},{9,1},{2,10},{10,2},{3,11},{11,3},{4,12},{12,4},... | collective-permute-start | bytes 3145736 | tf_op jit(solution)/shard_map/ppermute | solution.py:19
  15.0 3.5 %all-to-all-start.4 = ((f32[8,64,256]{2,1,0:T(8,128)}), f32[8,64,256]{2,1,0:T(8,128)S(1)}, u32[]{:S(2)}, u32[]{:S(2)}) async-start(f32[8,64,256]{2,1,0:T(8,128)} %broadcast_in_dim.18), calls=%async_computation.4 | async-start | bytes 1048576 | tf_op jit(solution)/shard_map/all_to_all | solution.py:15
  19.9 16.5 %all-to-all-done.4 = f32[8,64,256]{2,1,0:T(8,128)S(1)} async-done(((f32[8,64,256]{2,1,0:T(8,128)}), f32[8,64,256]{2,1,0:T(8,128)S(1)}, u32[]{:S(2)}, u32[]{:S(2)}) %all-to-all-start.4) | async-done | bytes 524320 | tf_op jit(solution)/shard_map/all_to_all | solution.py:15
  36.4 31.4 %conditional.1 = (f32[3,16,256]{2,1,0:T(8,128)S(1)}) conditional(s32[]{:T(128)} %convert_element_type.47, (pred[]{:T(512)}, pred[]{:T(512)}, f32[64,256]{1,0:T(8,128)S(1)}, pred[]{:T(512)}, f32[512,512]{1,0:T(8,128)S(1)}, /*index=5*/f32[512,512]{1,0:T(8,128)S(1)}, f32[8,64,256]{2,1,0:T(8,128)S(1)}, u32[]{:T(128)}, u32[]{:T(128)}, ...), branch_computations={%region_0.1_spmd, %region_1.2_spmd} | conditional | flops 1611963904 | bytes 16114938 | solution.py:86
  37.4 2.2 %fusion = f32[512,256]{1,0:T(8,128)S(1)} fusion(f32[512,256]{1,0:T(8,128)S(1)} %bitcast.154, f32[512,256]{1,0:T(8,128)S(1)} %bitcast.152, f32[512,512]{1,0:T(8,128)S(1)} %get-tuple-element.60, f32[512,512]{1,0:T(8,128)} %copy-done.6, pred[]{:T(512)} %get-tuple-element.59, s32[]{:T(128)S(6)} %select_n.130, s32[512]{0:T(512)S(1)} %get-tuple-element.141, ...), kind=kOutput, calls=%fused_computation.3 | convolution fusion | flops 806092800 | bytes 3674629 | tf_op jit(solution)/shard_map/cond/branch_0_fun/dot_general | solution.py:23
  39.7 28.1 %all_to_all.41 = f32[32,16,256]{2,1,0:T(8,128)S(1)} all-to-all(f32[32,16,256]{2,1,0:T(8,128)S(1)} %bitcast.153), channel_id=1, replica_groups=mesh['x'=4,'z'=8,'core'=2,'row'=8] {'z','x'}, dimensions={0} | all-to-all | bytes 1048576 | tf_op jit(solution)/shard_map/cond/branch_0_fun/all_to_all | solution.py:35
  67.9 19.9 %all_to_all.42 = f32[8,64,256]{2,1,0:T(8,128)S(1)} all-to-all(f32[8,64,256]{2,1,0:T(8,128)S(1)} %broadcast_in_dim.21), channel_id=1, replica_groups=mesh['x'=4,'z'=8,'core'=2,'row'=8] {'row'}, dimensions={0} | all-to-all | bytes 1048576 | tf_op jit(solution)/shard_map/all_to_all | solution.py:15
  88.5 3.7 %all-to-all-start.5 = ((f32[8,3,16,256]{3,2,1,0:T(8,128)}), f32[8,3,16,256]{3,2,1,0:T(8,128)S(1)}, u32[]{:S(2)}, u32[]{:S(2)}) async-start(f32[8,3,16,256]{3,2,1,0:T(8,128)} %broadcast_in_dim.19), calls=%async_computation.5 | async-start | bytes 786432 | tf_op jit(solution)/shard_map/all_to_all | solution.py:15
  92.3 1.7 gather_fusion
  94.1 11.6 %all-to-all-done.5 = f32[8,3,16,256]{3,2,1,0:T(8,128)S(1)} async-done(((f32[8,3,16,256]{3,2,1,0:T(8,128)}), f32[8,3,16,256]{3,2,1,0:T(8,128)S(1)}, u32[]{:S(2)}, u32[]{:S(2)}) %all-to-all-start.5) | async-done | bytes 393248 | tf_op jit(solution)/shard_map/all_to_all | solution.py:15
  105.8 12.5 %all_gather.6 = f32[6,64,256]{2,1,0:T(8,128)S(1)} all-gather(f32[6,16,256]{2,1,0:T(8,128)S(1)} %fusion.49), channel_id=1, replica_groups=mesh['x'=4,'z'=8,'core'=2,'row'=8] {'x'}, dimensions={1}, use_global_device_ids=true | all-gather | bytes 491520 | tf_op jit(solution)/shard_map/all_gather | solution.py:117
  118.2 4.6 %collective-permute-start.3 = (f32[6,64,256]{2,1,0:T(8,128)S(1)}, f32[6,64,256]{2,1,0:T(8,128)S(1)}, u32[]{:S(2)}, u32[]{:S(2)}) collective-permute-start(f32[6,64,256]{2,1,0:T(8,128)S(1)} %all_gather.6), channel_id=1, source_target_pairs={{0,8},{8,0},{1,9},{9,1},{2,10},{10,2},{3,11},{11,3},{4,12},{12,4},... | collective-permute-start | bytes 1179656 | tf_op jit(solution)/shard_map/ppermute | solution.py:19
  122.9 13.5 %all_gather.7 = f32[3,5,64,256]{3,2,1,0:T(8,128)S(1)} all-gather(f32[3,5,16,256]{3,2,1,0:T(8,128)S(1)} %copy_bitcast_fusion), channel_id=1, replica_groups=mesh['x'=4,'z'=8,'core'=2,'row'=8] {'x'}, dimensions={2}, use_global_device_ids=true | all-gather | bytes 1228800 | tf_op jit(solution)/shard_map/all_gather | solution.py:123
  137.1 3.3 %collective-permute-start.4 = (f32[3,320,256]{2,1,0:T(8,128)S(1)}, f32[3,320,256]{2,1,0:T(8,128)}, u32[]{:S(2)}, u32[]{:S(2)}) collective-permute-start(f32[3,320,256]{2,1,0:T(8,128)S(1)} %bitcast.145), channel_id=1, source_target_pairs={{0,8},{8,0},{1,9},{9,1},{2,10},{10,2},{3,11},{11,3},{4,12},{12,4},... | collective-permute-start | bytes 2949128 | tf_op jit(solution)/shard_map/ppermute | solution.py:19
  142.5 3.5 %all-to-all-start.7 = ((f32[8,64,256]{2,1,0:T(8,128)}), f32[8,64,256]{2,1,0:T(8,128)S(1)}, u32[]{:S(2)}, u32[]{:S(2)}) async-start(f32[8,64,256]{2,1,0:T(8,128)} %broadcast_in_dim.22), calls=%async_computation.7 | async-start | bytes 1048576 | tf_op jit(solution)/shard_map/all_to_all | solution.py:15
  146.0 1.1 fusion.30
  147.4 1.1 fusion.36
  148.8 1.4 fusion.12
  150.2 1.2 fusion.10
  151.4 12.6 %all-to-all-done.7 = f32[8,64,256]{2,1,0:T(8,128)S(1)} async-done(((f32[8,64,256]{2,1,0:T(8,128)}), f32[8,64,256]{2,1,0:T(8,128)S(1)}, u32[]{:S(2)}, u32[]{:S(2)}) %all-to-all-start.7) | async-done | bytes 524320 | tf_op jit(solution)/shard_map/all_to_all | solution.py:15
  165.3 20.0 %all_to_all.43 = f32[8,64,256]{2,1,0:T(8,128)S(1)} all-to-all(f32[8,64,256]{2,1,0:T(8,128)S(1)} %broadcast_in_dim.23), channel_id=1, replica_groups=mesh['x'=4,'z'=8,'core'=2,'row'=8] {'row'}, dimensions={0} | all-to-all | bytes 1048576 | tf_op jit(solution)/shard_map/all_to_all | solution.py:15
  185.9 1.4 fusion.13
  187.3 1.4 fusion.16
  (70 shorter events, 13.6 us)
Async XLA Ops:
  0.0 19.3 %copy-start = (f32[512,256]{1,0:T(8,128)S(1)}, f32[512,256]{1,0:T(8,128)}, u32[]{:S(2)}) copy-start(f32[512,256]{1,0:T(8,128)} %param.7) | copy-start | bytes 1572868
  0.0 14.1 %copy-start.5 = (f32[1,64,512]{2,1,0:T(8,128)S(1)}, f32[1,64,512]{2,1,0:T(8,128)}, u32[]{:S(2)}) copy-start(f32[1,64,512]{2,1,0:T(8,128)} %param.9) | copy-start | bytes 393220
  1.0 10.7 %copy-start.9 = (s32[64]{0:T(128)S(1)}, s32[64]{0:T(128)}, u32[]{:S(2)}) copy-start(s32[64]{0:T(128)} %param.10) | copy-start | bytes 772
  1.0 13.2 %collective-permute-start.1 = (f32[64,256]{1,0:T(8,128)S(1)}, f32[64,256]{1,0:T(8,128)S(1)}, u32[]{:S(2)}, u32[]{:S(2)}) collective-permute-start(f32[64,256]{1,0:T(8,128)S(1)} %slice_select_fusion.8), channel_id=1, source_target_pairs={{0,8},{8,0},{1,9},{9,1},{2,10},{10,2},{3,11},{11,3},{4,12},{12,4},... | collective-permute-start | bytes 196616 | tf_op jit(solution)/shard_map/ppermute | solution.py:19
  9.7 26.7 %collective-permute-start.2 = (f32[512,512]{1,0:T(8,128)}, f32[512,512]{1,0:T(8,128)S(1)}, u32[]{:S(2)}, u32[]{:S(2)}) collective-permute-start(f32[512,512]{1,0:T(8,128)} %bitcast.135), channel_id=1, source_target_pairs={{0,8},{8,0},{1,9},{9,1},{2,10},{10,2},{3,11},{11,3},{4,12},{12,4},... | collective-permute-start | bytes 3145736 | tf_op jit(solution)/shard_map/ppermute | solution.py:19
  14.2 22.2 %copy-start.1 = (f32[1,512,512]{2,1,0:T(8,128)S(1)}, f32[1,512,512]{2,1,0:T(8,128)}, u32[]{:S(2)}) copy-start(f32[1,512,512]{2,1,0:T(8,128)} %param.8) | copy-start | bytes 3145732
  15.0 21.4 %all-to-all-start.4 = ((f32[8,64,256]{2,1,0:T(8,128)}), f32[8,64,256]{2,1,0:T(8,128)S(1)}, u32[]{:S(2)}, u32[]{:S(2)}) async-start(f32[8,64,256]{2,1,0:T(8,128)} %broadcast_in_dim.18), calls=%async_computation.4 | async-start | bytes 1048576 | tf_op jit(solution)/shard_map/all_to_all | solution.py:15
  18.6 0.7 copy-start.10
  36.4 1.0 copy-start.6
  88.5 17.2 %all-to-all-start.5 = ((f32[8,3,16,256]{3,2,1,0:T(8,128)}), f32[8,3,16,256]{3,2,1,0:T(8,128)S(1)}, u32[]{:S(2)}, u32[]{:S(2)}) async-start(f32[8,3,16,256]{3,2,1,0:T(8,128)} %broadcast_in_dim.19), calls=%async_computation.5 | async-start | bytes 786432 | tf_op jit(solution)/shard_map/all_to_all | solution.py:15
  94.0 56.2 %copy-start.2 = (f32[448,256]{1,0:T(8,128)}, f32[448,256]{1,0:T(8,128)S(1)}, u32[]{:S(2)}) copy-start(f32[448,256]{1,0:T(8,128)S(1)} %gather_fusion) | copy-start | bytes 1376260
  118.2 22.4 %collective-permute-start.3 = (f32[6,64,256]{2,1,0:T(8,128)S(1)}, f32[6,64,256]{2,1,0:T(8,128)S(1)}, u32[]{:S(2)}, u32[]{:S(2)}) collective-permute-start(f32[6,64,256]{2,1,0:T(8,128)S(1)} %all_gather.6), channel_id=1, source_target_pairs={{0,8},{8,0},{1,9},{9,1},{2,10},{10,2},{3,11},{11,3},{4,12},{12,4},... | collective-permute-start | bytes 1179656 | tf_op jit(solution)/shard_map/ppermute | solution.py:19
  137.1 11.7 %collective-permute-start.4 = (f32[3,320,256]{2,1,0:T(8,128)S(1)}, f32[3,320,256]{2,1,0:T(8,128)}, u32[]{:S(2)}, u32[]{:S(2)}) collective-permute-start(f32[3,320,256]{2,1,0:T(8,128)S(1)} %bitcast.145), channel_id=1, source_target_pairs={{0,8},{8,0},{1,9},{9,1},{2,10},{10,2},{3,11},{11,3},{4,12},{12,4},... | collective-permute-start | bytes 2949128 | tf_op jit(solution)/shard_map/ppermute | solution.py:19
  140.7 0.8 copy-start.7
  142.5 21.5 %all-to-all-start.7 = ((f32[8,64,256]{2,1,0:T(8,128)}), f32[8,64,256]{2,1,0:T(8,128)S(1)}, u32[]{:S(2)}, u32[]{:S(2)}) async-start(f32[8,64,256]{2,1,0:T(8,128)} %broadcast_in_dim.22), calls=%async_computation.7 | async-start | bytes 1048576 | tf_op jit(solution)/shard_map/all_to_all | solution.py:15
  148.7 1.5 copy-start.3
  164.0 1.0 copy-start.8
  164.1 1.0 slice-start
  189.2 1.0 copy-start.4

commit v8 on v7

--- a/solution.py
+++ b/solution.py
@@ -83,6 +83,7 @@
     part = jnp.where(own_core == core, kept, swapped(sent))
     lower = jnp.where(own_core == core, below, swapped(below))
     whole = sent_to_all(part, ROW).reshape(pivots, -1)
+    lower, whole = lax.optimization_barrier((lower, whole))
     kept = lax.cond(
         twice,
         own_slots,
@@ -120,25 +121,21 @@
     def own_group(g, k):
         return [f[pairs.index((g, k))] for f in first]
 
+    rows = [working[g * slab : (g + 1) * slab] for g in range(PANELS - 1)]
+    tail = working[(PANELS - 1) * slab :]
+    rows[0] = rows[0] + product(own_group(1, 0), pivot[0])
+    rows, first, pivot, kept = lax.optimization_barrier((rows, first, pivot, kept))
+
     rest = lax.all_gather(kept[PANELS:].swapaxes(0, 1), "x", axis=2, tiled=True)
     rest = rest.reshape(PANELS, -1, pivots // 2)
     rest = rest, swapped(rest)
-
-    rows = [working[g * slab : (g + 1) * slab] for g in range(PANELS - 1)]
-    tail = working[(PANELS - 1) * slab :]
+    pivot.append(to_all_rows(rows[0]))
+    rows[1] = rows[1] + product(own_group(2, 0), pivot[0])
+    rows[1] = rows[1] + product(own_group(2, 1), pivot[1])
+    rows, first, pivot = lax.optimization_barrier((rows, first, pivot))
+    pivot.append(to_all_rows(rows[1]))
     solved = []
-
-    rows[0] = rows[0] + product(own_group(1, 0), pivot[0])
-    rows, first, pivot = lax.optimization_barrier((rows, first, pivot))
-    pivot.append(to_all_rows(rows[0]))
-    solved.append(product(own_group(0, 0), pivot[0]))
-    rows[1] = rows[1] + product(own_group(2, 0), pivot[0])
-    tail = tail + product([r[0] for r in rest], pivot[0])
-    rows[1] = rows[1] + product(own_group(2, 1), pivot[1])
-    rows, tail, solved = lax.optimization_barrier((rows, tail, solved))
-    pivot.append(to_all_rows(rows[1]))
-    pivot, first, rest, tail = lax.optimization_barrier((pivot, first, rest, tail))
-    for k in range(1, PANELS):
+    for k in range(PANELS):
         solved.append(product(own_group(k, k), pivot[k]))
         tail = tail + product([r[k] for r in rest], pivot[k])
     return jnp.concatenate([*solved, tail])

time: 192 us -> 171 us (0.89)
  blocking collectives: 93.9 us -> 49.7 us
  starting transfers between devices: 29.3 us -> 46.8 us
  matrix products: 13.2 us -> 17.1 us
  waiting for transfers between devices: 40.7 us -> 38.7 us
    all_to_all x2 -> x0, blocking collectives: 39.9 us -> none  [sent_to_all(): lax.all_to_all(jnp.broadcast_to(x[None], (count, *x.shape)), axis, 0, 0,...]
    all_to_all x3 -> x5, starting transfers between devices: 10.7 us -> 24 us  [sent_to_all(): lax.all_to_all(jnp.broadcast_to(x[None], (count, *x.shape)), axis, 0, 0,...]
    ppermute x4, starting transfers between devices: 18.6 us -> 22.8 us  [swapped(): return lax.ppermute(x, 'core', SWAP)]
    dot_general x19, matrix products: 13.2 us -> 17.1 us  [dot(): jnp.dot(a, b, precision=lax.Precision.HIGHEST, preferred_element_type=jnp...]
    all_to_all x3 -> x5, waiting for transfers between devices: 40.7 us -> 37.7 us  [sent_to_all(): lax.all_to_all(jnp.broadcast_to(x[None], (count, *x.shape)), axis, 0, 0,...]
    all_gather x1, blocking collectives: 12.5 us -> 9.93 us  [per_device(): first = lax.all_gather(first, 'x', axis=1, tiled=True)]
  transfers between devices with their start and end apart: 7 -> 9, of which waited for: 3 -> 4; matrix products, arithmetic and copies ran while one was open for 6% -> 12% of each run, Pallas kernels for 0% -> 0%
where the time goes in v8:
time: 171 us; the launch traced here: 170 us
  blocking collectives  49.7 us (29%)
  starting transfers between devices  46.8 us (27%)
  waiting for transfers between devices  38.7 us (23%)
  matrix products  17.1 us (10%)
  local copies, waits for them, and re-layouts  11.2 us (7%)
  other arithmetic  3.45 us (2%)
  between operations  2.42 us (1%)
    all_to_all x5, waiting for transfers between devices, sent_to_all(): lax.all_to_all(jnp.broadcast_to(x[None], (count, *x.shape)), axis, 0, 0,...  37.7 us
    all_to_all x1, blocking collectives, spread(): lax.all_to_all(operator.reshape(count, rows // count, columns), CHIP, 0,...  27.3 us
    all_to_all x5, starting transfers between devices, sent_to_all(): lax.all_to_all(jnp.broadcast_to(x[None], (count, *x.shape)), axis, 0, 0,...  24 us
    ppermute x4, starting transfers between devices, swapped(): return lax.ppermute(x, 'core', SWAP)  22.8 us
    dot_general x19, matrix products, dot(): jnp.dot(a, b, precision=lax.Precision.HIGHEST, preferred_element_type=jnp...  17.1 us
    all_gather x1, blocking collectives, per_device(): rest = lax.all_gather(kept[PANELS:].swapaxes(0, 1), 'x', axis=2, tiled=True)  12.4 us
    all_gather x1, blocking collectives, per_device(): first = lax.all_gather(first, 'x', axis=1, tiled=True)  9.93 us
    broadcast_in_dim x5, local copies, waits for them, and re-layouts, sent_to_all(): jnp.broadcast_to(x[None], (count, *x.shape))  4.13 us
  transfers between devices with their start and end apart: 9, of which 4 were waited for; matrix products, arithmetic and copies ran while one was open for 12% of the time, Pallas kernels for 0%

profile of v8, /device:TPU:1, one launch (start us, length us, event | category | flops | bytes accessed | tf_op | source)
XLA Modules:
  0.0 169.5 jit_solution(15311449653487968370)
XLA Ops:
  0.0 8.9 %collective-permute-start.2 = (f32[512,512]{1,0:T(8,128)}, f32[512,512]{1,0:T(8,128)}, u32[]{:S(2)}, u32[]{:S(2)}) collective-permute-start(f32[512,512]{1,0:T(8,128)} %bitcast.139), channel_id=1, source_target_pairs={{0,8},{8,0},{1,9},{9,1},{2,10},{10,2},{3,11},{11,3},{4,12},{12,4},... | collective-permute-start | bytes 3145736 | tf_op jit(solution)/shard_map/ppermute | solution.py:19
  9.8 2.1 %collective-permute-start.1 = (f32[64,256]{1,0:T(8,128)S(1)}, f32[64,256]{1,0:T(8,128)S(1)}, u32[]{:S(2)}, u32[]{:S(2)}) collective-permute-start(f32[64,256]{1,0:T(8,128)S(1)} %slice_select_fusion.8), channel_id=1, source_target_pairs={{0,8},{8,0},{1,9},{9,1},{2,10},{10,2},{3,11},{11,3},{4,12},{12,4},... | collective-permute-start | bytes 196616 | tf_op jit(solution)/shard_map/ppermute | solution.py:19
  15.4 3.5 %all-to-all-start.4 = ((f32[8,64,256]{2,1,0:T(8,128)}), f32[8,64,256]{2,1,0:T(8,128)S(1)}, u32[]{:S(2)}, u32[]{:S(2)}) async-start(f32[8,64,256]{2,1,0:T(8,128)} %broadcast_in_dim.18), calls=%async_computation.4 | async-start | bytes 1048576 | tf_op jit(solution)/shard_map/all_to_all | solution.py:15
  18.9 1.4 broadcast_select_fusion
  20.4 16.4 %all-to-all-done.4 = f32[8,64,256]{2,1,0:T(8,128)S(1)} async-done(((f32[8,64,256]{2,1,0:T(8,128)}), f32[8,64,256]{2,1,0:T(8,128)S(1)}, u32[]{:S(2)}, u32[]{:S(2)}) %all-to-all-start.4) | async-done | bytes 524320 | tf_op jit(solution)/shard_map/all_to_all | solution.py:15
  36.8 28.4 %conditional.1 = (f32[3,16,256]{2,1,0:T(8,128)S(1)}) conditional(s32[]{:T(128)} %convert_element_type.47, (pred[]{:T(512)}, pred[]{:T(512)}, f32[64,256]{1,0:T(8,128)S(1)}, f32[512,512]{1,0:T(8,128)S(1)}, f32[512,256]{1,0:T(8,128)S(1)}, /*index=5*/u32[]{:T(128)}, u32[]{:T(128)}, u32[]{:T(128)}) %tuple.44, (s32[]{:T(128)}, pred[]{:T(512)}, pred[]{:T(512)}, ...), branch_computations={%region_0.1_spmd, %region_1.2_spmd} | conditional | flops 1611963904 | bytes 16114938 | solution.py:87
  37.8 27.3 %all_to_all.41 = f32[32,16,256]{2,1,0:T(8,128)S(1)} all-to-all(f32[32,16,256]{2,1,0:T(8,128)S(1)} %bitcast.148), channel_id=1, replica_groups=mesh['x'=4,'z'=8,'core'=2,'row'=8] {'z','x'}, dimensions={0} | all-to-all | bytes 1048576 | tf_op jit(solution)/shard_map/cond/branch_0_fun/all_to_all | solution.py:35
  66.0 3.6 %all-to-all-start.5 = ((f32[8,3,16,256]{3,2,1,0:T(8,128)}), f32[8,3,16,256]{3,2,1,0:T(8,128)S(1)}, u32[]{:S(2)}, u32[]{:S(2)}) async-start(f32[8,3,16,256]{3,2,1,0:T(8,128)} %broadcast_in_dim.19), calls=%async_computation.5 | async-start | bytes 786432 | tf_op jit(solution)/shard_map/all_to_all | solution.py:15
  71.1 1.7 %gather_fusion = f32[448,256]{1,0:T(8,128)S(1)} fusion(f32[512,256]{1,0:T(8,128)S(1)} %copy-done, s32[1024]{0:T(1024)S(1)} %pad_clamp_fusion.1), kind=kCustom, calls=%fused_computation | custom fusion | bytes 919296 | tf_op jit(solution)/shard_map/gather | solution.py:105
  72.8 9.3 %all-to-all-done.5 = f32[8,3,16,256]{3,2,1,0:T(8,128)S(1)} async-done(((f32[8,3,16,256]{3,2,1,0:T(8,128)}), f32[8,3,16,256]{3,2,1,0:T(8,128)S(1)}, u32[]{:S(2)}, u32[]{:S(2)}) %all-to-all-start.5) | async-done | bytes 393248 | tf_op jit(solution)/shard_map/all_to_all | solution.py:15
  82.9 3.5 %all-to-all-start.6 = ((f32[8,64,256]{2,1,0:T(8,128)}), f32[8,64,256]{2,1,0:T(8,128)S(1)}, u32[]{:S(2)}, u32[]{:S(2)}) async-start(f32[8,64,256]{2,1,0:T(8,128)} %broadcast_in_dim.21), calls=%async_computation.6 | async-start | bytes 1048576 | tf_op jit(solution)/shard_map/all_to_all | solution.py:15
  86.5 9.9 %all_gather.6 = f32[6,64,256]{2,1,0:T(8,128)S(1)} all-gather(f32[6,16,256]{2,1,0:T(8,128)S(1)} %fusion.38), channel_id=1, replica_groups=mesh['x'=4,'z'=8,'core'=2,'row'=8] {'x'}, dimensions={1}, use_global_device_ids=true | all-gather | bytes 491520 | tf_op jit(solution)/shard_map/all_gather | solution.py:118
  96.4 7.7 %collective-permute-start.3 = (f32[6,64,256]{2,1,0:T(8,128)S(1)}, f32[6,64,256]{2,1,0:T(8,128)S(1)}, u32[]{:S(2)}, u32[]{:S(2)}) collective-permute-start(f32[6,64,256]{2,1,0:T(8,128)S(1)} %all_gather.6), channel_id=1, source_target_pairs={{0,8},{8,0},{1,9},{9,1},{2,10},{10,2},{3,11},{11,3},{4,12},{12,4},... | collective-permute-start | bytes 1179656 | tf_op jit(solution)/shard_map/ppermute | solution.py:19
  106.5 6.8 %all-to-all-start.7 = ((f32[8,64,256]{2,1,0:T(8,128)}), f32[8,64,256]{2,1,0:T(8,128)S(1)}, u32[]{:S(2)}, u32[]{:S(2)}) async-start(f32[8,64,256]{2,1,0:T(8,128)} %broadcast_in_dim.22), calls=%async_computation.7 | async-start | bytes 1048576 | tf_op jit(solution)/shard_map/all_to_all | solution.py:15
  113.4 12.4 %all_gather.7 = f32[3,5,64,256]{3,2,1,0:T(8,128)S(1)} all-gather(f32[3,5,16,256]{3,2,1,0:T(8,128)S(1)} %slice_bitcast_fusion.6), channel_id=1, replica_groups=mesh['x'=4,'z'=8,'core'=2,'row'=8] {'x'}, dimensions={2}, use_global_device_ids=true | all-gather | bytes 1228800 | tf_op jit(solution)/shard_map/all_gather | solution.py:129
  125.8 4.2 %collective-permute-start.4 = (f32[3,320,256]{2,1,0:T(8,128)S(1)}, f32[3,320,256]{2,1,0:T(8,128)}, u32[]{:S(2)}, u32[]{:S(2)}) collective-permute-start(f32[3,320,256]{2,1,0:T(8,128)S(1)} %bitcast.142), channel_id=1, source_target_pairs={{0,8},{8,0},{1,9},{9,1},{2,10},{10,2},{3,11},{11,3},{4,12},{12,4},... | collective-permute-start | bytes 2949128 | tf_op jit(solution)/shard_map/ppermute | solution.py:19
  138.6 6.5 %all-to-all-start.8 = ((f32[8,64,256]{2,1,0:T(8,128)}), f32[8,64,256]{2,1,0:T(8,128)S(1)}, u32[]{:S(2)}, u32[]{:S(2)}) async-start(f32[8,64,256]{2,1,0:T(8,128)} %broadcast_in_dim.23), calls=%async_computation.8 | async-start | bytes 1048576 | tf_op jit(solution)/shard_map/all_to_all | solution.py:15
  145.1 1.2 convolution_add_fusion.5
  146.3 1.8 %convolution_add_fusion.4 = f32[64,256]{1,0:T(8,128)} fusion(f32[64,256]{1,0:T(8,128)S(1)} %copy-done.14, f32[256,256]{1,0:T(8,128)S(1)} %bitcast.134, f32[6,64,256]{2,1,0:T(8,128)} %copy-done.11), kind=kOutput, calls=%fused_computation.39 | convolution fusion | flops 50348032 | bytes 458752 | tf_op jit(solution)/shard_map/dot_general | solution.py:23
  148.1 1.2 fusion.46
  149.7 1.4 convolution_add_fusion.1
  151.1 12.0 %all-to-all-done.8 = f32[8,64,256]{2,1,0:T(8,128)S(1)} async-done(((f32[8,64,256]{2,1,0:T(8,128)}), f32[8,64,256]{2,1,0:T(8,128)S(1)}, u32[]{:S(2)}, u32[]{:S(2)}) %all-to-all-start.8) | async-done | bytes 524320 | tf_op jit(solution)/shard_map/all_to_all | solution.py:15
  165.7 1.5 convolution_add_fusion
  167.2 1.4 fusion.10
  (85 shorter events, 21.3 us)
Async XLA Ops:
  0.0 70.3 %copy-start = (f32[512,256]{1,0:T(8,128)S(1)}, f32[512,256]{1,0:T(8,128)}, u32[]{:S(2)}) copy-start(f32[512,256]{1,0:T(8,128)} %param.7) | copy-start | bytes 1572868
  0.0 18.9 %collective-permute-start.2 = (f32[512,512]{1,0:T(8,128)}, f32[512,512]{1,0:T(8,128)}, u32[]{:S(2)}, u32[]{:S(2)}) collective-permute-start(f32[512,512]{1,0:T(8,128)} %bitcast.139), channel_id=1, source_target_pairs={{0,8},{8,0},{1,9},{9,1},{2,10},{10,2},{3,11},{11,3},{4,12},{12,4},... | collective-permute-start | bytes 3145736 | tf_op jit(solution)/shard_map/ppermute | solution.py:19
  8.9 3.0 %copy-start.15 = (s32[64]{0:T(128)S(1)}, s32[64]{0:T(128)}, u32[]{:S(2)}) copy-start(s32[64]{0:T(128)} %param.10) | copy-start | bytes 772
  8.9 5.6 %copy-start.10 = (f32[1,64,512]{2,1,0:T(8,128)S(1)}, f32[1,64,512]{2,1,0:T(8,128)}, u32[]{:S(2)}) copy-start(f32[1,64,512]{2,1,0:T(8,128)} %param.9) | copy-start | bytes 393220
  9.8 9.1 %copy-start.1 = (f32[1,512,512]{2,1,0:T(8,128)S(1)}, f32[1,512,512]{2,1,0:T(8,128)}, u32[]{:S(2)}) copy-start(f32[1,512,512]{2,1,0:T(8,128)} %param.8) | copy-start | bytes 3145732
  9.8 4.7 %collective-permute-start.1 = (f32[64,256]{1,0:T(8,128)S(1)}, f32[64,256]{1,0:T(8,128)S(1)}, u32[]{:S(2)}, u32[]{:S(2)}) collective-permute-start(f32[64,256]{1,0:T(8,128)S(1)} %slice_select_fusion.8), channel_id=1, source_target_pairs={{0,8},{8,0},{1,9},{9,1},{2,10},{10,2},{3,11},{11,3},{4,12},{12,4},... | collective-permute-start | bytes 196616 | tf_op jit(solution)/shard_map/ppermute | solution.py:19
  15.4 21.4 %all-to-all-start.4 = ((f32[8,64,256]{2,1,0:T(8,128)}), f32[8,64,256]{2,1,0:T(8,128)S(1)}, u32[]{:S(2)}, u32[]{:S(2)}) async-start(f32[8,64,256]{2,1,0:T(8,128)} %broadcast_in_dim.18), calls=%async_computation.4 | async-start | bytes 1048576 | tf_op jit(solution)/shard_map/all_to_all | solution.py:15
  66.0 16.1 %all-to-all-start.5 = ((f32[8,3,16,256]{3,2,1,0:T(8,128)}), f32[8,3,16,256]{3,2,1,0:T(8,128)S(1)}, u32[]{:S(2)}, u32[]{:S(2)}) async-start(f32[8,3,16,256]{3,2,1,0:T(8,128)} %broadcast_in_dim.19), calls=%async_computation.5 | async-start | bytes 786432 | tf_op jit(solution)/shard_map/all_to_all | solution.py:15
  72.8 32.7 %copy-start.2 = (f32[448,256]{1,0:T(8,128)}, f32[448,256]{1,0:T(8,128)S(1)}, u32[]{:S(2)}) copy-start(f32[448,256]{1,0:T(8,128)S(1)} %gather_fusion) | copy-start | bytes 1376260
  82.9 21.2 %all-to-all-start.6 = ((f32[8,64,256]{2,1,0:T(8,128)}), f32[8,64,256]{2,1,0:T(8,128)S(1)}, u32[]{:S(2)}, u32[]{:S(2)}) async-start(f32[8,64,256]{2,1,0:T(8,128)} %broadcast_in_dim.21), calls=%async_computation.6 | async-start | bytes 1048576 | tf_op jit(solution)/shard_map/all_to_all | solution.py:15
  96.4 34.7 %copy-start.4 = (f32[6,64,256]{2,1,0:T(8,128)}, f32[6,64,256]{2,1,0:T(8,128)S(1)}, u32[]{:S(2)}) copy-start(f32[6,64,256]{2,1,0:T(8,128)S(1)} %all_gather.6) | copy-start | bytes 1179652
  96.4 9.0 %collective-permute-start.3 = (f32[6,64,256]{2,1,0:T(8,128)S(1)}, f32[6,64,256]{2,1,0:T(8,128)S(1)}, u32[]{:S(2)}, u32[]{:S(2)}) collective-permute-start(f32[6,64,256]{2,1,0:T(8,128)S(1)} %all_gather.6), channel_id=1, source_target_pairs={{0,8},{8,0},{1,9},{9,1},{2,10},{10,2},{3,11},{11,3},{4,12},{12,4},... | collective-permute-start | bytes 1179656 | tf_op jit(solution)/shard_map/ppermute | solution.py:19
  105.4 1.1 copy-start.11
  106.5 26.5 %all-to-all-start.7 = ((f32[8,64,256]{2,1,0:T(8,128)}), f32[8,64,256]{2,1,0:T(8,128)S(1)}, u32[]{:S(2)}, u32[]{:S(2)}) async-start(f32[8,64,256]{2,1,0:T(8,128)} %broadcast_in_dim.22), calls=%async_computation.7 | async-start | bytes 1048576 | tf_op jit(solution)/shard_map/all_to_all | solution.py:15
  125.8 23.9 %collective-permute-start.4 = (f32[3,320,256]{2,1,0:T(8,128)S(1)}, f32[3,320,256]{2,1,0:T(8,128)}, u32[]{:S(2)}, u32[]{:S(2)}) collective-permute-start(f32[3,320,256]{2,1,0:T(8,128)S(1)} %bitcast.142), channel_id=1, source_target_pairs={{0,8},{8,0},{1,9},{9,1},{2,10},{10,2},{3,11},{11,3},{4,12},{12,4},... | collective-permute-start | bytes 2949128 | tf_op jit(solution)/shard_map/ppermute | solution.py:19
  133.0 1.0 copy-start.5
  138.6 24.6 %all-to-all-start.8 = ((f32[8,64,256]{2,1,0:T(8,128)}), f32[8,64,256]{2,1,0:T(8,128)S(1)}, u32[]{:S(2)}, u32[]{:S(2)}) async-start(f32[8,64,256]{2,1,0:T(8,128)} %broadcast_in_dim.23), calls=%async_computation.8 | async-start | bytes 1048576 | tf_op jit(solution)/shard_map/all_to_all | solution.py:15
  145.1 1.2 copy-start.14
  146.3 1.8 %copy-start.9 = (f32[1,5,64,256]{3,2,1,0:T(8,128)S(1)}, f32[1,5,64,256]{3,2,1,0:T(8,128)}, u32[]{:S(2)}) copy-start(f32[1,5,64,256]{3,2,1,0:T(8,128)} %get-tuple-element.137) | copy-start | bytes 983044
  148.1 1.2 copy-start.8
  163.2 1.0 copy-start.7
  165.7 1.5 copy-start.3
  165.7 1.5 copy-start.6
  167.2 1.5 copy-start.12
  (3 other events, 2.4 us)

commit v9 on v7

--- a/solution.py
+++ b/solution.py
@@ -28,14 +28,12 @@
     return jnp.where(on_first, low, high), jnp.where(on_first, high, low)
 
 
-def spread(operator, sources):
-    rows, columns = operator.shape
+def spread(operators, sources):
     count = lax.axis_size(CHIP)
-    operator, sources = lax.optimization_barrier((operator, sources))
-    pieces = lax.all_to_all(
-        operator.reshape(count, rows // count, columns), CHIP, 0, 0, tiled=True
-    )
-    return jnp.stack([lax.dynamic_index_in_dim(pieces, s, 0, keepdims=False) for s in sources])
+    sent = [o.reshape(count, 1, -1, o.shape[1]) for o in operators]
+    sent, sources = lax.optimization_barrier((sent, sources))
+    pieces = lax.all_to_all(jnp.concatenate(sent, axis=1), CHIP, 0, 0, tiled=True)
+    return [lax.dynamic_index_in_dim(pieces, s, 0, keepdims=False) for s in sources]
 
 
 def operator_of(below, inverse, own_rows, panel):
@@ -45,16 +43,19 @@
     return jnp.where(group == panel, jnp.tile(own_rows, (below.shape[0] // slab, 1)), product)
 
 
-def shared_slots(lower, whole, part, below, inverse, on_first, panel, panel_core, sources, cores):
-    return spread(operator_of(lower, whole, part, panel), sources)
+def one_slot(main, whole, spare, mine, panels, sources, is_main):
+    lower, part = main
+    return jnp.stack([p[0] for p in spread([operator_of(lower, whole, part, panels[0])], sources)])
 
 
-def own_slots(lower, whole, part, below, inverse, on_first, panel, panel_core, sources, cores):
-    whole = sent_to_all(inverse, ROW).reshape(-1, inverse.shape[1])
-    mine, other = halves(operator_of(below, whole, inverse, panel_core), on_first, 1)
-    mine, other = spread(mine, sources), spread(swapped(other), sources)
-    here = [(c == 0) == on_first for c in cores]
-    return jnp.stack([jnp.where(h, mine[k], other[k]) for k, h in enumerate(here)])
+def two_slots(main, whole, spare, mine, panels, sources, is_main):
+    lower, part = main
+    operators = [operator_of(lower, whole, part, panels[0])]
+    lower, part = (jnp.where(mine, got, kept) for kept, got in spare)
+    whole = sent_to_all(part, ROW).reshape(whole.shape)
+    operators.append(operator_of(lower, whole, part, panels[1]))
+    pieces = spread(operators, sources)
+    return jnp.stack([jnp.where(m, p[0], p[1]) for m, p in zip(is_main, pieces)])
 
 
 def per_device(rhs_block, below, inverse, owner_map, row_perm):
@@ -70,33 +71,39 @@
     owners = [owner_map[k].astype(jnp.uint32) for k in range(PANELS)]
     chips = [o >> 1 for o in owners]
     cores = [(o & 1).astype(jnp.int32) for o in owners]
-    twice = (chips[0] == chips[1]) | (chips[0] == chips[2]) | (chips[1] == chips[2])
     held = [h == chip for h in chips]
     own_core = jnp.where(held[0], cores[0], jnp.where(held[1], cores[1], cores[2]))
-    panel = jnp.where(held[0], 0, jnp.where(held[1], 1, 2))
-    panel_core = jnp.where(
-        held[0] & (cores[0] == core), 0, jnp.where(held[1] & (cores[1] == core), 1, 2)
-    )
+    panels = [
+        jnp.where(held[0], 0, jnp.where(held[1], 1, 2)),
+        jnp.where(held[2], 2, jnp.where(held[1], 1, 0)),
+    ]
+    is_main = [
+        chips[0] == chips[0],
+        chips[1] != chips[0],
+        (chips[2] != chips[0]) & (chips[2] != chips[1]),
+    ]
     sources = [(h % nz) * nx + h // nz for h in chips]
 
+    mine = own_core == core
     kept, sent = halves(inverse, on_first, 1)
-    part = jnp.where(own_core == core, kept, swapped(sent))
-    lower = jnp.where(own_core == core, below, swapped(below))
+    got = swapped(sent)
+    part = jnp.where(mine, kept, got)
+    got_below = swapped(below)
+    lower = jnp.where(mine, below, got_below)
     whole = sent_to_all(part, ROW).reshape(pivots, -1)
+    lower, whole = lax.optimization_barrier((lower, whole))
+    spare = (below, got_below), (kept, got)
     kept = lax.cond(
-        twice,
-        own_slots,
-        shared_slots,
-        lower,
+        ~(is_main[1] & is_main[2]),
+        two_slots,
+        one_slot,
+        (lower, part),
         whole,
-        part,
-        below,
-        inverse,
-        on_first,
-        panel,
-        panel_core,
+        spare,
+        mine,
+        panels,
         sources,
-        cores,
+        is_main,
     )
 
     def permuted(start, end):

time: 192 us -> 188 us (0.979)
  blocking collectives: 93.9 us -> 87.6 us
  starting transfers between devices: 29.3 us -> 35.5 us
  waiting for transfers between devices: 40.7 us -> 37.1 us
    ppermute x4, starting transfers between devices: 18.6 us -> 23.8 us  [swapped(): return lax.ppermute(x, 'core', SWAP)]
    all_to_all x3, waiting for transfers between devices: 40.7 us -> 37.1 us  [sent_to_all(): lax.all_to_all(jnp.broadcast_to(x[None], (count, *x.shape)), axis, 0, 0,...]
    all_to_all x2, blocking collectives: 39.9 us -> 37.1 us  [sent_to_all(): lax.all_to_all(jnp.broadcast_to(x[None], (count, *x.shape)), axis, 0, 0,...]
    all_gather x1, blocking collectives: 12.5 us -> 10.3 us  [per_device(): first = lax.all_gather(first, 'x', axis=1, tiled=True)]
  transfers between devices with their start and end apart: 7 -> 7, of which waited for: 3 -> 3; matrix products, arithmetic and copies ran while one was open for 6% -> 7% of each run, Pallas kernels for 0% -> 0%
where the time goes in v9:
time: 188 us; the launch traced here: 187 us
  blocking collectives  87.6 us (47%)
  waiting for transfers between devices  37.1 us (20%)
  starting transfers between devices  35.5 us (19%)
  matrix products  11.9 us (6%)
  local copies, waits for them, and re-layouts  9.06 us (5%)
  other arithmetic  3.44 us (2%)
  between operations  2.44 us (1%)
    all_to_all x3, waiting for transfers between devices, sent_to_all(): lax.all_to_all(jnp.broadcast_to(x[None], (count, *x.shape)), axis, 0, 0,...  37.1 us
    all_to_all x2, blocking collectives, sent_to_all(): lax.all_to_all(jnp.broadcast_to(x[None], (count, *x.shape)), axis, 0, 0,...  37.1 us
    all_to_all x1, blocking collectives, spread(): lax.all_to_all(jnp.concatenate(sent, axis=1), CHIP, 0, 0, tiled=True)  27.3 us
    ppermute x4, starting transfers between devices, swapped(): return lax.ppermute(x, 'core', SWAP)  23.8 us
    all_gather x1, blocking collectives, per_device(): rest = lax.all_gather(kept[PANELS:].swapaxes(0, 1), 'x', axis=2, tiled=True)  12.9 us
    dot_general x19, matrix products, dot(): jnp.dot(a, b, precision=lax.Precision.HIGHEST, preferred_element_type=jnp...  11.9 us
    all_to_all x3, starting transfers between devices, sent_to_all(): lax.all_to_all(jnp.broadcast_to(x[None], (count, *x.shape)), axis, 0, 0,...  11.7 us
    all_gather x1, blocking collectives, per_device(): first = lax.all_gather(first, 'x', axis=1, tiled=True)  10.3 us
  transfers between devices with their start and end apart: 7, of which 3 were waited for; matrix products, arithmetic and copies ran while one was open for 7% of the time, Pallas kernels for 0%

profile of v9, /device:TPU:1, one launch (start us, length us, event | category | flops | bytes accessed | tf_op | source)
XLA Modules:
  0.0 187.1 jit_solution(10402984746961479109)
XLA Ops:
  0.0 8.9 %collective-permute-start.1 = (f32[512,512]{1,0:T(8,128)}, f32[512,512]{1,0:T(8,128)}, u32[]{:S(2)}, u32[]{:S(2)}) collective-permute-start(f32[512,512]{1,0:T(8,128)} %bitcast.155), channel_id=1, source_target_pairs={{0,8},{8,0},{1,9},{9,1},{2,10},{10,2},{3,11},{11,3},{4,12},{12,4},... | collective-permute-start | bytes 3145736 | tf_op jit(solution)/shard_map/ppermute | solution.py:19
  9.8 1.9 %collective-permute-start = (f32[64,256]{1,0:T(8,128)S(1)}, f32[64,256]{1,0:T(8,128)S(1)}, u32[]{:S(2)}, u32[]{:S(2)}) collective-permute-start(f32[64,256]{1,0:T(8,128)S(1)} %slice_select_fusion.6), channel_id=1, source_target_pairs={{0,8},{8,0},{1,9},{9,1},{2,10},{10,2},{3,11},{11,3},{4,12},{12,4},... | collective-permute-start | bytes 196616 | tf_op jit(solution)/shard_map/ppermute | solution.py:19
  15.3 3.5 %all-to-all-start.3 = ((f32[8,64,256]{2,1,0:T(8,128)}), f32[8,64,256]{2,1,0:T(8,128)S(1)}, u32[]{:S(2)}, u32[]{:S(2)}) async-start(f32[8,64,256]{2,1,0:T(8,128)} %broadcast_in_dim.19), calls=%async_computation.3 | async-start | bytes 1048576 | tf_op jit(solution)/shard_map/all_to_all | solution.py:15
  20.2 1.4 broadcast_select_fusion.1
  21.6 15.0 %all-to-all-done.3 = f32[8,64,256]{2,1,0:T(8,128)S(1)} async-done(((f32[8,64,256]{2,1,0:T(8,128)}), f32[8,64,256]{2,1,0:T(8,128)S(1)}, u32[]{:S(2)}, u32[]{:S(2)}) %all-to-all-start.3) | async-done | bytes 524320 | tf_op jit(solution)/shard_map/all_to_all | solution.py:15
  36.6 28.4 %conditional.1 = (f32[3,16,256]{2,1,0:T(8,128)S(1)}) conditional(s32[]{:T(128)} %convert_element_type.47, (s32[]{:T(128)}, f32[64,256]{1,0:T(8,128)S(1)}, f32[512,512]{1,0:T(8,128)S(1)}, f32[512,256]{1,0:T(8,128)S(1)}, u32[]{:T(128)}, /*index=5*/u32[]{:T(128)}, u32[]{:T(128)}) %tuple.37, (s32[]{:T(128)}, f32[64,256]{1,0:T(8,128)S(1)}, ...), branch_computations={%region_0.1_spmd, %region_1.2_spmd} | conditional | flops 1612238336 | bytes 16823980 | solution.py:96
  37.7 27.3 %all_to_all.37 = f32[32,1,16,256]{3,2,1,0:T(8,128)S(1)} all-to-all(f32[32,1,16,256]{3,2,1,0:T(8,128)S(1)} %bitcast.170), channel_id=1, replica_groups=mesh['x'=4,'z'=8,'core'=2,'row'=8] {'z','x'}, dimensions={0} | all-to-all | bytes 1048576 | tf_op jit(solution)/shard_map/cond/branch_0_fun/all_to_all | solution.py:35
  65.1 17.1 %all_to_all.38 = f32[8,64,256]{2,1,0:T(8,128)S(1)} all-to-all(f32[8,64,256]{2,1,0:T(8,128)S(1)} %broadcast_in_dim.22), channel_id=1, replica_groups=mesh['x'=4,'z'=8,'core'=2,'row'=8] {'row'}, dimensions={0} | all-to-all | bytes 1048576 | tf_op jit(solution)/shard_map/all_to_all | solution.py:15
  83.0 4.8 %all-to-all-start.4 = ((f32[8,3,16,256]{3,2,1,0:T(8,128)}), f32[8,3,16,256]{3,2,1,0:T(8,128)S(1)}, u32[]{:S(2)}, u32[]{:S(2)}) async-start(f32[8,3,16,256]{3,2,1,0:T(8,128)} %broadcast_in_dim.20), calls=%async_computation.4 | async-start | bytes 786432 | tf_op jit(solution)/shard_map/all_to_all | solution.py:15
  87.8 1.7 gather_fusion
  89.6 9.5 %all-to-all-done.4 = f32[8,3,16,256]{3,2,1,0:T(8,128)S(1)} async-done(((f32[8,3,16,256]{3,2,1,0:T(8,128)}), f32[8,3,16,256]{3,2,1,0:T(8,128)S(1)}, u32[]{:S(2)}, u32[]{:S(2)}) %all-to-all-start.4) | async-done | bytes 393248 | tf_op jit(solution)/shard_map/all_to_all | solution.py:15
  99.1 10.3 %all_gather.6 = f32[6,64,256]{2,1,0:T(8,128)S(1)} all-gather(f32[6,16,256]{2,1,0:T(8,128)S(1)} %fusion.52), channel_id=1, replica_groups=mesh['x'=4,'z'=8,'core'=2,'row'=8] {'x'}, dimensions={1}, use_global_device_ids=true | all-gather | bytes 491520 | tf_op jit(solution)/shard_map/all_gather | solution.py:124
  109.4 8.9 %collective-permute-start.2 = (f32[6,64,256]{2,1,0:T(8,128)S(1)}, f32[6,64,256]{2,1,0:T(8,128)S(1)}, u32[]{:S(2)}, u32[]{:S(2)}) collective-permute-start(f32[6,64,256]{2,1,0:T(8,128)S(1)} %all_gather.6), channel_id=1, source_target_pairs={{0,8},{8,0},{1,9},{9,1},{2,10},{10,2},{3,11},{11,3},{4,12},{12,4},... | collective-permute-start | bytes 1179656 | tf_op jit(solution)/shard_map/ppermute | solution.py:19
  118.3 12.9 %all_gather.7 = f32[3,5,64,256]{3,2,1,0:T(8,128)S(1)} all-gather(f32[3,5,16,256]{3,2,1,0:T(8,128)S(1)} %copy_bitcast_fusion), channel_id=1, replica_groups=mesh['x'=4,'z'=8,'core'=2,'row'=8] {'x'}, dimensions={2}, use_global_device_ids=true | all-gather | bytes 1228800 | tf_op jit(solution)/shard_map/all_gather | solution.py:130
  131.9 4.1 %collective-permute-start.3 = (f32[3,320,256]{2,1,0:T(8,128)S(1)}, f32[3,320,256]{2,1,0:T(8,128)}, u32[]{:S(2)}, u32[]{:S(2)}) collective-permute-start(f32[3,320,256]{2,1,0:T(8,128)S(1)} %bitcast.163), channel_id=1, source_target_pairs={{0,8},{8,0},{1,9},{9,1},{2,10},{10,2},{3,11},{11,3},{4,12},{12,4},... | collective-permute-start | bytes 2949128 | tf_op jit(solution)/shard_map/ppermute | solution.py:19
  138.2 3.5 %all-to-all-start.6 = ((f32[8,64,256]{2,1,0:T(8,128)}), f32[8,64,256]{2,1,0:T(8,128)S(1)}, u32[]{:S(2)}, u32[]{:S(2)}) async-start(f32[8,64,256]{2,1,0:T(8,128)} %broadcast_in_dim.23), calls=%async_computation.6 | async-start | bytes 1048576 | tf_op jit(solution)/shard_map/all_to_all | solution.py:15
  141.7 1.1 fusion.33
  143.1 1.1 fusion.39
  144.4 1.4 fusion.15
  145.9 1.2 fusion.13
  147.1 12.6 %all-to-all-done.6 = f32[8,64,256]{2,1,0:T(8,128)S(1)} async-done(((f32[8,64,256]{2,1,0:T(8,128)}), f32[8,64,256]{2,1,0:T(8,128)S(1)}, u32[]{:S(2)}, u32[]{:S(2)}) %all-to-all-start.6) | async-done | bytes 524320 | tf_op jit(solution)/shard_map/all_to_all | solution.py:15
  161.0 20.0 %all_to_all.39 = f32[8,64,256]{2,1,0:T(8,128)S(1)} all-to-all(f32[8,64,256]{2,1,0:T(8,128)S(1)} %broadcast_in_dim.24), channel_id=1, replica_groups=mesh['x'=4,'z'=8,'core'=2,'row'=8] {'row'}, dimensions={0} | all-to-all | bytes 1048576 | tf_op jit(solution)/shard_map/all_to_all | solution.py:15
  181.5 1.4 fusion.16
  182.9 1.4 fusion.19
  (69 shorter events, 13.7 us)
Async XLA Ops:
  0.0 19.5 %copy-start = (f32[512,256]{1,0:T(8,128)S(1)}, f32[512,256]{1,0:T(8,128)}, u32[]{:S(2)}) copy-start(f32[512,256]{1,0:T(8,128)} %param.7) | copy-start | bytes 1572868
  0.0 20.2 %collective-permute-start.1 = (f32[512,512]{1,0:T(8,128)}, f32[512,512]{1,0:T(8,128)}, u32[]{:S(2)}, u32[]{:S(2)}) collective-permute-start(f32[512,512]{1,0:T(8,128)} %bitcast.155), channel_id=1, source_target_pairs={{0,8},{8,0},{1,9},{9,1},{2,10},{10,2},{3,11},{11,3},{4,12},{12,4},... | collective-permute-start | bytes 3145736 | tf_op jit(solution)/shard_map/ppermute | solution.py:19
  8.9 2.9 %copy-start.9 = (s32[64]{0:T(128)S(1)}, s32[64]{0:T(128)}, u32[]{:S(2)}) copy-start(s32[64]{0:T(128)} %param.10) | copy-start | bytes 772
  8.9 5.5 %copy-start.6 = (f32[1,64,512]{2,1,0:T(8,128)S(1)}, f32[1,64,512]{2,1,0:T(8,128)}, u32[]{:S(2)}) copy-start(f32[1,64,512]{2,1,0:T(8,128)} %param.9) | copy-start | bytes 393220
  9.8 4.5 %collective-permute-start = (f32[64,256]{1,0:T(8,128)S(1)}, f32[64,256]{1,0:T(8,128)S(1)}, u32[]{:S(2)}, u32[]{:S(2)}) collective-permute-start(f32[64,256]{1,0:T(8,128)S(1)} %slice_select_fusion.6), channel_id=1, source_target_pairs={{0,8},{8,0},{1,9},{9,1},{2,10},{10,2},{3,11},{11,3},{4,12},{12,4},... | collective-permute-start | bytes 196616 | tf_op jit(solution)/shard_map/ppermute | solution.py:19
  14.4 5.8 %copy-start.1 = (f32[1,512,512]{2,1,0:T(8,128)S(1)}, f32[1,512,512]{2,1,0:T(8,128)}, u32[]{:S(2)}) copy-start(f32[1,512,512]{2,1,0:T(8,128)} %param.8) | copy-start | bytes 3145732
  15.3 21.4 %all-to-all-start.3 = ((f32[8,64,256]{2,1,0:T(8,128)}), f32[8,64,256]{2,1,0:T(8,128)S(1)}, u32[]{:S(2)}, u32[]{:S(2)}) async-start(f32[8,64,256]{2,1,0:T(8,128)} %broadcast_in_dim.19), calls=%async_computation.3 | async-start | bytes 1048576 | tf_op jit(solution)/shard_map/all_to_all | solution.py:15
  18.8 0.7 copy-start.10
  83.0 16.1 %all-to-all-start.4 = ((f32[8,3,16,256]{3,2,1,0:T(8,128)}), f32[8,3,16,256]{3,2,1,0:T(8,128)S(1)}, u32[]{:S(2)}, u32[]{:S(2)}) async-start(f32[8,3,16,256]{3,2,1,0:T(8,128)} %broadcast_in_dim.20), calls=%async_computation.4 | async-start | bytes 786432 | tf_op jit(solution)/shard_map/all_to_all | solution.py:15
  89.5 56.4 %copy-start.3 = (f32[448,256]{1,0:T(8,128)}, f32[448,256]{1,0:T(8,128)S(1)}, u32[]{:S(2)}) copy-start(f32[448,256]{1,0:T(8,128)S(1)} %gather_fusion) | copy-start | bytes 1376260
  109.4 26.9 %collective-permute-start.2 = (f32[6,64,256]{2,1,0:T(8,128)S(1)}, f32[6,64,256]{2,1,0:T(8,128)S(1)}, u32[]{:S(2)}, u32[]{:S(2)}) collective-permute-start(f32[6,64,256]{2,1,0:T(8,128)S(1)} %all_gather.6), channel_id=1, source_target_pairs={{0,8},{8,0},{1,9},{9,1},{2,10},{10,2},{3,11},{11,3},{4,12},{12,4},... | collective-permute-start | bytes 1179656 | tf_op jit(solution)/shard_map/ppermute | solution.py:19
  131.9 12.5 %collective-permute-start.3 = (f32[3,320,256]{2,1,0:T(8,128)S(1)}, f32[3,320,256]{2,1,0:T(8,128)}, u32[]{:S(2)}, u32[]{:S(2)}) collective-permute-start(f32[3,320,256]{2,1,0:T(8,128)S(1)} %bitcast.163), channel_id=1, source_target_pairs={{0,8},{8,0},{1,9},{9,1},{2,10},{10,2},{3,11},{11,3},{4,12},{12,4},... | collective-permute-start | bytes 2949128 | tf_op jit(solution)/shard_map/ppermute | solution.py:19
  136.3 0.8 copy-start.7
  138.2 21.5 %all-to-all-start.6 = ((f32[8,64,256]{2,1,0:T(8,128)}), f32[8,64,256]{2,1,0:T(8,128)S(1)}, u32[]{:S(2)}, u32[]{:S(2)}) async-start(f32[8,64,256]{2,1,0:T(8,128)} %broadcast_in_dim.23), calls=%async_computation.6 | async-start | bytes 1048576 | tf_op jit(solution)/shard_map/all_to_all | solution.py:15
  144.4 1.5 copy-start.4
  159.7 1.0 copy-start.8
  159.7 1.0 slice-start
  184.9 1.0 copy-start.5

commit v10 on v9

--- a/solution.py
+++ b/solution.py
@@ -68,11 +68,15 @@
     nz, nx = lax.axis_size("z"), lax.axis_size("x")
     chip = (lax.axis_index("x") * nz + lax.axis_index("z")).astype(jnp.uint32)
 
-    owners = [owner_map[k].astype(jnp.uint32) for k in range(PANELS)]
+    owners = [owner_map[k] for k in range(PANELS)]
+    me = (lax.axis_index("x") * nz + lax.axis_index("z")) * 2 + core
+    first_mine, second_mine, third_mine = (o == me for o in owners)
+    mine = first_mine | (
+        (owners[0] != me ^ 1) & (second_mine | ((owners[1] != me ^ 1) & third_mine))
+    )
+    owners = [o.astype(jnp.uint32) for o in owners]
     chips = [o >> 1 for o in owners]
-    cores = [(o & 1).astype(jnp.int32) for o in owners]
     held = [h == chip for h in chips]
-    own_core = jnp.where(held[0], cores[0], jnp.where(held[1], cores[1], cores[2]))
     panels = [
         jnp.where(held[0], 0, jnp.where(held[1], 1, 2)),
         jnp.where(held[2], 2, jnp.where(held[1], 1, 0)),
@@ -84,7 +88,6 @@
     ]
     sources = [(h % nz) * nx + h // nz for h in chips]
 
-    mine = own_core == core
     kept, sent = halves(inverse, on_first, 1)
     got = swapped(sent)
     part = jnp.where(mine, kept, got)
@@ -138,16 +141,16 @@
     rows[0] = rows[0] + product(own_group(1, 0), pivot[0])
     rows, first, pivot = lax.optimization_barrier((rows, first, pivot))
     pivot.append(to_all_rows(rows[0]))
-    solved.append(product(own_group(0, 0), pivot[0]))
     rows[1] = rows[1] + product(own_group(2, 0), pivot[0])
-    tail = tail + product([r[0] for r in rest], pivot[0])
     rows[1] = rows[1] + product(own_group(2, 1), pivot[1])
-    rows, tail, solved = lax.optimization_barrier((rows, tail, solved))
+    rows, first, pivot, rest, tail = lax.optimization_barrier((rows, first, pivot, rest, tail))
     pivot.append(to_all_rows(rows[1]))
-    pivot, first, rest, tail = lax.optimization_barrier((pivot, first, rest, tail))
-    for k in range(1, PANELS):
+    for k in range(PANELS - 1):
         solved.append(product(own_group(k, k), pivot[k]))
         tail = tail + product([r[k] for r in rest], pivot[k])
+    pivot, first, rest, tail = lax.optimization_barrier((pivot, first, rest, tail))
+    solved.append(product(own_group(PANELS - 1, PANELS - 1), pivot[-1]))
+    tail = tail + product([r[-1] for r in rest], pivot[-1])
     return jnp.concatenate([*solved, tail])
 
 

time: 188 us -> 168 us (0.89)
  blocking collectives: 87.6 us -> 49.7 us
  starting transfers between devices: 35.5 us -> 47.1 us
  between operations: 2.44 us -> 5.85 us
    all_to_all x2 -> x0, blocking collectives: 37.1 us -> none  [sent_to_all(): lax.all_to_all(jnp.broadcast_to(x[None], (count, *x.shape)), axis, 0, 0,...]
    all_to_all x3 -> x5, starting transfers between devices: 11.7 us -> 24.1 us  [sent_to_all(): lax.all_to_all(jnp.broadcast_to(x[None], (count, *x.shape)), axis, 0, 0,...]
    all_to_all x3 -> x5, waiting for transfers between devices: 37.1 us -> 37.5 us  [sent_to_all(): lax.all_to_all(jnp.broadcast_to(x[None], (count, *x.shape)), axis, 0, 0,...]
  transfers between devices with their start and end apart: 7 -> 9, of which waited for: 3 -> 4; matrix products, arithmetic and copies ran while one was open for 7% -> 7% of each run, Pallas kernels for 0% -> 0%
where the time goes in v10:
time: 168 us; the launch traced here: 167 us
  blocking collectives  49.7 us (30%)
  starting transfers between devices  47.1 us (28%)
  waiting for transfers between devices  38.5 us (23%)
  matrix products  12.7 us (8%)
  local copies, waits for them, and re-layouts  9.35 us (6%)
  between operations  5.85 us (3%)
  other arithmetic  3.41 us (2%)
    all_to_all x5, waiting for transfers between devices, sent_to_all(): lax.all_to_all(jnp.broadcast_to(x[None], (count, *x.shape)), axis, 0, 0,...  37.5 us
    all_to_all x1, blocking collectives, spread(): lax.all_to_all(jnp.concatenate(sent, axis=1), CHIP, 0, 0, tiled=True)  27.3 us
    all_to_all x5, starting transfers between devices, sent_to_all(): lax.all_to_all(jnp.broadcast_to(x[None], (count, *x.shape)), axis, 0, 0,...  24.1 us
    ppermute x4, starting transfers between devices, swapped(): return lax.ppermute(x, 'core', SWAP)  23 us
    dot_general x19, matrix products, dot(): jnp.dot(a, b, precision=lax.Precision.HIGHEST, preferred_element_type=jnp...  12.7 us
    all_gather x1, blocking collectives, per_device(): rest = lax.all_gather(kept[PANELS:].swapaxes(0, 1), 'x', axis=2, tiled=True)  12.4 us
    all_gather x1, blocking collectives, per_device(): first = lax.all_gather(first, 'x', axis=1, tiled=True)  9.93 us
    broadcast_in_dim x5, local copies, waits for them, and re-layouts, sent_to_all(): jnp.broadcast_to(x[None], (count, *x.shape))  4.22 us
  transfers between devices with their start and end apart: 9, of which 4 were waited for; matrix products, arithmetic and copies ran while one was open for 7% of the time, Pallas kernels for 0%

profile of v10, /device:TPU:1, one launch (start us, length us, event | category | flops | bytes accessed | tf_op | source)
XLA Modules:
  0.0 166.6 jit_solution(1757196175804964812)
XLA Ops:
  0.0 8.9 %collective-permute-start.1 = (f32[512,512]{1,0:T(8,128)}, f32[512,512]{1,0:T(8,128)}, u32[]{:S(2)}, u32[]{:S(2)}) collective-permute-start(f32[512,512]{1,0:T(8,128)} %bitcast.153), channel_id=1, source_target_pairs={{0,8},{8,0},{1,9},{9,1},{2,10},{10,2},{3,11},{11,3},{4,12},{12,4},... | collective-permute-start | bytes 3145736 | tf_op jit(solution)/shard_map/ppermute | solution.py:19
  9.8 2.1 %collective-permute-start = (f32[64,256]{1,0:T(8,128)S(1)}, f32[64,256]{1,0:T(8,128)S(1)}, u32[]{:S(2)}, u32[]{:S(2)}) collective-permute-start(f32[64,256]{1,0:T(8,128)S(1)} %slice_select_fusion.6), channel_id=1, source_target_pairs={{0,8},{8,0},{1,9},{9,1},{2,10},{10,2},{3,11},{11,3},{4,12},{12,4},... | collective-permute-start | bytes 196616 | tf_op jit(solution)/shard_map/ppermute | solution.py:19
  16.8 3.5 %all-to-all-start.3 = ((f32[8,64,256]{2,1,0:T(8,128)}), f32[8,64,256]{2,1,0:T(8,128)S(1)}, u32[]{:S(2)}, u32[]{:S(2)}) async-start(f32[8,64,256]{2,1,0:T(8,128)} %broadcast_in_dim.19), calls=%async_computation.3 | async-start | bytes 1048576 | tf_op jit(solution)/shard_map/all_to_all | solution.py:15
  22.3 1.4 broadcast_select_fusion.1
  23.7 14.4 %all-to-all-done.3 = f32[8,64,256]{2,1,0:T(8,128)S(1)} async-done(((f32[8,64,256]{2,1,0:T(8,128)}), f32[8,64,256]{2,1,0:T(8,128)S(1)}, u32[]{:S(2)}, u32[]{:S(2)}) %all-to-all-start.3) | async-done | bytes 524320 | tf_op jit(solution)/shard_map/all_to_all | solution.py:15
  38.1 28.4 %conditional.1 = (f32[3,16,256]{2,1,0:T(8,128)S(1)}) conditional(s32[]{:T(128)} %convert_element_type.26, (s32[]{:T(128)}, f32[64,256]{1,0:T(8,128)S(1)}, f32[512,512]{1,0:T(8,128)S(1)}, f32[512,256]{1,0:T(8,128)S(1)}, u32[]{:T(128)}, /*index=5*/u32[]{:T(128)}, u32[]{:T(128)}) %tuple.37, (s32[]{:T(128)}, f32[64,256]{1,0:T(8,128)S(1)}, ...), branch_computations={%region_0.1_spmd, %region_1.2_spmd} | conditional | flops 1612238336 | bytes 16823980 | solution.py:99
  39.2 27.3 %all_to_all.37 = f32[32,1,16,256]{3,2,1,0:T(8,128)S(1)} all-to-all(f32[32,1,16,256]{3,2,1,0:T(8,128)S(1)} %bitcast.169), channel_id=1, replica_groups=mesh['x'=4,'z'=8,'core'=2,'row'=8] {'z','x'}, dimensions={0} | all-to-all | bytes 1048576 | tf_op jit(solution)/shard_map/cond/branch_0_fun/all_to_all | solution.py:35
  67.3 3.6 %all-to-all-start.4 = ((f32[8,3,16,256]{3,2,1,0:T(8,128)}), f32[8,3,16,256]{3,2,1,0:T(8,128)S(1)}, u32[]{:S(2)}, u32[]{:S(2)}) async-start(f32[8,3,16,256]{3,2,1,0:T(8,128)} %broadcast_in_dim.20), calls=%async_computation.4 | async-start | bytes 786432 | tf_op jit(solution)/shard_map/all_to_all | solution.py:15
  71.7 1.7 %gather_fusion = f32[448,256]{1,0:T(8,128)S(1)} fusion(f32[512,256]{1,0:T(8,128)S(1)} %copy-done, s32[1024]{0:T(1024)S(1)} %pad_clamp_fusion.1), kind=kCustom, calls=%fused_computation | custom fusion | bytes 919296 | tf_op jit(solution)/shard_map/gather | solution.py:114
  74.2 9.3 %all-to-all-done.4 = f32[8,3,16,256]{3,2,1,0:T(8,128)S(1)} async-done(((f32[8,3,16,256]{3,2,1,0:T(8,128)}), f32[8,3,16,256]{3,2,1,0:T(8,128)S(1)}, u32[]{:S(2)}, u32[]{:S(2)}) %all-to-all-start.4) | async-done | bytes 393248 | tf_op jit(solution)/shard_map/all_to_all | solution.py:15
  84.4 3.5 %all-to-all-start.5 = ((f32[8,64,256]{2,1,0:T(8,128)}), f32[8,64,256]{2,1,0:T(8,128)S(1)}, u32[]{:S(2)}, u32[]{:S(2)}) async-start(f32[8,64,256]{2,1,0:T(8,128)} %broadcast_in_dim.22), calls=%async_computation.5 | async-start | bytes 1048576 | tf_op jit(solution)/shard_map/all_to_all | solution.py:15
  87.9 9.9 %all_gather.6 = f32[6,64,256]{2,1,0:T(8,128)S(1)} all-gather(f32[6,16,256]{2,1,0:T(8,128)S(1)} %fusion.56), channel_id=1, replica_groups=mesh['x'=4,'z'=8,'core'=2,'row'=8] {'x'}, dimensions={1}, use_global_device_ids=true | all-gather | bytes 491520 | tf_op jit(solution)/shard_map/all_gather | solution.py:127
  97.9 7.7 %collective-permute-start.2 = (f32[6,64,256]{2,1,0:T(8,128)S(1)}, f32[6,64,256]{2,1,0:T(8,128)S(1)}, u32[]{:S(2)}, u32[]{:S(2)}) collective-permute-start(f32[6,64,256]{2,1,0:T(8,128)S(1)} %all_gather.6), channel_id=1, source_target_pairs={{0,8},{8,0},{1,9},{9,1},{2,10},{10,2},{3,11},{11,3},{4,12},{12,4},... | collective-permute-start | bytes 1179656 | tf_op jit(solution)/shard_map/ppermute | solution.py:19
  108.0 7.0 %all-to-all-start.6 = ((f32[8,64,256]{2,1,0:T(8,128)}), f32[8,64,256]{2,1,0:T(8,128)S(1)}, u32[]{:S(2)}, u32[]{:S(2)}) async-start(f32[8,64,256]{2,1,0:T(8,128)} %broadcast_in_dim.23), calls=%async_computation.6 | async-start | bytes 1048576 | tf_op jit(solution)/shard_map/all_to_all | solution.py:15
  115.0 12.4 %all_gather.7 = f32[3,5,64,256]{3,2,1,0:T(8,128)S(1)} all-gather(f32[3,5,16,256]{3,2,1,0:T(8,128)S(1)} %copy_bitcast_fusion), channel_id=1, replica_groups=mesh['x'=4,'z'=8,'core'=2,'row'=8] {'x'}, dimensions={2}, use_global_device_ids=true | all-gather | bytes 1228800 | tf_op jit(solution)/shard_map/all_gather | solution.py:133
  127.4 4.4 %collective-permute-start.3 = (f32[3,320,256]{2,1,0:T(8,128)S(1)}, f32[3,320,256]{2,1,0:T(8,128)}, u32[]{:S(2)}, u32[]{:S(2)}) collective-permute-start(f32[3,320,256]{2,1,0:T(8,128)S(1)} %bitcast.161), channel_id=1, source_target_pairs={{0,8},{8,0},{1,9},{9,1},{2,10},{10,2},{3,11},{11,3},{4,12},{12,4},... | collective-permute-start | bytes 2949128 | tf_op jit(solution)/shard_map/ppermute | solution.py:19
  131.8 1.1 fusion.43
  134.9 2.1 %fusion.18 = f32[320,256]{1,0:T(8,128)} fusion(f32[256,256]{1,0:T(8,128)S(1)} %bitcast.157, f32[3,320,256]{2,1,0:T(8,128)} %collective-permute-done.3), kind=kOutput, calls=%fused_computation.55 | convolution fusion | flops 251658240 | bytes 917504 | tf_op jit(solution)/shard_map/dot_general | solution.py:23
  137.9 6.5 %all-to-all-start.7 = ((f32[8,64,256]{2,1,0:T(8,128)}), f32[8,64,256]{2,1,0:T(8,128)S(1)}, u32[]{:S(2)}, u32[]{:S(2)}) async-start(f32[8,64,256]{2,1,0:T(8,128)} %broadcast_in_dim.24), calls=%async_computation.7 | async-start | bytes 1048576 | tf_op jit(solution)/shard_map/all_to_all | solution.py:15
  144.9 1.4 fusion.21
  147.4 1.2 add_add_fusion
  148.6 13.9 %all-to-all-done.7 = f32[8,64,256]{2,1,0:T(8,128)S(1)} async-done(((f32[8,64,256]{2,1,0:T(8,128)}), f32[8,64,256]{2,1,0:T(8,128)S(1)}, u32[]{:S(2)}, u32[]{:S(2)}) %all-to-all-start.7) | async-done | bytes 524320 | tf_op jit(solution)/shard_map/all_to_all | solution.py:15
  163.2 1.1 convolution_add_fusion.3
  164.3 1.4 fusion.13
  (80 shorter events, 15.0 us)
Async XLA Ops:
  0.0 71.7 %copy-start = (f32[512,256]{1,0:T(8,128)S(1)}, f32[512,256]{1,0:T(8,128)}, u32[]{:S(2)}) copy-start(f32[512,256]{1,0:T(8,128)} %param.7) | copy-start | bytes 1572868
  0.0 15.9 %copy-start.10 = (f32[1,64,512]{2,1,0:T(8,128)S(1)}, f32[1,64,512]{2,1,0:T(8,128)}, u32[]{:S(2)}) copy-start(f32[1,64,512]{2,1,0:T(8,128)} %param.9) | copy-start | bytes 393220
  0.0 22.3 %collective-permute-start.1 = (f32[512,512]{1,0:T(8,128)}, f32[512,512]{1,0:T(8,128)}, u32[]{:S(2)}, u32[]{:S(2)}) collective-permute-start(f32[512,512]{1,0:T(8,128)} %bitcast.153), channel_id=1, source_target_pairs={{0,8},{8,0},{1,9},{9,1},{2,10},{10,2},{3,11},{11,3},{4,12},{12,4},... | collective-permute-start | bytes 3145736 | tf_op jit(solution)/shard_map/ppermute | solution.py:19
  8.9 3.0 %copy-start.13 = (s32[64]{0:T(128)S(1)}, s32[64]{0:T(128)}, u32[]{:S(2)}) copy-start(s32[64]{0:T(128)} %param.10) | copy-start | bytes 772
  9.8 12.5 %copy-start.1 = (f32[1,512,512]{2,1,0:T(8,128)S(1)}, f32[1,512,512]{2,1,0:T(8,128)}, u32[]{:S(2)}) copy-start(f32[1,512,512]{2,1,0:T(8,128)} %param.8) | copy-start | bytes 3145732
  9.8 6.1 %collective-permute-start = (f32[64,256]{1,0:T(8,128)S(1)}, f32[64,256]{1,0:T(8,128)S(1)}, u32[]{:S(2)}, u32[]{:S(2)}) collective-permute-start(f32[64,256]{1,0:T(8,128)S(1)} %slice_select_fusion.6), channel_id=1, source_target_pairs={{0,8},{8,0},{1,9},{9,1},{2,10},{10,2},{3,11},{11,3},{4,12},{12,4},... | collective-permute-start | bytes 196616 | tf_op jit(solution)/shard_map/ppermute | solution.py:19
  16.8 21.4 %all-to-all-start.3 = ((f32[8,64,256]{2,1,0:T(8,128)}), f32[8,64,256]{2,1,0:T(8,128)S(1)}, u32[]{:S(2)}, u32[]{:S(2)}) async-start(f32[8,64,256]{2,1,0:T(8,128)} %broadcast_in_dim.19), calls=%async_computation.3 | async-start | bytes 1048576 | tf_op jit(solution)/shard_map/all_to_all | solution.py:15
  67.3 16.1 %all-to-all-start.4 = ((f32[8,3,16,256]{3,2,1,0:T(8,128)}), f32[8,3,16,256]{3,2,1,0:T(8,128)S(1)}, u32[]{:S(2)}, u32[]{:S(2)}) async-start(f32[8,3,16,256]{3,2,1,0:T(8,128)} %broadcast_in_dim.20), calls=%async_computation.4 | async-start | bytes 786432 | tf_op jit(solution)/shard_map/all_to_all | solution.py:15
  73.5 33.4 %copy-start.3 = (f32[448,256]{1,0:T(8,128)}, f32[448,256]{1,0:T(8,128)S(1)}, u32[]{:S(2)}) copy-start(f32[448,256]{1,0:T(8,128)S(1)} %gather_fusion) | copy-start | bytes 1376260
  83.4 4.5 %copy-start.6 = (f32[8,3,16,256]{3,2,1,0:T(8,128)}, f32[8,3,16,256]{3,2,1,0:T(8,128)S(1)}, u32[]{:S(2)}) copy-start(f32[8,3,16,256]{3,2,1,0:T(8,128)S(1)} %all-to-all-done.4) | copy-start | bytes 1179652
  84.4 21.2 %all-to-all-start.5 = ((f32[8,64,256]{2,1,0:T(8,128)}), f32[8,64,256]{2,1,0:T(8,128)S(1)}, u32[]{:S(2)}, u32[]{:S(2)}) async-start(f32[8,64,256]{2,1,0:T(8,128)} %broadcast_in_dim.22), calls=%async_computation.5 | async-start | bytes 1048576 | tf_op jit(solution)/shard_map/all_to_all | solution.py:15
  97.9 7.7 %copy-start.4 = (f32[6,64,256]{2,1,0:T(8,128)}, f32[6,64,256]{2,1,0:T(8,128)S(1)}, u32[]{:S(2)}) copy-start(f32[6,64,256]{2,1,0:T(8,128)S(1)} %all_gather.6) | copy-start | bytes 1179652
  97.9 9.0 %collective-permute-start.2 = (f32[6,64,256]{2,1,0:T(8,128)S(1)}, f32[6,64,256]{2,1,0:T(8,128)S(1)}, u32[]{:S(2)}, u32[]{:S(2)}) collective-permute-start(f32[6,64,256]{2,1,0:T(8,128)S(1)} %all_gather.6), channel_id=1, source_target_pairs={{0,8},{8,0},{1,9},{9,1},{2,10},{10,2},{3,11},{11,3},{4,12},{12,4},... | collective-permute-start | bytes 1179656 | tf_op jit(solution)/shard_map/ppermute | solution.py:19
  106.9 1.1 copy-start.11
  108.0 7.0 %copy-start.7 = (f32[8,3,16,256]{3,2,1,0:T(8,128)S(1)}, f32[8,3,16,256]{3,2,1,0:T(8,128)}, u32[]{:S(2)}) copy-start(f32[8,3,16,256]{3,2,1,0:T(8,128)} %copy-done.6) | copy-start | bytes 1179652
  108.0 25.1 %all-to-all-start.6 = ((f32[8,64,256]{2,1,0:T(8,128)}), f32[8,64,256]{2,1,0:T(8,128)S(1)}, u32[]{:S(2)}, u32[]{:S(2)}) async-start(f32[8,64,256]{2,1,0:T(8,128)} %broadcast_in_dim.23), calls=%async_computation.6 | async-start | bytes 1048576 | tf_op jit(solution)/shard_map/all_to_all | solution.py:15
  127.4 5.5 %copy-start.5 = (f32[6,64,256]{2,1,0:T(8,128)S(1)}, f32[6,64,256]{2,1,0:T(8,128)}, u32[]{:S(2)}) copy-start(f32[6,64,256]{2,1,0:T(8,128)} %copy-done.4) | copy-start | bytes 1179652
  127.4 7.0 %collective-permute-start.3 = (f32[3,320,256]{2,1,0:T(8,128)S(1)}, f32[3,320,256]{2,1,0:T(8,128)}, u32[]{:S(2)}, u32[]{:S(2)}) collective-permute-start(f32[3,320,256]{2,1,0:T(8,128)S(1)} %bitcast.161), channel_id=1, source_target_pairs={{0,8},{8,0},{1,9},{9,1},{2,10},{10,2},{3,11},{11,3},{4,12},{12,4},... | collective-permute-start | bytes 2949128 | tf_op jit(solution)/shard_map/ppermute | solution.py:19
  133.1 1.0 copy-start.12
  133.2 0.9 slice-start
  137.9 24.6 %all-to-all-start.7 = ((f32[8,64,256]{2,1,0:T(8,128)}), f32[8,64,256]{2,1,0:T(8,128)S(1)}, u32[]{:S(2)}, u32[]{:S(2)}) async-start(f32[8,64,256]{2,1,0:T(8,128)} %broadcast_in_dim.24), calls=%async_computation.7 | async-start | bytes 1048576 | tf_op jit(solution)/shard_map/all_to_all | solution.py:15
  146.3 1.0 slice-start.1
  146.3 1.1 copy-start.8
  163.2 1.2 copy-start.9
  (1 other events, 0.7 us)

commit v11 on v9

--- a/solution.py
+++ b/solution.py
@@ -73,6 +73,7 @@
     cores = [(o & 1).astype(jnp.int32) for o in owners]
     held = [h == chip for h in chips]
     own_core = jnp.where(held[0], cores[0], jnp.where(held[1], cores[1], cores[2]))
+    mine = own_core == core
     panels = [
         jnp.where(held[0], 0, jnp.where(held[1], 1, 2)),
         jnp.where(held[2], 2, jnp.where(held[1], 1, 0)),
@@ -84,7 +85,6 @@
     ]
     sources = [(h % nz) * nx + h // nz for h in chips]
 
-    mine = own_core == core
     kept, sent = halves(inverse, on_first, 1)
     got = swapped(sent)
     part = jnp.where(mine, kept, got)
@@ -138,16 +138,18 @@
     rows[0] = rows[0] + product(own_group(1, 0), pivot[0])
     rows, first, pivot = lax.optimization_barrier((rows, first, pivot))
     pivot.append(to_all_rows(rows[0]))
-    solved.append(product(own_group(0, 0), pivot[0]))
     rows[1] = rows[1] + product(own_group(2, 0), pivot[0])
-    tail = tail + product([r[0] for r in rest], pivot[0])
-    rows[1] = rows[1] + product(own_group(2, 1), pivot[1])
-    rows, tail, solved = lax.optimization_barrier((rows, tail, solved))
+    rows, pivot, last = lax.optimization_barrier((rows, pivot, own_group(2, 1)))
+    rows[1] = rows[1] + product(last, pivot[1])
+    rows, first, pivot, rest, tail = lax.optimization_barrier((rows, first, pivot, rest, tail))
     pivot.append(to_all_rows(rows[1]))
-    pivot, first, rest, tail = lax.optimization_barrier((pivot, first, rest, tail))
-    for k in range(1, PANELS):
+    for k in range(PANELS - 1):
         solved.append(product(own_group(k, k), pivot[k]))
         tail = tail + product([r[k] for r in rest], pivot[k])
+    last = own_group(PANELS - 1, PANELS - 1), [r[-1] for r in rest]
+    pivot, last, tail = lax.optimization_barrier((pivot, last, tail))
+    solved.append(product(last[0], pivot[-1]))
+    tail = tail + product(last[1], pivot[-1])
     return jnp.concatenate([*solved, tail])
 
 

time: 188 us -> 179 us (0.952)
  blocking collectives: 87.6 us -> 69.1 us
  starting transfers between devices: 35.5 us -> 40.4 us
  local copies, waits for them, and re-layouts: 9.06 us -> 13 us
  waiting for transfers between devices: 37.1 us -> 39.4 us
    all_to_all x2 -> x1, blocking collectives: 37.1 us -> 17.1 us  [sent_to_all(): lax.all_to_all(jnp.broadcast_to(x[None], (count, *x.shape)), axis, 0, 0,...]
    all_to_all x3 -> x4, starting transfers between devices: 11.7 us -> 18 us  [sent_to_all(): lax.all_to_all(jnp.broadcast_to(x[None], (count, *x.shape)), axis, 0, 0,...]
    squeeze x0 -> x5, local copies, waits for them, and re-layouts: none -> 3.33 us  [the longest x2 2.47 us: per_device(): last = (own_group(PANELS - 1, PANELS - 1), [r[-1] for r in rest])]
    all_to_all x3 -> x4, waiting for transfers between devices: 37.1 us -> 38.4 us  [sent_to_all(): lax.all_to_all(jnp.broadcast_to(x[None], (count, *x.shape)), axis, 0, 0,...]
  transfers between devices with their start and end apart: 7 -> 8, of which waited for: 3 -> 4; matrix products, arithmetic and copies ran while one was open for 7% -> 7% of each run, Pallas kernels for 0% -> 0%
where the time goes in v11:
time: 179 us; the launch traced here: 178 us
  blocking collectives  69.1 us (39%)
  starting transfers between devices  40.4 us (23%)
  waiting for transfers between devices  39.4 us (22%)
  local copies, waits for them, and re-layouts  13 us (7%)
  matrix products  10.1 us (6%)
  other arithmetic  3.45 us (2%)
  between operations  2.36 us (1%)
    all_to_all x4, waiting for transfers between devices, sent_to_all(): lax.all_to_all(jnp.broadcast_to(x[None], (count, *x.shape)), axis, 0, 0,...  38.4 us
    all_to_all x1, blocking collectives, spread(): lax.all_to_all(jnp.concatenate(sent, axis=1), CHIP, 0, 0, tiled=True)  27.3 us
    ppermute x4, starting transfers between devices, swapped(): return lax.ppermute(x, 'core', SWAP)  22.4 us
    all_to_all x4, starting transfers between devices, sent_to_all(): lax.all_to_all(jnp.broadcast_to(x[None], (count, *x.shape)), axis, 0, 0,...  18 us
    all_to_all x1, blocking collectives, sent_to_all(): lax.all_to_all(jnp.broadcast_to(x[None], (count, *x.shape)), axis, 0, 0,...  17.1 us
    all_gather x1, blocking collectives, per_device(): rest = lax.all_gather(kept[PANELS:].swapaxes(0, 1), 'x', axis=2, tiled=True)  13.2 us
    all_gather x1, blocking collectives, per_device(): first = lax.all_gather(first, 'x', axis=1, tiled=True)  11.5 us
    dot_general x19, matrix products, dot(): jnp.dot(a, b, precision=lax.Precision.HIGHEST, preferred_element_type=jnp...  10.1 us
  transfers between devices with their start and end apart: 8, of which 4 were waited for; matrix products, arithmetic and copies ran while one was open for 7% of the time, Pallas kernels for 0%

profile of v11, /device:TPU:1, one launch (start us, length us, event | category | flops | bytes accessed | tf_op | source)
XLA Modules:
  0.0 177.9 jit_solution(17527043072376441062)
XLA Ops:
  0.0 8.9 %collective-permute-start.1 = (f32[512,512]{1,0:T(8,128)}, f32[512,512]{1,0:T(8,128)}, u32[]{:S(2)}, u32[]{:S(2)}) collective-permute-start(f32[512,512]{1,0:T(8,128)} %bitcast.154), channel_id=1, source_target_pairs={{0,8},{8,0},{1,9},{9,1},{2,10},{10,2},{3,11},{11,3},{4,12},{12,4},... | collective-permute-start | bytes 3145736 | tf_op jit(solution)/shard_map/ppermute | solution.py:19
  9.8 1.9 %collective-permute-start = (f32[64,256]{1,0:T(8,128)S(1)}, f32[64,256]{1,0:T(8,128)S(1)}, u32[]{:S(2)}, u32[]{:S(2)}) collective-permute-start(f32[64,256]{1,0:T(8,128)S(1)} %slice_select_fusion.6), channel_id=1, source_target_pairs={{0,8},{8,0},{1,9},{9,1},{2,10},{10,2},{3,11},{11,3},{4,12},{12,4},... | collective-permute-start | bytes 196616 | tf_op jit(solution)/shard_map/ppermute | solution.py:19
  15.1 3.5 %all-to-all-start.3 = ((f32[8,64,256]{2,1,0:T(8,128)}), f32[8,64,256]{2,1,0:T(8,128)S(1)}, u32[]{:S(2)}, u32[]{:S(2)}) async-start(f32[8,64,256]{2,1,0:T(8,128)} %broadcast_in_dim.19), calls=%async_computation.3 | async-start | bytes 1048576 | tf_op jit(solution)/shard_map/all_to_all | solution.py:15
  20.0 1.4 broadcast_select_fusion.1
  21.5 15.0 %all-to-all-done.3 = f32[8,64,256]{2,1,0:T(8,128)S(1)} async-done(((f32[8,64,256]{2,1,0:T(8,128)}), f32[8,64,256]{2,1,0:T(8,128)S(1)}, u32[]{:S(2)}, u32[]{:S(2)}) %all-to-all-start.3) | async-done | bytes 524320 | tf_op jit(solution)/shard_map/all_to_all | solution.py:15
  36.5 28.4 %conditional.1 = (f32[3,16,256]{2,1,0:T(8,128)S(1)}) conditional(s32[]{:T(128)} %convert_element_type.47, (s32[]{:T(128)}, f32[64,256]{1,0:T(8,128)S(1)}, f32[512,512]{1,0:T(8,128)S(1)}, f32[512,256]{1,0:T(8,128)S(1)}, u32[]{:T(128)}, /*index=5*/u32[]{:T(128)}, u32[]{:T(128)}) %tuple.41, (s32[]{:T(128)}, f32[64,256]{1,0:T(8,128)S(1)}, ...), branch_computations={%region_0.1_spmd, %region_1.2_spmd} | conditional | flops 1612238336 | bytes 16823980 | solution.py:96
  36.5 1.0 fusion
  37.5 27.3 %all_to_all.37 = f32[32,1,16,256]{3,2,1,0:T(8,128)S(1)} all-to-all(f32[32,1,16,256]{3,2,1,0:T(8,128)S(1)} %bitcast.170), channel_id=1, replica_groups=mesh['x'=4,'z'=8,'core'=2,'row'=8] {'z','x'}, dimensions={0} | all-to-all | bytes 1048576 | tf_op jit(solution)/shard_map/cond/branch_0_fun/all_to_all | solution.py:35
  64.9 17.1 %all_to_all.38 = f32[8,64,256]{2,1,0:T(8,128)S(1)} all-to-all(f32[8,64,256]{2,1,0:T(8,128)S(1)} %broadcast_in_dim.22), channel_id=1, replica_groups=mesh['x'=4,'z'=8,'core'=2,'row'=8] {'row'}, dimensions={0} | all-to-all | bytes 1048576 | tf_op jit(solution)/shard_map/all_to_all | solution.py:15
  82.8 4.3 %all-to-all-start.4 = ((f32[8,3,16,256]{3,2,1,0:T(8,128)}), f32[8,3,16,256]{3,2,1,0:T(8,128)S(1)}, u32[]{:S(2)}, u32[]{:S(2)}) async-start(f32[8,3,16,256]{3,2,1,0:T(8,128)} %broadcast_in_dim.20), calls=%async_computation.4 | async-start | bytes 786432 | tf_op jit(solution)/shard_map/all_to_all | solution.py:15
  87.1 1.7 gather_fusion
  88.9 9.5 %all-to-all-done.4 = f32[8,3,16,256]{3,2,1,0:T(8,128)S(1)} async-done(((f32[8,3,16,256]{3,2,1,0:T(8,128)}), f32[8,3,16,256]{3,2,1,0:T(8,128)S(1)}, u32[]{:S(2)}, u32[]{:S(2)}) %all-to-all-start.4) | async-done | bytes 393248 | tf_op jit(solution)/shard_map/all_to_all | solution.py:15
  98.5 11.5 %all_gather.6 = f32[6,64,256]{2,1,0:T(8,128)S(1)} all-gather(f32[6,16,256]{2,1,0:T(8,128)S(1)} %fusion.42), channel_id=1, replica_groups=mesh['x'=4,'z'=8,'core'=2,'row'=8] {'x'}, dimensions={1}, use_global_device_ids=true | all-gather | bytes 491520 | tf_op jit(solution)/shard_map/all_gather | solution.py:124
  110.0 7.8 %collective-permute-start.2 = (f32[6,64,256]{2,1,0:T(8,128)S(1)}, f32[6,64,256]{2,1,0:T(8,128)S(1)}, u32[]{:S(2)}, u32[]{:S(2)}) collective-permute-start(f32[6,64,256]{2,1,0:T(8,128)S(1)} %all_gather.6), channel_id=1, source_target_pairs={{0,8},{8,0},{1,9},{9,1},{2,10},{10,2},{3,11},{11,3},{4,12},{12,4},... | collective-permute-start | bytes 1179656 | tf_op jit(solution)/shard_map/ppermute | solution.py:19
  118.1 1.0 collective-permute-done.2
  120.2 3.5 %all-to-all-start.6 = ((f32[8,64,256]{2,1,0:T(8,128)}), f32[8,64,256]{2,1,0:T(8,128)S(1)}, u32[]{:S(2)}, u32[]{:S(2)}) async-start(f32[8,64,256]{2,1,0:T(8,128)} %broadcast_in_dim.23), calls=%async_computation.6 | async-start | bytes 1048576 | tf_op jit(solution)/shard_map/all_to_all | solution.py:15
  123.7 13.2 %all_gather.7 = f32[3,5,64,256]{3,2,1,0:T(8,128)S(1)} all-gather(f32[3,5,16,256]{3,2,1,0:T(8,128)S(1)} %copy_bitcast_fusion), channel_id=1, replica_groups=mesh['x'=4,'z'=8,'core'=2,'row'=8] {'x'}, dimensions={2}, use_global_device_ids=true | all-gather | bytes 1228800 | tf_op jit(solution)/shard_map/all_gather | solution.py:130
  137.0 3.8 %collective-permute-start.3 = (f32[3,320,256]{2,1,0:T(8,128)S(1)}, f32[3,320,256]{2,1,0:T(8,128)}, u32[]{:S(2)}, u32[]{:S(2)}) collective-permute-start(f32[3,320,256]{2,1,0:T(8,128)S(1)} %bitcast.162), channel_id=1, source_target_pairs={{0,8},{8,0},{1,9},{9,1},{2,10},{10,2},{3,11},{11,3},{4,12},{12,4},... | collective-permute-start | bytes 2949128 | tf_op jit(solution)/shard_map/ppermute | solution.py:19
  140.7 1.1 fusion.33
  144.1 1.7 slice_bitcast_fusion
  145.9 2.2 %fusion.16 = f32[320,256]{1,0:T(8,128)} fusion(f32[256,256]{1,0:T(8,128)S(1)} %bitcast.157, f32[3,320,256]{2,1,0:T(8,128)} %collective-permute-done.3), kind=kOutput, calls=%fused_computation.53 | convolution fusion | flops 251658240 | bytes 917504 | tf_op jit(solution)/shard_map/dot_general | solution.py:23
  149.4 6.7 %all-to-all-start.7 = ((f32[8,64,256]{2,1,0:T(8,128)}), f32[8,64,256]{2,1,0:T(8,128)S(1)}, u32[]{:S(2)}, u32[]{:S(2)}) async-start(f32[8,64,256]{2,1,0:T(8,128)} %broadcast_in_dim.24), calls=%async_computation.7 | async-start | bytes 1048576 | tf_op jit(solution)/shard_map/all_to_all | solution.py:15
  157.4 1.4 fusion.19
  160.3 13.8 %all-to-all-done.7 = f32[8,64,256]{2,1,0:T(8,128)S(1)} async-done(((f32[8,64,256]{2,1,0:T(8,128)}), f32[8,64,256]{2,1,0:T(8,128)S(1)}, u32[]{:S(2)}, u32[]{:S(2)}) %all-to-all-start.7) | async-done | bytes 524320 | tf_op jit(solution)/shard_map/all_to_all | solution.py:15
  (83 shorter events, 16.1 us)
Async XLA Ops:
  0.0 19.3 %copy-start = (f32[512,256]{1,0:T(8,128)S(1)}, f32[512,256]{1,0:T(8,128)}, u32[]{:S(2)}) copy-start(f32[512,256]{1,0:T(8,128)} %param.7) | copy-start | bytes 1572868
  0.0 20.0 %collective-permute-start.1 = (f32[512,512]{1,0:T(8,128)}, f32[512,512]{1,0:T(8,128)}, u32[]{:S(2)}, u32[]{:S(2)}) collective-permute-start(f32[512,512]{1,0:T(8,128)} %bitcast.154), channel_id=1, source_target_pairs={{0,8},{8,0},{1,9},{9,1},{2,10},{10,2},{3,11},{11,3},{4,12},{12,4},... | collective-permute-start | bytes 3145736 | tf_op jit(solution)/shard_map/ppermute | solution.py:19
  8.9 2.9 %copy-start.12 = (s32[64]{0:T(128)S(1)}, s32[64]{0:T(128)}, u32[]{:S(2)}) copy-start(s32[64]{0:T(128)} %param.10) | copy-start | bytes 772
  8.9 5.3 %copy-start.9 = (f32[1,64,512]{2,1,0:T(8,128)S(1)}, f32[1,64,512]{2,1,0:T(8,128)}, u32[]{:S(2)}) copy-start(f32[1,64,512]{2,1,0:T(8,128)} %param.9) | copy-start | bytes 393220
  9.8 4.4 %collective-permute-start = (f32[64,256]{1,0:T(8,128)S(1)}, f32[64,256]{1,0:T(8,128)S(1)}, u32[]{:S(2)}, u32[]{:S(2)}) collective-permute-start(f32[64,256]{1,0:T(8,128)S(1)} %slice_select_fusion.6), channel_id=1, source_target_pairs={{0,8},{8,0},{1,9},{9,1},{2,10},{10,2},{3,11},{11,3},{4,12},{12,4},... | collective-permute-start | bytes 196616 | tf_op jit(solution)/shard_map/ppermute | solution.py:19
  14.2 5.8 %copy-start.1 = (f32[1,512,512]{2,1,0:T(8,128)S(1)}, f32[1,512,512]{2,1,0:T(8,128)}, u32[]{:S(2)}) copy-start(f32[1,512,512]{2,1,0:T(8,128)} %param.8) | copy-start | bytes 3145732
  15.1 21.4 %all-to-all-start.3 = ((f32[8,64,256]{2,1,0:T(8,128)}), f32[8,64,256]{2,1,0:T(8,128)S(1)}, u32[]{:S(2)}, u32[]{:S(2)}) async-start(f32[8,64,256]{2,1,0:T(8,128)} %broadcast_in_dim.19), calls=%async_computation.3 | async-start | bytes 1048576 | tf_op jit(solution)/shard_map/all_to_all | solution.py:15
  18.6 0.7 copy-start.13
  82.8 15.7 %all-to-all-start.4 = ((f32[8,3,16,256]{3,2,1,0:T(8,128)}), f32[8,3,16,256]{3,2,1,0:T(8,128)S(1)}, u32[]{:S(2)}, u32[]{:S(2)}) async-start(f32[8,3,16,256]{3,2,1,0:T(8,128)} %broadcast_in_dim.20), calls=%async_computation.4 | async-start | bytes 786432 | tf_op jit(solution)/shard_map/all_to_all | solution.py:15
  88.9 30.3 %copy-start.3 = (f32[448,256]{1,0:T(8,128)}, f32[448,256]{1,0:T(8,128)S(1)}, u32[]{:S(2)}) copy-start(f32[448,256]{1,0:T(8,128)S(1)} %gather_fusion) | copy-start | bytes 1376260
  110.0 8.1 %copy-start.4 = (f32[6,64,256]{2,1,0:T(8,128)}, f32[6,64,256]{2,1,0:T(8,128)S(1)}, u32[]{:S(2)}) copy-start(f32[6,64,256]{2,1,0:T(8,128)S(1)} %all_gather.6) | copy-start | bytes 1179652
  110.0 9.2 %collective-permute-start.2 = (f32[6,64,256]{2,1,0:T(8,128)S(1)}, f32[6,64,256]{2,1,0:T(8,128)S(1)}, u32[]{:S(2)}, u32[]{:S(2)}) collective-permute-start(f32[6,64,256]{2,1,0:T(8,128)S(1)} %all_gather.6), channel_id=1, source_target_pairs={{0,8},{8,0},{1,9},{9,1},{2,10},{10,2},{3,11},{11,3},{4,12},{12,4},... | collective-permute-start | bytes 1179656 | tf_op jit(solution)/shard_map/ppermute | solution.py:19
  119.1 1.1 copy-start.10
  120.2 23.3 %all-to-all-start.6 = ((f32[8,64,256]{2,1,0:T(8,128)}), f32[8,64,256]{2,1,0:T(8,128)S(1)}, u32[]{:S(2)}, u32[]{:S(2)}) async-start(f32[8,64,256]{2,1,0:T(8,128)} %broadcast_in_dim.23), calls=%async_computation.6 | async-start | bytes 1048576 | tf_op jit(solution)/shard_map/all_to_all | solution.py:15
  137.0 4.9 %copy-start.5 = (f32[6,64,256]{2,1,0:T(8,128)S(1)}, f32[6,64,256]{2,1,0:T(8,128)}, u32[]{:S(2)}) copy-start(f32[6,64,256]{2,1,0:T(8,128)} %copy-done.4) | copy-start | bytes 1179652
  137.0 7.2 %collective-permute-start.3 = (f32[3,320,256]{2,1,0:T(8,128)S(1)}, f32[3,320,256]{2,1,0:T(8,128)}, u32[]{:S(2)}, u32[]{:S(2)}) collective-permute-start(f32[3,320,256]{2,1,0:T(8,128)S(1)} %bitcast.162), channel_id=1, source_target_pairs={{0,8},{8,0},{1,9},{9,1},{2,10},{10,2},{3,11},{11,3},{4,12},{12,4},... | collective-permute-start | bytes 2949128 | tf_op jit(solution)/shard_map/ppermute | solution.py:19
  141.9 0.8 slice-start
  145.9 2.2 %copy-start.11 = (f32[6,64,256]{2,1,0:T(8,128)S(1)}, f32[6,64,256]{2,1,0:T(8,128)}, u32[]{:S(2)}) copy-start(f32[6,64,256]{2,1,0:T(8,128)} %copy-done.10) | copy-start | bytes 1179652
  149.4 24.7 %all-to-all-start.7 = ((f32[8,64,256]{2,1,0:T(8,128)}), f32[8,64,256]{2,1,0:T(8,128)S(1)}, u32[]{:S(2)}, u32[]{:S(2)}) async-start(f32[8,64,256]{2,1,0:T(8,128)} %broadcast_in_dim.24), calls=%async_computation.7 | async-start | bytes 1048576 | tf_op jit(solution)/shard_map/all_to_all | solution.py:15
  158.8 1.0 slice-start.1
  158.8 1.1 copy-start.8
  174.2 1.0 copy-start.6
  175.6 1.0 copy-start.7

commit v12 on v11

--- a/solution.py
+++ b/solution.py
@@ -13,6 +13,13 @@
 def sent_to_all(x, axis):
     count = lax.axis_size(axis)
     return lax.all_to_all(jnp.broadcast_to(x[None], (count, *x.shape)), axis, 0, 0, tiled=True)
+
+
+def sent_to_all_rows_reversed(x):
+    count = lax.axis_size(ROW)
+    tiles = jnp.broadcast_to(x[None], (count, *x.shape))
+    groups = [list(range(count))[::-1]]
+    return lax.all_to_all(tiles, ROW, 0, 0, tiled=True, axis_index_groups=groups)[::-1]
 
 
 def swapped(x):
@@ -110,8 +117,8 @@
         rows = row_perm[start:end] - position * rows_dev
         return rhs_block.at[rows].get(mode="promise_in_bounds")
 
-    def to_all_rows(rows):
-        return halves(sent_to_all(rows, ROW).reshape(pivots, columns), on_first, 0)
+    def to_all_rows(rows, send=lambda x: sent_to_all(x, ROW)):
+        return halves(send(rows).reshape(pivots, columns), on_first, 0)
 
     def product(a, b):
         return dot(a[0], b[0]) + dot(a[1], b[1])
@@ -137,7 +144,7 @@
 
     rows[0] = rows[0] + product(own_group(1, 0), pivot[0])
     rows, first, pivot = lax.optimization_barrier((rows, first, pivot))
-    pivot.append(to_all_rows(rows[0]))
+    pivot.append(to_all_rows(rows[0], sent_to_all_rows_reversed))
     rows[1] = rows[1] + product(own_group(2, 0), pivot[0])
     rows, pivot, last = lax.optimization_barrier((rows, pivot, own_group(2, 1)))
     rows[1] = rows[1] + product(last, pivot[1])

time: 179 us -> 177 us (0.989)
  blocking collectives: 69.1 us -> 67.2 us
    all_to_all x4 -> x3, starting transfers between devices: 18 us -> 12.5 us  [sent_to_all(): lax.all_to_all(jnp.broadcast_to(x[None], (count, *x.shape)), axis, 0, 0,...]
    all_to_all x0 -> x1, starting transfers between devices: none -> 3.95 us  [sent_to_all_rows_reversed(): lax.all_to_all(tiles, ROW, 0, 0, tiled=True, axis_index_groups=groups)[::-1]]
    all_to_all x4 -> x3, waiting for transfers between devices: 38.4 us -> 38.3 us  [sent_to_all(): lax.all_to_all(jnp.broadcast_to(x[None], (count, *x.shape)), axis, 0, 0,...]
where the time goes in v12:
time: 177 us; the launch traced here: 176 us
  blocking collectives  67.2 us (38%)
  starting transfers between devices  40.5 us (23%)
  waiting for transfers between devices  39.4 us (22%)
  local copies, waits for them, and re-layouts  13.1 us (7%)
  matrix products  10.1 us (6%)
  other arithmetic  3.45 us (2%)
  between operations  2.48 us (1%)
    all_to_all x3, waiting for transfers between devices, sent_to_all(): lax.all_to_all(jnp.broadcast_to(x[None], (count, *x.shape)), axis, 0, 0,...  38.3 us
    all_to_all x1, blocking collectives, spread(): lax.all_to_all(jnp.concatenate(sent, axis=1), CHIP, 0, 0, tiled=True)  27.3 us
    ppermute x4, starting transfers between devices, swapped(): return lax.ppermute(x, 'core', SWAP)  24 us
    all_to_all x1, blocking collectives, sent_to_all(): lax.all_to_all(jnp.broadcast_to(x[None], (count, *x.shape)), axis, 0, 0,...  17.1 us
    all_gather x1, blocking collectives, per_device(): rest = lax.all_gather(kept[PANELS:].swapaxes(0, 1), 'x', axis=2, tiled=True)  12.5 us
    all_to_all x3, starting transfers between devices, sent_to_all(): lax.all_to_all(jnp.broadcast_to(x[None], (count, *x.shape)), axis, 0, 0,...  12.5 us
    all_gather x1, blocking collectives, per_device(): first = lax.all_gather(first, 'x', axis=1, tiled=True)  10.3 us
    dot_general x19, matrix products, dot(): jnp.dot(a, b, precision=lax.Precision.HIGHEST, preferred_element_type=jnp...  10.1 us
  transfers between devices with their start and end apart: 8, of which 4 were waited for; matrix products, arithmetic and copies ran while one was open for 7% of the time, Pallas kernels for 0%

profile of v12, /device:TPU:1, one launch (start us, length us, event | category | flops | bytes accessed | tf_op | source)
XLA Modules:
  0.0 176.3 jit_solution(17496264097597544024)
XLA Ops:
  0.0 8.9 %collective-permute-start.1 = (f32[512,512]{1,0:T(8,128)}, f32[512,512]{1,0:T(8,128)}, u32[]{:S(2)}, u32[]{:S(2)}) collective-permute-start(f32[512,512]{1,0:T(8,128)} %bitcast.154), channel_id=1, source_target_pairs={{0,8},{8,0},{1,9},{9,1},{2,10},{10,2},{3,11},{11,3},{4,12},{12,4},... | collective-permute-start | bytes 3145736 | tf_op jit(solution)/shard_map/ppermute | solution.py:26
  9.8 1.9 %collective-permute-start = (f32[64,256]{1,0:T(8,128)S(1)}, f32[64,256]{1,0:T(8,128)S(1)}, u32[]{:S(2)}, u32[]{:S(2)}) collective-permute-start(f32[64,256]{1,0:T(8,128)S(1)} %slice_select_fusion.4), channel_id=1, source_target_pairs={{0,8},{8,0},{1,9},{9,1},{2,10},{10,2},{3,11},{11,3},{4,12},{12,4},... | collective-permute-start | bytes 196616 | tf_op jit(solution)/shard_map/ppermute | solution.py:26
  15.3 3.5 %all-to-all-start.3 = ((f32[8,64,256]{2,1,0:T(8,128)}), f32[8,64,256]{2,1,0:T(8,128)S(1)}, u32[]{:S(2)}, u32[]{:S(2)}) async-start(f32[8,64,256]{2,1,0:T(8,128)} %broadcast_in_dim.19), calls=%async_computation.3 | async-start | bytes 1048576 | tf_op jit(solution)/shard_map/all_to_all | solution.py:15
  20.2 1.4 broadcast_select_fusion.1
  21.6 15.0 %all-to-all-done.3 = f32[8,64,256]{2,1,0:T(8,128)S(1)} async-done(((f32[8,64,256]{2,1,0:T(8,128)}), f32[8,64,256]{2,1,0:T(8,128)S(1)}, u32[]{:S(2)}, u32[]{:S(2)}) %all-to-all-start.3) | async-done | bytes 524320 | tf_op jit(solution)/shard_map/all_to_all | solution.py:15
  36.6 28.4 %conditional.1 = (f32[3,16,256]{2,1,0:T(8,128)S(1)}) conditional(s32[]{:T(128)} %convert_element_type.47, (s32[]{:T(128)}, f32[64,256]{1,0:T(8,128)S(1)}, f32[512,512]{1,0:T(8,128)S(1)}, f32[512,256]{1,0:T(8,128)S(1)}, u32[]{:T(128)}, /*index=5*/u32[]{:T(128)}, u32[]{:T(128)}) %tuple.42, (s32[]{:T(128)}, f32[64,256]{1,0:T(8,128)S(1)}, ...), branch_computations={%region_0.1_spmd, %region_1.2_spmd} | conditional | flops 1612238336 | bytes 16823980 | solution.py:103
  36.7 1.0 fusion
  37.7 27.3 %all_to_all.37 = f32[32,1,16,256]{3,2,1,0:T(8,128)S(1)} all-to-all(f32[32,1,16,256]{3,2,1,0:T(8,128)S(1)} %bitcast.170), channel_id=1, replica_groups=mesh['x'=4,'z'=8,'core'=2,'row'=8] {'z','x'}, dimensions={0} | all-to-all | bytes 1048576 | tf_op jit(solution)/shard_map/cond/branch_0_fun/all_to_all | solution.py:42
  65.1 17.1 %all_to_all.38 = f32[8,64,256]{2,1,0:T(8,128)S(1)} all-to-all(f32[8,64,256]{2,1,0:T(8,128)S(1)} %broadcast_in_dim.22), channel_id=1, replica_groups=mesh['x'=4,'z'=8,'core'=2,'row'=8] {'row'}, dimensions={0} | all-to-all | bytes 1048576 | tf_op jit(solution)/shard_map/all_to_all | solution.py:15
  83.0 4.8 %all-to-all-start.4 = ((f32[8,3,16,256]{3,2,1,0:T(8,128)}), f32[8,3,16,256]{3,2,1,0:T(8,128)S(1)}, u32[]{:S(2)}, u32[]{:S(2)}) async-start(f32[8,3,16,256]{3,2,1,0:T(8,128)} %broadcast_in_dim.20), calls=%async_computation.4 | async-start | bytes 786432 | tf_op jit(solution)/shard_map/all_to_all | solution.py:15
  87.8 1.7 gather_fusion
  89.6 9.5 %all-to-all-done.4 = f32[8,3,16,256]{3,2,1,0:T(8,128)S(1)} async-done(((f32[8,3,16,256]{3,2,1,0:T(8,128)}), f32[8,3,16,256]{3,2,1,0:T(8,128)S(1)}, u32[]{:S(2)}, u32[]{:S(2)}) %all-to-all-start.4) | async-done | bytes 393248 | tf_op jit(solution)/shard_map/all_to_all | solution.py:15
  99.1 10.3 %all_gather.6 = f32[6,64,256]{2,1,0:T(8,128)S(1)} all-gather(f32[6,16,256]{2,1,0:T(8,128)S(1)} %fusion.42), channel_id=1, replica_groups=mesh['x'=4,'z'=8,'core'=2,'row'=8] {'x'}, dimensions={1}, use_global_device_ids=true | all-gather | bytes 491520 | tf_op jit(solution)/shard_map/all_gather | solution.py:131
  109.4 8.9 %collective-permute-start.2 = (f32[6,64,256]{2,1,0:T(8,128)S(1)}, f32[6,64,256]{2,1,0:T(8,128)S(1)}, u32[]{:S(2)}, u32[]{:S(2)}) collective-permute-start(f32[6,64,256]{2,1,0:T(8,128)S(1)} %all_gather.6), channel_id=1, source_target_pairs={{0,8},{8,0},{1,9},{9,1},{2,10},{10,2},{3,11},{11,3},{4,12},{12,4},... | collective-permute-start | bytes 1179656 | tf_op jit(solution)/shard_map/ppermute | solution.py:26
  118.6 1.0 collective-permute-done.2
  120.7 4.0 %all-to-all-start.6 = ((f32[8,64,256]{2,1,0:T(8,128)}), f32[8,64,256]{2,1,0:T(8,128)S(1)}, u32[]{:S(2)}, u32[]{:S(2)}) async-start(f32[8,64,256]{2,1,0:T(8,128)} %broadcast_in_dim.23), calls=%async_computation.6 | async-start | bytes 1048576 | tf_op jit(solution)/shard_map/all_to_all | solution.py:22
  124.7 12.5 %all_gather.7 = f32[3,5,64,256]{3,2,1,0:T(8,128)S(1)} all-gather(f32[3,5,16,256]{3,2,1,0:T(8,128)S(1)} %copy_bitcast_fusion), channel_id=1, replica_groups=mesh['x'=4,'z'=8,'core'=2,'row'=8] {'x'}, dimensions={2}, use_global_device_ids=true | all-gather | bytes 1228800 | tf_op jit(solution)/shard_map/all_gather | solution.py:137
  137.2 4.4 %collective-permute-start.3 = (f32[3,320,256]{2,1,0:T(8,128)S(1)}, f32[3,320,256]{2,1,0:T(8,128)}, u32[]{:S(2)}, u32[]{:S(2)}) collective-permute-start(f32[3,320,256]{2,1,0:T(8,128)S(1)} %bitcast.162), channel_id=1, source_target_pairs={{0,8},{8,0},{1,9},{9,1},{2,10},{10,2},{3,11},{11,3},{4,12},{12,4},... | collective-permute-start | bytes 2949128 | tf_op jit(solution)/shard_map/ppermute | solution.py:26
  141.6 1.1 fusion.33
  145.0 1.7 slice_bitcast_fusion
  146.7 2.2 %fusion.16 = f32[320,256]{1,0:T(8,128)} fusion(f32[256,256]{1,0:T(8,128)S(1)} %bitcast.157, f32[3,320,256]{2,1,0:T(8,128)} %collective-permute-done.3), kind=kOutput, calls=%fused_computation.53 | convolution fusion | flops 251658240 | bytes 917504 | tf_op jit(solution)/shard_map/dot_general | solution.py:30
  150.3 4.3 %all-to-all-start.7 = ((f32[8,64,256]{2,1,0:T(8,128)}), f32[8,64,256]{2,1,0:T(8,128)S(1)}, u32[]{:S(2)}, u32[]{:S(2)}) async-start(f32[8,64,256]{2,1,0:T(8,128)} %broadcast_in_dim.24), calls=%async_computation.7 | async-start | bytes 1048576 | tf_op jit(solution)/shard_map/all_to_all | solution.py:15
  155.8 1.4 fusion.19
  158.7 13.8 %all-to-all-done.7 = f32[8,64,256]{2,1,0:T(8,128)S(1)} async-done(((f32[8,64,256]{2,1,0:T(8,128)}), f32[8,64,256]{2,1,0:T(8,128)S(1)}, u32[]{:S(2)}, u32[]{:S(2)}) %all-to-all-start.7) | async-done | bytes 524320 | tf_op jit(solution)/shard_map/all_to_all | solution.py:15
  (84 shorter events, 16.2 us)
Async XLA Ops:
  0.0 19.5 %copy-start = (f32[512,256]{1,0:T(8,128)S(1)}, f32[512,256]{1,0:T(8,128)}, u32[]{:S(2)}) copy-start(f32[512,256]{1,0:T(8,128)} %param.7) | copy-start | bytes 1572868
  0.0 20.2 %collective-permute-start.1 = (f32[512,512]{1,0:T(8,128)}, f32[512,512]{1,0:T(8,128)}, u32[]{:S(2)}, u32[]{:S(2)}) collective-permute-start(f32[512,512]{1,0:T(8,128)} %bitcast.154), channel_id=1, source_target_pairs={{0,8},{8,0},{1,9},{9,1},{2,10},{10,2},{3,11},{11,3},{4,12},{12,4},... | collective-permute-start | bytes 3145736 | tf_op jit(solution)/shard_map/ppermute | solution.py:26
  8.9 2.9 %copy-start.12 = (s32[64]{0:T(128)S(1)}, s32[64]{0:T(128)}, u32[]{:S(2)}) copy-start(s32[64]{0:T(128)} %param.10) | copy-start | bytes 772
  8.9 5.5 %copy-start.9 = (f32[1,64,512]{2,1,0:T(8,128)S(1)}, f32[1,64,512]{2,1,0:T(8,128)}, u32[]{:S(2)}) copy-start(f32[1,64,512]{2,1,0:T(8,128)} %param.9) | copy-start | bytes 393220
  9.8 4.5 %collective-permute-start = (f32[64,256]{1,0:T(8,128)S(1)}, f32[64,256]{1,0:T(8,128)S(1)}, u32[]{:S(2)}, u32[]{:S(2)}) collective-permute-start(f32[64,256]{1,0:T(8,128)S(1)} %slice_select_fusion.4), channel_id=1, source_target_pairs={{0,8},{8,0},{1,9},{9,1},{2,10},{10,2},{3,11},{11,3},{4,12},{12,4},... | collective-permute-start | bytes 196616 | tf_op jit(solution)/shard_map/ppermute | solution.py:26
  14.4 5.8 %copy-start.1 = (f32[1,512,512]{2,1,0:T(8,128)S(1)}, f32[1,512,512]{2,1,0:T(8,128)}, u32[]{:S(2)}) copy-start(f32[1,512,512]{2,1,0:T(8,128)} %param.8) | copy-start | bytes 3145732
  15.3 21.4 %all-to-all-start.3 = ((f32[8,64,256]{2,1,0:T(8,128)}), f32[8,64,256]{2,1,0:T(8,128)S(1)}, u32[]{:S(2)}, u32[]{:S(2)}) async-start(f32[8,64,256]{2,1,0:T(8,128)} %broadcast_in_dim.19), calls=%async_computation.3 | async-start | bytes 1048576 | tf_op jit(solution)/shard_map/all_to_all | solution.py:15
  18.8 0.7 copy-start.13
  83.0 16.1 %all-to-all-start.4 = ((f32[8,3,16,256]{3,2,1,0:T(8,128)}), f32[8,3,16,256]{3,2,1,0:T(8,128)S(1)}, u32[]{:S(2)}, u32[]{:S(2)}) async-start(f32[8,3,16,256]{3,2,1,0:T(8,128)} %broadcast_in_dim.20), calls=%async_computation.4 | async-start | bytes 786432 | tf_op jit(solution)/shard_map/all_to_all | solution.py:15
  89.5 30.1 %copy-start.3 = (f32[448,256]{1,0:T(8,128)}, f32[448,256]{1,0:T(8,128)S(1)}, u32[]{:S(2)}) copy-start(f32[448,256]{1,0:T(8,128)S(1)} %gather_fusion) | copy-start | bytes 1376260
  109.4 9.2 %copy-start.4 = (f32[6,64,256]{2,1,0:T(8,128)}, f32[6,64,256]{2,1,0:T(8,128)S(1)}, u32[]{:S(2)}) copy-start(f32[6,64,256]{2,1,0:T(8,128)S(1)} %all_gather.6) | copy-start | bytes 1179652
  109.4 10.2 %collective-permute-start.2 = (f32[6,64,256]{2,1,0:T(8,128)S(1)}, f32[6,64,256]{2,1,0:T(8,128)S(1)}, u32[]{:S(2)}, u32[]{:S(2)}) collective-permute-start(f32[6,64,256]{2,1,0:T(8,128)S(1)} %all_gather.6), channel_id=1, source_target_pairs={{0,8},{8,0},{1,9},{9,1},{2,10},{10,2},{3,11},{11,3},{4,12},{12,4},... | collective-permute-start | bytes 1179656 | tf_op jit(solution)/shard_map/ppermute | solution.py:26
  119.6 1.1 copy-start.10
  120.7 23.6 %all-to-all-start.6 = ((f32[8,64,256]{2,1,0:T(8,128)}), f32[8,64,256]{2,1,0:T(8,128)S(1)}, u32[]{:S(2)}, u32[]{:S(2)}) async-start(f32[8,64,256]{2,1,0:T(8,128)} %broadcast_in_dim.23), calls=%async_computation.6 | async-start | bytes 1048576 | tf_op jit(solution)/shard_map/all_to_all | solution.py:22
  137.2 5.5 %copy-start.5 = (f32[6,64,256]{2,1,0:T(8,128)S(1)}, f32[6,64,256]{2,1,0:T(8,128)}, u32[]{:S(2)}) copy-start(f32[6,64,256]{2,1,0:T(8,128)} %copy-done.4) | copy-start | bytes 1179652
  137.2 7.8 %collective-permute-start.3 = (f32[3,320,256]{2,1,0:T(8,128)S(1)}, f32[3,320,256]{2,1,0:T(8,128)}, u32[]{:S(2)}, u32[]{:S(2)}) collective-permute-start(f32[3,320,256]{2,1,0:T(8,128)S(1)} %bitcast.162), channel_id=1, source_target_pairs={{0,8},{8,0},{1,9},{9,1},{2,10},{10,2},{3,11},{11,3},{4,12},{12,4},... | collective-permute-start | bytes 2949128 | tf_op jit(solution)/shard_map/ppermute | solution.py:26
  142.7 0.8 slice-start
  146.7 2.2 %copy-start.11 = (f32[6,64,256]{2,1,0:T(8,128)S(1)}, f32[6,64,256]{2,1,0:T(8,128)}, u32[]{:S(2)}) copy-start(f32[6,64,256]{2,1,0:T(8,128)} %copy-done.10) | copy-start | bytes 1179652
  150.3 22.3 %all-to-all-start.7 = ((f32[8,64,256]{2,1,0:T(8,128)}), f32[8,64,256]{2,1,0:T(8,128)S(1)}, u32[]{:S(2)}, u32[]{:S(2)}) async-start(f32[8,64,256]{2,1,0:T(8,128)} %broadcast_in_dim.24), calls=%async_computation.7 | async-start | bytes 1048576 | tf_op jit(solution)/shard_map/all_to_all | solution.py:15
  157.2 1.0 slice-start.1
  157.2 1.1 copy-start.8
  172.6 1.0 copy-start.6
  174.0 1.0 copy-start.7

commit v13 on v11

--- a/solution.py
+++ b/solution.py
@@ -43,19 +43,23 @@
     return jnp.where(group == panel, jnp.tile(own_rows, (below.shape[0] // slab, 1)), product)
 
 
-def one_slot(main, whole, spare, mine, panels, sources, is_main):
+def one_slot(main, whole, spare, mine, panels, sources, is_main, pivot_rows):
     lower, part = main
-    return jnp.stack([p[0] for p in spread([operator_of(lower, whole, part, panels[0])], sources)])
+    operator = operator_of(lower, whole, part, panels[0])
+    pieces = spread([operator], sources)
+    pivot = lax.all_gather(pivot_rows, ROW, tiled=True)
+    return jnp.stack([p[0] for p in pieces]), pivot
 
 
-def two_slots(main, whole, spare, mine, panels, sources, is_main):
+def two_slots(main, whole, spare, mine, panels, sources, is_main, pivot_rows):
     lower, part = main
     operators = [operator_of(lower, whole, part, panels[0])]
     lower, part = (jnp.where(mine, got, kept) for kept, got in spare)
     whole = sent_to_all(part, ROW).reshape(whole.shape)
     operators.append(operator_of(lower, whole, part, panels[1]))
     pieces = spread(operators, sources)
-    return jnp.stack([jnp.where(m, p[0], p[1]) for m, p in zip(is_main, pieces)])
+    pivot = lax.all_gather(pivot_rows, ROW, tiled=True)
+    return jnp.stack([jnp.where(m, p[0], p[1]) for m, p in zip(is_main, pieces)]), pivot
 
 
 def per_device(rhs_block, below, inverse, owner_map, row_perm):
@@ -93,7 +97,12 @@
     whole = sent_to_all(part, ROW).reshape(pivots, -1)
     lower, whole = lax.optimization_barrier((lower, whole))
     spare = (below, got_below), (kept, got)
-    kept = lax.cond(
+
+    def permuted(start, end):
+        rows = row_perm[start:end] - position * rows_dev
+        return rhs_block.at[rows].get(mode="promise_in_bounds")
+
+    kept, pivot = lax.cond(
         ~(is_main[1] & is_main[2]),
         two_slots,
         one_slot,
@@ -104,11 +113,8 @@
         panels,
         sources,
         is_main,
+        permuted(0, slab),
     )
-
-    def permuted(start, end):
-        rows = row_perm[start:end] - position * rows_dev
-        return rhs_block.at[rows].get(mode="promise_in_bounds")
 
     def to_all_rows(rows):
         return halves(sent_to_all(rows, ROW).reshape(pivots, columns), on_first, 0)
@@ -117,7 +123,7 @@
         return dot(a[0], b[0]) + dot(a[1], b[1])
 
     kept = sent_to_all(kept, "z")
-    pivot = [to_all_rows(permuted(0, slab))]
+    pivot = [halves(pivot, on_first, 0)]
     working = permuted(slab, rows_dev)
     pairs = [(g, k) for g in range(PANELS) for k in range(g + 1)]
     first = jnp.stack([kept[g, k] for g, k in pairs])

time: 179 us -> 175 us (0.978)
  blocking collectives: 69.1 us -> 44.8 us
  starting transfers between devices: 40.4 us -> 58.1 us
  local copies, waits for them, and re-layouts: 13 us -> 14.9 us
  waiting for transfers between devices: 39.4 us -> 37.6 us
    all_to_all x2 -> x0, blocking collectives: 44.4 us -> none  [the longest x1 27.3 us: spread(): lax.all_to_all(jnp.concatenate(sent, axis=1), CHIP, 0, 0, tiled=True)]
    all_gather x0 -> x1, blocking collectives: none -> 22 us  [one_slot(): pivot = lax.all_gather(pivot_rows, ROW, tiled=True)]
    all_to_all x0 -> x1, starting transfers between devices: none -> 10.9 us  [spread(): lax.all_to_all(jnp.concatenate(sent, axis=1), CHIP, 0, 0, tiled=True)]
    ppermute x4, starting transfers between devices: 22.4 us -> 27 us  [swapped(): return lax.ppermute(x, 'core', SWAP)]
    all_to_all x4, starting transfers between devices: 18 us -> 20.2 us  [sent_to_all(): lax.all_to_all(jnp.broadcast_to(x[None], (count, *x.shape)), axis, 0, 0,...]
    cond x0 -> x1, local copies, waits for them, and re-layouts: none -> 1.87 us
    all_to_all x4, waiting for transfers between devices: 38.4 us -> 36.5 us  [sent_to_all(): lax.all_to_all(jnp.broadcast_to(x[None], (count, *x.shape)), axis, 0, 0,...]
  transfers between devices with their start and end apart: 8 -> 9, of which waited for: 4 -> 4; matrix products, arithmetic and copies ran while one was open for 7% -> 8% of each run, Pallas kernels for 0% -> 0%
where the time goes in v13:
time: 175 us; the launch traced here: 174 us
  starting transfers between devices  58.1 us (33%)
  blocking collectives  44.8 us (26%)
  waiting for transfers between devices  37.6 us (21%)
  local copies, waits for them, and re-layouts  14.9 us (9%)
  matrix products  10.9 us (6%)
  other arithmetic  4.64 us (3%)
  between operations  2.57 us (1%)
    all_to_all x4, waiting for transfers between devices, sent_to_all(): lax.all_to_all(jnp.broadcast_to(x[None], (count, *x.shape)), axis, 0, 0,...  36.5 us
    ppermute x4, starting transfers between devices, swapped(): return lax.ppermute(x, 'core', SWAP)  27 us
    all_gather x1, blocking collectives, one_slot(): pivot = lax.all_gather(pivot_rows, ROW, tiled=True)  22 us
    all_to_all x4, starting transfers between devices, sent_to_all(): lax.all_to_all(jnp.broadcast_to(x[None], (count, *x.shape)), axis, 0, 0,...  20.2 us
    all_gather x1, blocking collectives, per_device(): rest = lax.all_gather(kept[PANELS:].swapaxes(0, 1), 'x', axis=2, tiled=True)  12.7 us
    all_to_all x1, starting transfers between devices, spread(): lax.all_to_all(jnp.concatenate(sent, axis=1), CHIP, 0, 0, tiled=True)  10.9 us
    dot_general x19, matrix products, dot(): jnp.dot(a, b, precision=lax.Precision.HIGHEST, preferred_element_type=jnp...  10.9 us
    all_gather x1, blocking collectives, per_device(): first = lax.all_gather(first, 'x', axis=1, tiled=True)  10.2 us
  transfers between devices with their start and end apart: 9, of which 4 were waited for; matrix products, arithmetic and copies ran while one was open for 8% of the time, Pallas kernels for 0%

profile of v13, /device:TPU:1, one launch (start us, length us, event | category | flops | bytes accessed | tf_op | source)
XLA Modules:
  0.0 173.6 jit_solution(12609668457453311787)
XLA Ops:
  0.0 8.9 %collective-permute-start.1 = (f32[512,512]{1,0:T(8,128)}, f32[512,512]{1,0:T(8,128)}, u32[]{:S(2)}, u32[]{:S(2)}) collective-permute-start(f32[512,512]{1,0:T(8,128)} %bitcast.144), channel_id=1, source_target_pairs={{0,8},{8,0},{1,9},{9,1},{2,10},{10,2},{3,11},{11,3},{4,12},{12,4},... | collective-permute-start | bytes 3145736 | tf_op jit(solution)/shard_map/ppermute | solution.py:19
  9.8 1.9 %collective-permute-start = (f32[64,256]{1,0:T(8,128)S(1)}, f32[64,256]{1,0:T(8,128)S(1)}, u32[]{:S(2)}, u32[]{:S(2)}) collective-permute-start(f32[64,256]{1,0:T(8,128)S(1)} %slice_select_fusion.6), channel_id=1, source_target_pairs={{0,8},{8,0},{1,9},{9,1},{2,10},{10,2},{3,11},{11,3},{4,12},{12,4},... | collective-permute-start | bytes 196616 | tf_op jit(solution)/shard_map/ppermute | solution.py:19
  15.4 3.5 %all-to-all-start.3 = ((f32[8,64,256]{2,1,0:T(8,128)}), f32[8,64,256]{2,1,0:T(8,128)S(1)}, u32[]{:S(2)}, u32[]{:S(2)}) async-start(f32[8,64,256]{2,1,0:T(8,128)} %broadcast_in_dim.17), calls=%async_computation.3 | async-start | bytes 1048576 | tf_op jit(solution)/shard_map/all_to_all | solution.py:15
  20.3 1.4 broadcast_select_fusion.1
  21.8 15.0 %all-to-all-done.3 = f32[8,64,256]{2,1,0:T(8,128)S(1)} async-done(((f32[8,64,256]{2,1,0:T(8,128)}), f32[8,64,256]{2,1,0:T(8,128)S(1)}, u32[]{:S(2)}, u32[]{:S(2)}) %all-to-all-start.3) | async-done | bytes 524320 | tf_op jit(solution)/shard_map/all_to_all | solution.py:15
  36.8 36.7 %conditional.1 = (f32[3,16,256]{2,1,0:T(8,128)S(1)}, f32[512,256]{1,0:T(8,128)}, f32[512,256]{1,0:T(8,128)}) conditional(s32[]{:T(128)} %convert_element_type.47, (s32[]{:T(128)}, f32[64,256]{1,0:T(8,128)S(1)}, f32[512,512]{1,0:T(8,128)S(1)}, f32[512,256]{1,0:T(8,128)S(1)}, u32[]{:T(128)}, /*index=5*/u32[]{:T(128)}, u32[]{:T(128)}, ...), branch_computations={%region_0.1_spmd, %region_1.2_spmd} | conditional | flops 1612238336 | bytes 18462396 | solution.py:105
  36.8 1.8 %fusion = f32[512,256]{1,0:T(8,128)} fusion(f32[512,256]{1,0:T(8,128)S(1)} %bitcast.160, f32[512,512]{1,0:T(8,128)S(1)} %get-tuple-element.75, f32[512,256]{1,0:T(8,128)S(1)} %get-tuple-element.76, s32[]{:T(128)} %get-tuple-element.73, s32[512]{0:T(512)S(1)} %get-tuple-element.186, s32[512]{0:T(512)S(1)} %get-tuple-element.187, pred[512]{0:T(512)(128)(4,1)S(1)} %fusion.3), kind=kOutput, calls=%fused_computation.3 | convolution fusion | flops 805830656 | bytes 2626052 | tf_op jit(solution)/shard_map/cond/branch_0_fun/dot_general | solution.py:23
  38.6 10.9 %all-to-all-start = ((f32[32,1,16,256]{3,2,1,0:T(8,128)}), f32[32,1,16,256]{3,2,1,0:T(8,128)S(1)}, u32[]{:S(2)}, u32[]{:S(2)}) async-start(f32[32,1,16,256]{3,2,1,0:T(8,128)} %bitcast.2), calls=%async_computation | async-start | bytes 1048576 | tf_op jit(solution)/shard_map/cond/branch_0_fun/all_to_all | solution.py:35
  49.6 22.0 %all_gather.8 = f32[512,256]{1,0:T(8,128)} all-gather(f32[64,256]{1,0:T(8,128)S(1)} %get-tuple-element.84), channel_id=1, replica_groups=mesh['x'=4,'z'=8,'core'=2,'row'=8] {'row'}, dimensions={0}, use_global_device_ids=true | all-gather | bytes 589824 | tf_op jit(solution)/shard_map/cond/branch_0_fun/all_gather | solution.py:50
  71.6 1.9 %copy.34 = f32[512,256]{1,0:T(8,128)} copy(f32[512,256]{1,0:T(8,128)} %all_gather.8) | data formatting | bytes 1048576 | tf_op jit(solution)/shard_map/cond
  74.2 6.7 %all-to-all-start.4 = ((f32[8,3,16,256]{3,2,1,0:T(8,128)}), f32[8,3,16,256]{3,2,1,0:T(8,128)S(1)}, u32[]{:S(2)}, u32[]{:S(2)}) async-start(f32[8,3,16,256]{3,2,1,0:T(8,128)} %broadcast_in_dim.19), calls=%async_computation.4 | async-start | bytes 786432 | tf_op jit(solution)/shard_map/all_to_all | solution.py:15
  81.0 1.7 gather_fusion
  82.7 1.2 slice_select_fusion.5
  84.0 7.7 %all-to-all-done.4 = f32[8,3,16,256]{3,2,1,0:T(8,128)S(1)} async-done(((f32[8,3,16,256]{3,2,1,0:T(8,128)}), f32[8,3,16,256]{3,2,1,0:T(8,128)S(1)}, u32[]{:S(2)}, u32[]{:S(2)}) %all-to-all-start.4) | async-done | bytes 393248 | tf_op jit(solution)/shard_map/all_to_all | solution.py:15
  91.7 10.2 %all_gather.12 = f32[6,64,256]{2,1,0:T(8,128)S(1)} all-gather(f32[6,16,256]{2,1,0:T(8,128)S(1)} %fusion.42), channel_id=1, replica_groups=mesh['x'=4,'z'=8,'core'=2,'row'=8] {'x'}, dimensions={1}, use_global_device_ids=true | all-gather | bytes 491520 | tf_op jit(solution)/shard_map/all_gather | solution.py:130
  101.9 12.2 %collective-permute-start.2 = (f32[6,64,256]{2,1,0:T(8,128)S(1)}, f32[6,64,256]{2,1,0:T(8,128)S(1)}, u32[]{:S(2)}, u32[]{:S(2)}) collective-permute-start(f32[6,64,256]{2,1,0:T(8,128)S(1)} %all_gather.12), channel_id=1, source_target_pairs={{0,8},{8,0},{1,9},{9,1},{2,10},{10,2},{3,11},{11,3},{4,12},{12,4},... | collective-permute-start | bytes 1179656 | tf_op jit(solution)/shard_map/ppermute | solution.py:19
  116.5 3.5 %all-to-all-start.5 = ((f32[8,64,256]{2,1,0:T(8,128)}), f32[8,64,256]{2,1,0:T(8,128)S(1)}, u32[]{:S(2)}, u32[]{:S(2)}) async-start(f32[8,64,256]{2,1,0:T(8,128)} %broadcast_in_dim.20), calls=%async_computation.5 | async-start | bytes 1048576 | tf_op jit(solution)/shard_map/all_to_all | solution.py:15
  120.0 12.7 %all_gather.13 = f32[3,5,64,256]{3,2,1,0:T(8,128)S(1)} all-gather(f32[3,5,16,256]{3,2,1,0:T(8,128)S(1)} %copy_bitcast_fusion), channel_id=1, replica_groups=mesh['x'=4,'z'=8,'core'=2,'row'=8] {'x'}, dimensions={2}, use_global_device_ids=true | all-gather | bytes 1228800 | tf_op jit(solution)/shard_map/all_gather | solution.py:136
  132.7 4.0 %collective-permute-start.3 = (f32[3,320,256]{2,1,0:T(8,128)S(1)}, f32[3,320,256]{2,1,0:T(8,128)}, u32[]{:S(2)}, u32[]{:S(2)}) collective-permute-start(f32[3,320,256]{2,1,0:T(8,128)S(1)} %bitcast.152), channel_id=1, source_target_pairs={{0,8},{8,0},{1,9},{9,1},{2,10},{10,2},{3,11},{11,3},{4,12},{12,4},... | collective-permute-start | bytes 2949128 | tf_op jit(solution)/shard_map/ppermute | solution.py:19
  140.1 1.7 slice_bitcast_fusion
  141.8 2.2 %fusion.16 = f32[320,256]{1,0:T(8,128)} fusion(f32[256,256]{1,0:T(8,128)S(1)} %bitcast.147, f32[3,320,256]{2,1,0:T(8,128)} %collective-permute-done.3), kind=kOutput, calls=%fused_computation.53 | convolution fusion | flops 251658240 | bytes 917504 | tf_op jit(solution)/shard_map/dot_general | solution.py:23
  145.4 6.5 %all-to-all-start.6 = ((f32[8,64,256]{2,1,0:T(8,128)}), f32[8,64,256]{2,1,0:T(8,128)S(1)}, u32[]{:S(2)}, u32[]{:S(2)}) async-start(f32[8,64,256]{2,1,0:T(8,128)} %broadcast_in_dim.21), calls=%async_computation.6 | async-start | bytes 1048576 | tf_op jit(solution)/shard_map/all_to_all | solution.py:15
  153.1 1.4 fusion.19
  156.0 13.8 %all-to-all-done.6 = f32[8,64,256]{2,1,0:T(8,128)S(1)} async-done(((f32[8,64,256]{2,1,0:T(8,128)}), f32[8,64,256]{2,1,0:T(8,128)S(1)}, u32[]{:S(2)}, u32[]{:S(2)}) %all-to-all-start.6) | async-done | bytes 524320 | tf_op jit(solution)/shard_map/all_to_all | solution.py:15
  (84 shorter events, 18.2 us)
Async XLA Ops:
  0.0 19.6 %copy-start = (f32[512,256]{1,0:T(8,128)S(1)}, f32[512,256]{1,0:T(8,128)}, u32[]{:S(2)}) copy-start(f32[512,256]{1,0:T(8,128)} %param.7) | copy-start | bytes 1572868
  0.0 20.3 %collective-permute-start.1 = (f32[512,512]{1,0:T(8,128)}, f32[512,512]{1,0:T(8,128)}, u32[]{:S(2)}, u32[]{:S(2)}) collective-permute-start(f32[512,512]{1,0:T(8,128)} %bitcast.144), channel_id=1, source_target_pairs={{0,8},{8,0},{1,9},{9,1},{2,10},{10,2},{3,11},{11,3},{4,12},{12,4},... | collective-permute-start | bytes 3145736 | tf_op jit(solution)/shard_map/ppermute | solution.py:19
  8.9 2.9 %copy-start.12 = (s32[64]{0:T(128)S(1)}, s32[64]{0:T(128)}, u32[]{:S(2)}) copy-start(s32[64]{0:T(128)} %param.10) | copy-start | bytes 772
  8.9 5.6 %copy-start.9 = (f32[1,64,512]{2,1,0:T(8,128)S(1)}, f32[1,64,512]{2,1,0:T(8,128)}, u32[]{:S(2)}) copy-start(f32[1,64,512]{2,1,0:T(8,128)} %param.9) | copy-start | bytes 393220
  9.8 4.7 %collective-permute-start = (f32[64,256]{1,0:T(8,128)S(1)}, f32[64,256]{1,0:T(8,128)S(1)}, u32[]{:S(2)}, u32[]{:S(2)}) collective-permute-start(f32[64,256]{1,0:T(8,128)S(1)} %slice_select_fusion.6), channel_id=1, source_target_pairs={{0,8},{8,0},{1,9},{9,1},{2,10},{10,2},{3,11},{11,3},{4,12},{12,4},... | collective-permute-start | bytes 196616 | tf_op jit(solution)/shard_map/ppermute | solution.py:19
  14.5 5.8 %copy-start.1 = (f32[1,512,512]{2,1,0:T(8,128)S(1)}, f32[1,512,512]{2,1,0:T(8,128)}, u32[]{:S(2)}) copy-start(f32[1,512,512]{2,1,0:T(8,128)} %param.8) | copy-start | bytes 3145732
  15.4 21.4 %all-to-all-start.3 = ((f32[8,64,256]{2,1,0:T(8,128)}), f32[8,64,256]{2,1,0:T(8,128)S(1)}, u32[]{:S(2)}, u32[]{:S(2)}) async-start(f32[8,64,256]{2,1,0:T(8,128)} %broadcast_in_dim.17), calls=%async_computation.3 | async-start | bytes 1048576 | tf_op jit(solution)/shard_map/all_to_all | solution.py:15
  18.9 0.7 copy-start.13
  38.6 32.9 %all-to-all-start = ((f32[32,1,16,256]{3,2,1,0:T(8,128)}), f32[32,1,16,256]{3,2,1,0:T(8,128)S(1)}, u32[]{:S(2)}, u32[]{:S(2)}) async-start(f32[32,1,16,256]{3,2,1,0:T(8,128)} %bitcast.2), calls=%async_computation | async-start | bytes 1048576 | tf_op jit(solution)/shard_map/cond/branch_0_fun/all_to_all | solution.py:35
  74.2 17.5 %all-to-all-start.4 = ((f32[8,3,16,256]{3,2,1,0:T(8,128)}), f32[8,3,16,256]{3,2,1,0:T(8,128)S(1)}, u32[]{:S(2)}, u32[]{:S(2)}) async-start(f32[8,3,16,256]{3,2,1,0:T(8,128)} %broadcast_in_dim.19), calls=%async_computation.4 | async-start | bytes 786432 | tf_op jit(solution)/shard_map/all_to_all | solution.py:15
  82.7 32.7 %copy-start.3 = (f32[448,256]{1,0:T(8,128)}, f32[448,256]{1,0:T(8,128)S(1)}, u32[]{:S(2)}) copy-start(f32[448,256]{1,0:T(8,128)S(1)} %gather_fusion) | copy-start | bytes 1376260
  101.9 12.5 %copy-start.4 = (f32[6,64,256]{2,1,0:T(8,128)}, f32[6,64,256]{2,1,0:T(8,128)S(1)}, u32[]{:S(2)}) copy-start(f32[6,64,256]{2,1,0:T(8,128)S(1)} %all_gather.12) | copy-start | bytes 1179652
  101.9 13.6 %collective-permute-start.2 = (f32[6,64,256]{2,1,0:T(8,128)S(1)}, f32[6,64,256]{2,1,0:T(8,128)S(1)}, u32[]{:S(2)}, u32[]{:S(2)}) collective-permute-start(f32[6,64,256]{2,1,0:T(8,128)S(1)} %all_gather.12), channel_id=1, source_target_pairs={{0,8},{8,0},{1,9},{9,1},{2,10},{10,2},{3,11},{11,3},{4,12},{12,4},... | collective-permute-start | bytes 1179656 | tf_op jit(solution)/shard_map/ppermute | solution.py:19
  115.4 1.1 copy-start.10
  116.5 23.0 %all-to-all-start.5 = ((f32[8,64,256]{2,1,0:T(8,128)}), f32[8,64,256]{2,1,0:T(8,128)S(1)}, u32[]{:S(2)}, u32[]{:S(2)}) async-start(f32[8,64,256]{2,1,0:T(8,128)} %broadcast_in_dim.20), calls=%async_computation.5 | async-start | bytes 1048576 | tf_op jit(solution)/shard_map/all_to_all | solution.py:15
  132.7 5.1 %copy-start.5 = (f32[6,64,256]{2,1,0:T(8,128)S(1)}, f32[6,64,256]{2,1,0:T(8,128)}, u32[]{:S(2)}) copy-start(f32[6,64,256]{2,1,0:T(8,128)} %copy-done.4) | copy-start | bytes 1179652
  132.7 7.4 %collective-permute-start.3 = (f32[3,320,256]{2,1,0:T(8,128)S(1)}, f32[3,320,256]{2,1,0:T(8,128)}, u32[]{:S(2)}, u32[]{:S(2)}) collective-permute-start(f32[3,320,256]{2,1,0:T(8,128)S(1)} %bitcast.152), channel_id=1, source_target_pairs={{0,8},{8,0},{1,9},{9,1},{2,10},{10,2},{3,11},{11,3},{4,12},{12,4},... | collective-permute-start | bytes 2949128 | tf_op jit(solution)/shard_map/ppermute | solution.py:19
  137.8 0.8 slice-start
  141.8 2.2 %copy-start.11 = (f32[6,64,256]{2,1,0:T(8,128)S(1)}, f32[6,64,256]{2,1,0:T(8,128)}, u32[]{:S(2)}) copy-start(f32[6,64,256]{2,1,0:T(8,128)} %copy-done.10) | copy-start | bytes 1179652
  145.4 24.5 %all-to-all-start.6 = ((f32[8,64,256]{2,1,0:T(8,128)}), f32[8,64,256]{2,1,0:T(8,128)S(1)}, u32[]{:S(2)}, u32[]{:S(2)}) async-start(f32[8,64,256]{2,1,0:T(8,128)} %broadcast_in_dim.21), calls=%async_computation.6 | async-start | bytes 1048576 | tf_op jit(solution)/shard_map/all_to_all | solution.py:15
  154.5 1.0 slice-start.1
  154.5 1.1 copy-start.8
  169.9 1.0 copy-start.6
  171.3 1.0 copy-start.7
